TPU v7x, 128 devices: a whole 4x4x4 slice. The times are simulated.
128 devices in a mesh: dp: 2 (over y_hi), ctx: 16 (over x, z), tensor: 4 (over y_lo, core).
Axes of the slice: x: 4, y: 4 (y_hi: 2, y_lo: 2; y = y_hi * 2 + y_lo), z: 4, core: 2. Of those that a mesh axis runs over, the one named last changes fastest.
Arguments:
- values: bfloat16 [2, 4096, 4096], P('dp', 'ctx', 'tensor'), may hold values from -6 to 6
- b_proj: bfloat16 [2, 4096, 128], P('dp', 'ctx'), may hold values from -0.1875 to 0.1875
- c_proj: bfloat16 [2, 4096, 128], P('dp', 'ctx'), may hold values from -0.52734375 to 0.52734375
- step_sizes: float32 [2, 64, 4096], P('dp', 'tensor', 'ctx'), may hold values from 0.5 to 2
- decay_rates: float32 [64], P('tensor'), may hold values from 0.05 to 60
- skip_gain: float32 [64], P('tensor'), may hold values from 0.5 to 1.5
- w_out: bfloat16 [4096, 4096], P(None, 'tensor'), may hold values from -0.09375 to 0.09375
- d_out: bfloat16 [2, 4096, 4096], P('dp', 'ctx'), may hold values from -6 to 6
Outputs:
- d_values: bfloat16 [2, 4096, 4096], P('dp', 'ctx', 'tensor')
- d_b: float32 [2, 4096, 128], P('dp', 'ctx')
- d_c: float32 [2, 4096, 128], P('dp', 'ctx')
- d_steps: float32 [2, 64, 4096], P('dp', 'tensor', 'ctx')
- d_rates: float32 [64], P('tensor')
- d_skip: float32 [64], P('tensor')
- d_w: float32 [4096, 4096], P(('dp', 'ctx'), 'tensor')
All inputs are finite; a program needn't handle non-finite values.
Results may differ from a plain program's by a relative error of at most 0.006.
Values sent between devices are 32-bit elements; how exact they have to be, the bound alone decides.
No kernel may reach another device: no remote copies, remote signals or barrier semaphores. Data moves between devices by JAX's collectives and lax.ppermute only.
A program may use at most 128 MiB of HBM per device.

v0:
```python
import jax
import jax.numpy as jnp
from jax import lax
from jax.sharding import PartitionSpec as P

high = lax.Precision.HIGHEST


def prefix(value, axis, combine, identity, reverse):
    length, position = (lax.axis_size(axis), lax.axis_index(axis))
    everything = jax.tree.map(lambda part: lax.all_gather(part, axis), value)
    start = jax.tree.map(
        lambda part, zero: jnp.broadcast_to(jnp.asarray(zero, part.dtype), part.shape),
        value,
        identity,
    )

    def hop(k, before):
        at = length - 1 - k if reverse else k
        reached = at > position if reverse else at < position
        new = combine(before, jax.tree.map(lambda part: part[at], everything))
        return jax.tree.map(lambda a, b: jnp.where(reached, a, b), new, before)

    return lax.fori_loop(0, length, hop, start)


def run_blocks(chan_vals, b_rows, c_rows, step_rows, rates, gains, start_state, length):
    total_len = chan_vals.shape[0]
    heads_here = chan_vals.shape[1]
    head_width = chan_vals.shape[2]
    state_width = b_rows.shape[1]
    block = min(256, total_len)
    nblocks = total_len // block
    vals_blk = chan_vals.reshape(nblocks, block, heads_here, head_width)
    b_blk = b_rows.reshape(nblocks, block, state_width)
    c_blk = c_rows.reshape(nblocks, block, state_width)
    step_blk = step_rows.reshape(heads_here, nblocks, block).transpose(1, 0, 2)
    position = jnp.arange(block)
    lower = position[:, None] >= position[None, :]

    def advance(state, pieces):
        vals_one, b_one, c_one, step_one = pieces
        logdecay = -step_one * rates[:, None] / length
        running = jnp.cumsum(logdecay, axis=1)
        between = running[:, :, None] - running[:, None, :]
        weights = jnp.exp(jnp.where(lower[None], between, -jnp.inf))
        intersection = jnp.einsum("in,jn->ij", c_one, b_one, precision=high)
        mixing = weights * intersection[None] * step_one[:, None, :]
        inside = jnp.einsum("hij,jhp->ihp", mixing, vals_one, precision=high)
        carried = jnp.exp(running).T[:, :, None] * jnp.einsum(
            "in,hpn->ihp", c_one, state, precision=high
        )
        output = inside + carried + gains[None, :, None] * vals_one
        tail = jnp.exp(running[:, -1:] - running) * step_one
        fresh = jnp.einsum("hj,jhp,jn->hpn", tail, vals_one, b_one, precision=high)
        new_state = jnp.exp(running[:, -1])[:, None, None] * state + fresh
        return (new_state, output)

    end_state, outputs = lax.scan(advance, start_state, (vals_blk, b_blk, c_blk, step_blk))
    return (outputs.reshape(total_len, heads_here, head_width), end_state)


def chain(earlier, later):
    return (earlier[0] * later[0], earlier[1] * later[0][:, None, None] + later[1])


def body(values, b_proj, c_proj, step_sizes, decay_rates, skip_gain, w_out, d_out):
    tokens = values.shape[1]
    width = values.shape[2]
    heads_here = decay_rates.shape[0]
    head_width = width // heads_here
    length = tokens * lax.axis_size("ctx")
    chan_vals = values[0].astype(jnp.float32).reshape(tokens, heads_here, head_width)
    b_rows = b_proj[0].astype(jnp.float32)
    c_rows = c_proj[0].astype(jnp.float32)
    step_rows = step_sizes[0]
    cotangent = d_out[0]
    upstream = jnp.dot(cotangent, w_out, preferred_element_type=jnp.float32).astype(jnp.bfloat16)
    upstream_f = upstream.astype(jnp.float32).reshape(tokens, heads_here, head_width)
    running = jnp.cumsum(-step_rows * decay_rates[:, None] / length, axis=1)
    shard_total = running[:, -1]
    local_end = jnp.einsum(
        "ht,thp,tn->hpn",
        jnp.exp(shard_total[:, None] - running) * step_rows,
        chan_vals,
        b_rows,
        precision=high,
    )
    local_grad = jnp.einsum("ht,thp,tn->hpn", jnp.exp(running), upstream_f, c_rows, precision=high)
    shard_decay = jnp.exp(shard_total)
    neutral = (jnp.ones_like(shard_decay), jnp.zeros_like(local_end))
    _, state_in = prefix((shard_decay, local_end), "ctx", chain, neutral, False)
    _, grad_out = prefix((shard_decay, local_grad), "ctx", chain, neutral, True)

    def local_mix(vals, b_all, c_all, steps_all, rates, gains, start_state):
        return run_blocks(vals, b_all, c_all, steps_all, rates, gains, start_state, length)

    (mixed, _), pullback = jax.vjp(
        local_mix, chan_vals, b_rows, c_rows, step_rows, decay_rates, skip_gain, state_in
    )
    grad_vals, grad_b, grad_c, grad_steps, grad_rates, grad_skip, _ = pullback(
        (upstream_f, grad_out)
    )
    mixed_bf = mixed.reshape(tokens, width).astype(jnp.bfloat16)
    d_w = lax.psum_scatter(
        lax.dot_general(
            cotangent, mixed_bf, (((0,), (0,)), ((), ())), preferred_element_type=jnp.float32
        ),
        ("dp", "ctx"),
        scatter_dimension=0,
        tiled=True,
    )
    d_b, d_c = lax.psum((grad_b, grad_c), "tensor")
    d_rates, d_skip = lax.psum((grad_rates, grad_skip), ("dp", "ctx"))
    d_values = grad_vals.reshape(1, tokens, width).astype(jnp.bfloat16)
    return (d_values, d_b[None], d_c[None], grad_steps[None], d_rates, d_skip, d_w)


def solution(mesh):
    return jax.shard_map(
        body,
        mesh=mesh,
        in_specs=(
            P("dp", "ctx", "tensor"),
            P("dp", "ctx", None),
            P("dp", "ctx", None),
            P("dp", "tensor", "ctx"),
            P("tensor"),
            P("tensor"),
            P(None, "tensor"),
            P("dp", "ctx", None),
        ),
        out_specs=(
            P("dp", "ctx", "tensor"),
            P("dp", "ctx", None),
            P("dp", "ctx", None),
            P("dp", "tensor", "ctx"),
            P("tensor"),
            P("tensor"),
            P(("dp", "ctx"), "tensor"),
        ),
        check_vma=False,
    )
```

profile of v0, /device:TPU:0, one launch (start us, length us, event | category | flops | bytes accessed | tf_op | source)
XLA Modules:
  0.0 491.3 jit_solution(9471073004334104307)
XLA Ops:
  9.7 5.8 %fusion.55 = (f32[1024]{0:T(1024)S(1)}, bf16[256,1024]{1,0:T(8,128)(2,1)S(1)}) fusion(bf16[1,256,1024]{2,1,0:T(8,128)(2,1)} %param.12, bf16[4096,1024]{1,0:T(8,128)(2,1)} %param.18, bf16[1,256,4096]{2,1,0:T(8,128)(2,1)S(1)} %copy-done), kind=kOutput, calls=%fused_computation.55 | convolution fusion | flops 2148793344 | bytes 11538432 | tf_op jit(solution)/shard_map/dot_general | solution.py:78
  15.8 1.5 fusion.57
  17.4 1.2 copy.69
  20.5 42.1 %all-reduce.2 = f32[256]{0:T(256)S(1)} all-reduce(f32[256]{0:T(256)S(1)} %dynamic-update-slice), channel_id=2, replica_groups=mesh['dp'=2,'ctx'=16,'tensor'=4] {'ctx'}, use_global_device_ids=true, to_apply=%add.2 | all-reduce | flops 256 | bytes 2048
  62.7 28.3 %all-gather.6.cloned.1.call-done = f32[256,64,128]{2,1,0:T(8,128)} async-done(((f32[16,64,128]{2,1,0:T(8,128)}), f32[256,64,128]{2,1,0:T(8,128)}) %all-gather.6.cloned.1.call-update) | async-done | bytes 8388624 | tf_op jit(solution)/shard_map/all_gather | solution.py:11
  91.0 19.5 %while.20 = (s32[]{:T(128)}, f32[16,64,128]{2,1,0:T(8,128)S(1)}, s32[]{:T(128)}, f32[16,16]{1,0:T(8,128)S(1)}, f32[16,16,64,128]{3,2,1,0:T(8,128)}, /*index=5*/s32[]{:T(128)}, s32[]{:T(128)}, s32[]{:T(128)}, s32[]{:T(128)}) while((s32[]{:T(128)}, f32[16,64,128]{2,1,0:T(8,128)S(1)}, s32[]{:T(128)}, f32[16,16]{1,0:T(8,128)S(1)}, ...), condition=%wide.region_3.4_spmd.clone, body=%wide.region_2.3_spmd.clone.sunk | while | flops 524296 | bytes 1573231 | solution.py:24
  91.0 1.2 fusion.105
  92.2 1.2 fusion.105
  93.4 1.2 fusion.105
  94.7 1.2 fusion.105
  95.9 1.2 fusion.105
  97.1 1.2 fusion.105
  98.3 1.2 fusion.105
  99.6 1.2 fusion.105
  100.8 1.2 fusion.105
  102.0 1.2 fusion.105
  103.2 1.2 fusion.105
  104.5 1.2 fusion.105
  105.7 1.2 fusion.105
  106.9 1.2 fusion.105
  108.1 1.2 fusion.105
  109.3 1.2 fusion.105
  110.5 1.6 fusion.54
  112.9 1.5 fusion.49
  114.4 2.3 copy.68
  116.8 0.9 fusion.66
  117.7 67.3 %all-gather.8.cloned.1.call-done = f32[256,64,128]{2,1,0:T(8,128)} async-done(((f32[16,64,128]{2,1,0:T(8,128)}), f32[256,64,128]{2,1,0:T(8,128)}) %all-gather.8.cloned.1.call-update) | async-done | bytes 8388624 | tf_op jit(solution)/shard_map/all_gather | solution.py:11
  184.9 19.5 %while.21 = (s32[]{:T(128)}, f32[16,64,128]{2,1,0:T(8,128)S(1)}, s32[]{:T(128)}, f32[16,16]{1,0:T(8,128)S(1)}, f32[16,16,64,128]{3,2,1,0:T(8,128)}, /*index=5*/s32[]{:T(128)}, s32[]{:T(128)}) while((s32[]{:T(128)}, f32[16,64,128]{2,1,0:T(8,128)S(1)}, s32[]{:T(128)}, f32[16,16]{1,0:T(8,128)S(1)}, f32[16,16,64,128]{3,2,1,0:T(8,128)}, ...), condition=%wide.region_7.8_spmd.clone, body=%wide.region_6.7_spmd.clone.sunk | while | flops 524292 | bytes 1573169 | solution.py:24
  184.9 1.2 fusion.106
  186.2 1.2 fusion.106
  187.4 1.2 fusion.106
  188.6 1.2 fusion.106
  189.8 1.2 fusion.106
  191.0 1.2 fusion.106
  192.3 1.2 fusion.106
  193.5 1.2 fusion.106
  194.7 1.2 fusion.106
  195.9 1.2 fusion.106
  197.1 1.2 fusion.106
  198.3 1.2 fusion.106
  199.6 1.2 fusion.106
  200.8 1.2 fusion.106
  202.0 1.2 fusion.106
  203.2 1.2 fusion.106
  204.4 2.4 multiply_reduce_fusion.2
  206.8 4.9 %fusion.46 = bf16[256,16,64]{0,2,1:T(8,128)(2,1)S(1)} fusion(bf16[256,16,64]{0,2,1:T(8,128)(2,1)} %bitcast.192, f32[16,256]{1,0:T(8,128)S(1)} %bitcast.203, f32[256,256]{1,0:T(8,128)} %fusion.66, f32[16,256]{1,0:T(8,128)S(1)} %copy_bitcast_fusion, pred[256,256]{1,0:T(8,128)(4,1)S(1)} %iota_compare_fusion, f32[256,16,64]{0,2,1:T(8,128)S(1)} %get-tuple-element.514, ...), kind=kOutput, calls=%fused_computation.44 | convolution fusion | flops 811073536 | bytes 2474048 | tf_op jit(solution)/shard_map/jvp()/while/body/eval_jaxpr/hij,jhp->ihp/dot_general | solution.py:49
  211.8 8.1 %convolution_bitcast_fusion = f32[4096,1024]{0,1:T(8,128)} fusion(bf16[256,1024]{0,1:T(8,128)(2,1)S(1)} %bitcast.200, bf16[1,256,4096]{2,1,0:T(8,128)(2,1)S(1)} %copy-done), kind=kOutput, calls=%fused_computation.6 | convolution fusion | flops 2147483648 | bytes 19398656 | tf_op jit(solution)/shard_map/dot_general | solution.py:106
  221.4 4.9 %fusion.9 = (f32[16,256]{1,0:T(8,128)}, f32[16,256]{1,0:T(8,128)}, f32[16,256]{1,0:T(8,128)}, f32[256,256]{1,0:T(8,128)S(1)}) fusion(f32[16,256]{1,0:T(8,128)} %bitcast.202, f32[256,256]{1,0:T(8,128)} %fusion.66, f32[16,256]{1,0:T(8,128)} %copy-done.16, pred[256,256]{1,0:T(8,128)(4,1)} %copy-done.18, bf16[16,64,256]{2,1,0:T(8,128)(2,1)} %bitcast.196, ...), kind=kOutput, calls=%fused_computation.16 | convolution fusion | flops 147771392 | bytes 1720320 | tf_op jit(solution)/shard_map/transpose(jvp())/while/body/eval_jaxpr/hij,jhp->ihp/dot_general | solution.py:49
  226.4 3.6 fusion.40
  230.1 2.0 copy.74
  232.1 1.3 copy.71
  233.5 2.9 fusion.51
  236.3 1.0 fusion.53
  237.7 3.0 convolution_bitcast_fusion.3
  240.7 0.9 fusion.52
  242.4 0.9 copy_bitcast_fusion.1
  243.3 2.5 reduce-window.24
  246.0 1.6 fusion.77
  247.5 95.4 %all-reduce.3 = (f32[16]{0:T(128)}, f32[16]{0:T(128)}) all-reduce(f32[16]{0:T(128)S(1)} %get-tuple-element.509, f32[16]{0:T(128)} %reduce_sum.150), channel_id=1, replica_groups=mesh['dp'=2,'ctx'=16,'tensor'=4] {'dp','ctx'}, use_global_device_ids=true, to_apply=%region_18.19 | all-reduce | flops 32 | bytes 256 | tf_op jit(solution)/shard_map/psum | solution.py:114
  342.9 102.6 %reduce-scatter.2.cloned.1.call-done = f32[128,1024]{0,1:T(8,128)} async-done(((f32[4096,1024]{0,1:T(8,128)}), f32[128,1024]{0,1:T(8,128)}) %reduce-scatter.2.cloned.1.call-update) | async-done | bytes 524304 | tf_op jit(solution)/shard_map/reduce_scatter | solution.py:105
  445.5 2.0 copy.75
  447.6 34.0 %all-reduce.7.cloned.1.call-done = (f32[1,256,128]{2,1,0:T(8,128)}, f32[1,256,128]{2,1,0:T(8,128)}) async-done(((f32[1,256,128]{2,1,0:T(8,128)}, f32[1,256,128]{2,1,0:T(8,128)}), (f32[1,256,128]{2,1,0:T(8,128)}, f32[1,256,128]{2,1,0:T(8,128)})) %all-reduce.7.cloned.1.call-update) | async-done | bytes 262160 | tf_op jit(solution)/shard_map/psum | solution.py:113
  481.6 1.6 copy.116
  483.2 1.6 copy.117
  (120 shorter events, 7.9 us)
Async XLA Ops:
  7.2 2.5 copy-start
  7.2 83.8 %all-gather.6.cloned.1.call-start = ((), (), s32[]{:S(2)}) async-start(), calls=%async_computation.2 | async-start | bytes 8912896 | tf_op jit(solution)/shard_map/all_gather | solution.py:11
  9.6 102.5 %copy-start.20 = (f32[16,2]{0,1:T(2,128)}, f32[16,2]{0,1:T(2,128)S(1)}, u32[]{:S(2)}) copy-start(f32[16,2]{0,1:T(2,128)S(1)} %slice.21) | copy-start | bytes 388
  9.7 197.1 %copy-start.13 = (f32[256,16]{0,1:T(8,128)}, f32[256,16]{0,1:T(8,128)S(1)}, u32[]{:S(2)}) copy-start(f32[256,16]{0,1:T(8,128)S(1)} %exponential_bitcast_fusion) | copy-start | bytes 49156
  9.7 6.1 %copy-start.8 = (bf16[1,256,128]{2,1,0:T(8,128)(2,1)S(1)}, bf16[1,256,128]{2,1,0:T(8,128)(2,1)}, u32[]{:S(2)}) copy-start(bf16[1,256,128]{2,1,0:T(8,128)(2,1)} %param.14) | copy-start | bytes 196612
  9.7 9.0 %copy-start.25 = (u32[128]{0:T(128)S(1)}, u32[128]{0:T(128)}, u32[]{:S(2)}) copy-start(u32[128]{0:T(128)} %constant.193) | copy-start | bytes 1540
  15.5 1.8 copy-start.3
  15.8 1.6 copy-start.4
  17.3 167.6 %all-gather.8.cloned.1.call-start = ((), (), s32[]{:S(2)}) async-start(), calls=%async_computation.3 | async-start | bytes 8912896 | tf_op jit(solution)/shard_map/all_gather | solution.py:11
  18.6 94.2 %copy-start.2 = (bf16[1,256,1024]{1,2,0:T(8,128)(2,1)}, bf16[1,256,1024]{1,2,0:T(8,128)(2,1)S(1)}, u32[]{:S(2)}) copy-start(bf16[1,256,1024]{1,2,0:T(8,128)(2,1)S(1)} %copy.69) | copy-start | bytes 1572868
  18.6 91.9 %copy-start.6 = (bf16[1,256,128]{2,1,0:T(8,128)(2,1)S(1)}, bf16[1,256,128]{2,1,0:T(8,128)(2,1)}, u32[]{:S(2)}) copy-start(bf16[1,256,128]{2,1,0:T(8,128)(2,1)} %param.13) | copy-start | bytes 196612
  20.0 186.8 %copy-start.16 = (f32[16,256]{1,0:T(8,128)}, f32[16,256]{1,0:T(8,128)S(1)}, u32[]{:S(2)}) copy-start(f32[16,256]{1,0:T(8,128)S(1)} %copy_bitcast_fusion) | copy-start | bytes 49156
  20.2 91.9 %copy-start.21 = (f32[16]{0:T(128)}, f32[16]{0:T(128)S(1)}, u32[]{:S(2)}) copy-start(f32[16]{0:T(128)S(1)} %get-tuple-element.481) | copy-start | bytes 196
  91.0 21.1 %copy-start.11 = (f32[1,16,256]{2,1,0:T(8,128)S(1)}, f32[1,16,256]{2,1,0:T(8,128)}, u32[]{:S(2)}) copy-start(f32[1,16,256]{2,1,0:T(8,128)} %param.15) | copy-start | bytes 49156
  112.1 72.8 %copy-start.9 = (f32[256,16]{0,1:T(8,128)}, f32[256,16]{0,1:T(8,128)S(1)}, u32[]{:S(2)}) copy-start(f32[256,16]{0,1:T(8,128)S(1)} %get-tuple-element.511) | copy-start | bytes 49156
  112.8 72.1 %copy-start.14 = (f32[256,16]{0,1:T(8,128)}, f32[256,16]{0,1:T(8,128)S(1)}, u32[]{:S(2)}) copy-start(f32[256,16]{0,1:T(8,128)S(1)} %get-tuple-element.508) | copy-start | bytes 49156
  114.4 331.1 %reduce-scatter.2.cloned.1.call-start = ((), (), s32[]{:S(2)}) async-start(), calls=%async_computation.1 | async-start | bytes 17301504 | tf_op jit(solution)/shard_map/reduce_scatter | solution.py:105
  116.7 90.1 %copy-start.18 = (pred[256,256]{1,0:T(8,128)(4,1)}, pred[256,256]{1,0:T(8,128)(4,1)S(1)}, u32[]{:S(2)}) copy-start(pred[256,256]{1,0:T(8,128)(4,1)S(1)} %iota_compare_fusion) | copy-start | bytes 196612
  184.9 21.9 %copy-start.23 = (f32[16]{0:T(128)S(1)}, f32[16]{0:T(128)}, u32[]{:S(2)}) copy-start(f32[16]{0:T(128)} %param.17) | copy-start | bytes 196
  219.9 1.0 copy-start.22
  219.9 261.7 %all-reduce.7.cloned.1.call-start = ((), (), s32[]{:S(2)}) async-start(), calls=%async_computation.4 | async-start | bytes 524288 | tf_op jit(solution)/shard_map/psum | solution.py:113
  221.4 5.0 %copy-start.1 = (f32[256,1024]{0,1:T(8,128)S(1)}, f32[256,1024]{0,1:T(8,128)}, u32[]{:S(2)}) copy-start(f32[256,1024]{0,1:T(8,128)} %copy.68) | copy-start | bytes 3145732
  221.4 5.0 %copy-start.5 = (bf16[256,1024]{0,1:T(8,128)(2,1)S(1)}, bf16[256,1024]{0,1:T(8,128)(2,1)}, u32[]{:S(2)}) copy-start(bf16[256,1024]{0,1:T(8,128)(2,1)} %copy-done.4) | copy-start | bytes 1572868
  221.4 5.0 %copy-start.7 = (f32[256,16,64]{0,2,1:T(8,128)S(1)}, f32[256,16,64]{0,2,1:T(8,128)}, u32[]{:S(2)}) copy-start(f32[256,16,64]{0,2,1:T(8,128)} %get-tuple-element.512) | copy-start | bytes 3145732
  221.4 5.0 %copy-start.10 = (f32[256,256]{1,0:T(8,128)S(1)}, f32[256,256]{1,0:T(8,128)}, u32[]{:S(2)}) copy-start(f32[256,256]{1,0:T(8,128)} %fusion.66) | copy-start | bytes 786436
  221.4 5.0 %copy-start.12 = (f32[1,16,256]{2,1,0:T(8,128)S(1)}, f32[1,16,256]{2,1,0:T(8,128)}, u32[]{:S(2)}) copy-start(f32[1,16,256]{2,1,0:T(8,128)} %param.15) | copy-start | bytes 49156
  221.4 5.0 %copy-start.15 = (f32[256,16]{0,1:T(8,128)S(1)}, f32[256,16]{0,1:T(8,128)}, u32[]{:S(2)}) copy-start(f32[256,16]{0,1:T(8,128)} %copy-done.14) | copy-start | bytes 49156
  221.4 5.0 %copy-start.17 = (f32[16,256]{1,0:T(8,128)S(1)}, f32[16,256]{1,0:T(8,128)}, u32[]{:S(2)}) copy-start(f32[16,256]{1,0:T(8,128)} %copy-done.16) | copy-start | bytes 49156
  221.4 5.0 %copy-start.19 = (pred[256,256]{1,0:T(8,128)(4,1)S(1)}, pred[256,256]{1,0:T(8,128)(4,1)}, u32[]{:S(2)}) copy-start(pred[256,256]{1,0:T(8,128)(4,1)} %copy-done.18) | copy-start | bytes 196612
  221.4 5.0 %copy-start.24 = (f32[16]{0:T(128)S(1)}, f32[16]{0:T(128)}, u32[]{:S(2)}) copy-start(f32[16]{0:T(128)} %param.17) | copy-start | bytes 196
Sparse Core Ops, SparseCore 0:
  17.4 73.5 all-gather.5
  114.5 70.3 all-gather.7
  220.0 225.4 reduce-scatter.1
  448.5 33.0 all-reduce.6
where the time goes:
time: 495 us; the launch traced here: 491 us
  waiting for transfers between devices  232 us (47%)
  blocking collectives  137 us (28%)
  other arithmetic  47.9 us (10%)
  matrix products  43.2 us (9%)
  between operations  14.8 us (3%)
  local copies, waits for them, and re-layouts  14.3 us (3%)
    reduce_scatter x1, waiting for transfers between devices, body(): lax.psum_scatter(lax.dot_general(cotangent, mixed_bf, (((0,), (0,)), ((),...  103 us
    all_gather x2, waiting for transfers between devices, prefix(): everything = jax.tree.map(lambda part: lax.all_gather(part, axis), value)  95.6 us
    psum x1, blocking collectives, body(): d_rates, d_skip = lax.psum((grad_rates, grad_skip), ('dp', 'ctx'))  95.4 us
    unnamed x1, blocking collectives  42.1 us
    select_n x32, other arithmetic, hop(): return jax.tree.map(lambda a, b: jnp.where(reached, a, b), new, before)  37.6 us
    psum x1, waiting for transfers between devices, body(): d_b, d_c = lax.psum((grad_b, grad_c), 'tensor')  34 us
    dot_general x3, matrix products, advance(): inside = jnp.einsum('hij,jhp->ihp', mixing, vals_one, precision=high)  13.5 us
  transfers between devices with their start and end apart: 4, of which 4 were waited for; matrix products, arithmetic and copies ran while one was open for 7% of the time, Pallas kernels for 0%

commit v1 on v0

v1 whole, which is shorter than its diff:
```python
import functools

import jax
import jax.numpy as jnp
from jax import lax
from jax.experimental import pallas as pl
from jax.experimental.pallas import tpu as pltpu
from jax.sharding import PartitionSpec as P

F32 = jnp.float32
BF16 = jnp.bfloat16
NEG = -1e30
SIDE = 4


def dot(a, b, ca=1, cb=0):
    return lax.dot_general(a, b, (((ca,), (cb,)), ((), ())), preferred_element_type=F32)


def call(kernel, outs, name, scratch=(), scalars=0, flops=0, nbytes=0):
    vmem = pl.BlockSpec(memory_space=pltpu.VMEM)

    def run(*args):
        specs = [pl.BlockSpec(memory_space=pltpu.SMEM)] * scalars + [vmem] * (len(args) - scalars)
        return pl.pallas_call(
            kernel,
            out_shape=outs,
            in_specs=specs,
            out_specs=jax.tree.map(lambda _: vmem, outs),
            scratch_shapes=list(scratch),
            compiler_params=pltpu.CompilerParams(vmem_limit_bytes=56 * 1024 * 1024),
            cost_estimate=pl.CostEstimate(flops=flops, bytes_accessed=nbytes, transcendentals=0),
            name=name,
        )(*args)

    return run


def scan_lanes(x, reverse=False):
    n = x.shape[1]
    lane = lax.broadcasted_iota(jnp.int32, x.shape, 1)
    k = 1
    while k < n:
        if reverse:
            x = x + jnp.where(lane < n - k, pltpu.roll(x, n - k, 1), 0.0)
        else:
            x = x + jnp.where(lane >= k, pltpu.roll(x, k, 1), 0.0)
        k *= 2
    return x


def prep_kernel(pos, d_ref, z1, z2, z3, x1, x2, x3, oz, ox):
    dp, x, z, core = pos[0], pos[1], pos[2], pos[3]

    def column(d, xx, zz):
        at = (d * SIDE + lax.rem(xx, SIDE)) * SIDE + lax.rem(zz, SIDE)
        return d_ref[:, pl.ds(pl.multiple_of(at * 128, 128), 128)]

    mine = lax.rem(dp + core, 2)
    for k, (zr, xr) in enumerate(((z1, x1), (z2, x2), (z3, x3)), 1):
        for r in range(SIDE):
            cols = slice(r * 128, (r + 1) * 128)
            zr[:, cols] = column(mine, x + r, z + k).astype(F32)
            xr[:, cols] = column(mine, x + k, z + r).astype(F32)
    for kd in range(2):
        d = lax.rem(dp + kd, 2)
        for r in range(SIDE):
            cols = slice(r * 128, (r + 1) * 128)
            oz[kd, :, cols] = column(d, x + r, z)
            ox[kd, :, cols] = column(d, x, z + r)


def ends_kernel(v_ref, b_ref, s_ref, r_ref, vt_ref, end_ref, run_ref, *, length):
    heads, tokens = s_ref.shape
    width = v_ref.shape[1] // heads
    run = scan_lanes(s_ref[...] * (r_ref[...] * (-1.0 / length)))
    run_ref[...] = run
    last = run[:, tokens - 1 :]
    tail = jnp.exp(last - run) * s_ref[...]
    total = jnp.exp(last)
    b = b_ref[...]
    per = 128 // width
    for h in range(0, heads, per):
        vt = v_ref[:, h * width : (h + per) * width].astype(F32).T
        vt_ref[h * width : (h + per) * width, :] = vt.astype(BF16)
        for k in range(per):
            scaled = vt[k * width : (k + 1) * width] * tail[h + k : h + k + 1]
            end_ref[h + k, :width, :] = dot(scaled.astype(BF16), b)
            end_ref[h + k, width:, :] = jnp.broadcast_to(total[h + k : h + k + 1], (8, 128))


def before_kernel(e_ref, o_ref, keep_ref):
    shards, rows, _ = o_ref.shape
    state = jnp.zeros(o_ref.shape[1:], F32)
    for k in range(shards):
        o_ref[k] = state
        decay = e_ref[k, rows:, :]
        keep_ref[k] = decay
        if k < shards - 1:
            state = state * decay[0:1] + e_ref[k, :rows, :]


def after_kernel(e_ref, keep_ref, o_ref):
    shards = o_ref.shape[0]
    state = jnp.zeros(o_ref.shape[1:], F32)
    for k in reversed(range(shards)):
        o_ref[k] = state
        if k:
            state = state * keep_ref[k, 0:1] + e_ref[k]


def columns_of(run, wide_ref):
    heads, tokens = run.shape
    turned = jnp.concatenate([run, jnp.zeros((128 - heads, tokens), F32)], 0).T
    for h in range(heads):
        wide_ref[h] = jnp.broadcast_to(turned[:, h : h + 1], (tokens, 128))


def weights_of(wide, row, steps, tokens):
    i = lax.broadcasted_iota(jnp.int32, (tokens, tokens), 0)
    j = lax.broadcasted_iota(jnp.int32, (tokens, tokens), 1)
    between = jnp.concatenate([wide] * (tokens // 128), 1) - row
    return jnp.exp(jnp.where(i >= j, between, NEG)) * steps


def mix_kernel(g_ref, vt_ref, b_ref, c_ref, s_ref, run_ref, sin_ref, ma_ref, mb_ref, wide_ref, g2_ref):
    heads, tokens = s_ref.shape
    width = vt_ref.shape[0] // heads
    columns_of(run_ref[...], wide_ref)
    g2_ref[...] = dot(c_ref[...], b_ref[...], 1, 1)
    half = heads // 2

    def head(h, out_ref, base):
        row = run_ref[pl.ds(h, 1), :]
        mix = (weights_of(wide_ref[h], row, s_ref[pl.ds(h, 1), :], tokens) * g2_ref[...]).astype(BF16)
        at = pl.ds(pl.multiple_of(h * width, width), width)
        v = vt_ref[at, :]
        inside = dot(v, mix, 1, 1)
        carried = dot(sin_ref[h].astype(BF16), c_ref[...], 1, 1) * jnp.exp(row)
        to = pl.ds(pl.multiple_of((h - base) * width, width), width)
        out_ref[to, :] = inside + carried + g_ref[h] * v.astype(F32)

    lax.fori_loop(0, half, lambda h, _: head(h, ma_ref, 0), None, unroll=2)
    lax.fori_loop(half, heads, lambda h, _: head(h, mb_ref, half), None, unroll=2)


def grad_ends_kernel(ut_ref, c_ref, run_ref, o_ref):
    heads, width, _ = o_ref.shape
    grow = jnp.exp(run_ref[...])
    c = c_ref[...]
    for h in range(heads):
        scaled = ut_ref[h * width : (h + 1) * width, :].astype(F32) * grow[h : h + 1]
        o_ref[h] = dot(scaled.astype(BF16), c)


def back_kernel(
    g_ref, ut_ref, vt_ref, b_ref, c_ref, s_ref, run_ref, r_ref, sin_ref, gs_ref, ma_ref, mb_ref,
    dv_ref, dbc_ref, ds_ref, small_ref,
    wide_ref, g2_ref, ct_ref, bt_ref, ue_ref, vw_ref, r1_ref, q_ref, add_ref, skip_ref, dbt_ref, dct_ref, dvt_ref,
    *, length,
):
    heads, tokens = s_ref.shape
    width = vt_ref.shape[0] // heads
    half = heads // 2
    columns_of(run_ref[...], wide_ref)
    g2_ref[...] = dot(c_ref[...], b_ref[...], 1, 1)
    ct_ref[...] = c_ref[...].astype(F32).T.astype(BF16)
    bt_ref[...] = b_ref[...].astype(F32).T.astype(BF16)
    dbt_ref[...] = jnp.zeros_like(dbt_ref)
    dct_ref[...] = jnp.zeros_like(dct_ref)

    def head(h, mixed_ref, base):
        row = run_ref[pl.ds(h, 1), :]
        steps = s_ref[pl.ds(h, 1), :]
        last = row[:, tokens - 1 :]
        at = pl.ds(pl.multiple_of(h * width, width), width)
        v, u = vt_ref[at, :], ut_ref[at, :]
        vf, uf = v.astype(F32), u.astype(F32)
        weights = weights_of(wide_ref[h], row, steps, tokens)
        mix = (weights * g2_ref[...]).astype(BF16)
        pair = dot(u, v, 0, 0)
        dg = (pair * weights).astype(BF16)
        dct_ref[...] += dot(bt_ref[...], dg, 1, 1)
        dbt_ref[...] += dot(ct_ref[...], dg, 1, 0)
        tail = jnp.exp(last - row) * steps
        ue_ref[at, :] = (uf * jnp.exp(row)).astype(BF16)
        vw_ref[at, :] = (vf * tail).astype(BF16)
        gs = gs_ref[h]
        far = dot(gs.astype(BF16), bt_ref[...]) * tail
        near = dot(u, mix)
        both = near + far
        gain = g_ref[h]
        dvt_ref[at, :] = both + gain * uf
        out = mixed_ref[pl.ds(pl.multiple_of((h - base) * width, width), width), :] - gain * vf
        r1_ref[pl.ds(h, 1), :] = jnp.sum(uf * out, 0, keepdims=True)
        q_ref[pl.ds(h, 1), :] = jnp.sum(vf * both, 0, keepdims=True)
        kept = jnp.sum(sin_ref[h] * gs, 0, keepdims=True) * jnp.exp(last)
        add_ref[pl.ds(h, 1), :] = jnp.sum(vf * far, 0, keepdims=True) + jnp.concatenate(
            [kept, jnp.zeros((1, tokens - 128), F32)], 1
        )
        skip_ref[pl.ds(h, 1), :] = jnp.sum(uf * vf, 0, keepdims=True)

    lax.fori_loop(0, half, lambda h, _: head(h, ma_ref, 0), None, unroll=2)
    lax.fori_loop(half, heads, lambda h, _: head(h, mb_ref, half), None, unroll=2)

    states = sin_ref.shape[0] * sin_ref.shape[1]
    sin_t = sin_ref[...].reshape(states, 128).T.astype(BF16)
    gs_t = gs_ref[...].reshape(states, 128).T.astype(BF16)
    dbc_ref[0] = (dbt_ref[...] + dot(gs_t, vw_ref[...])).T
    dbc_ref[1] = (dct_ref[...] + dot(sin_t, ue_ref[...])).T
    for k in range(0, heads * width, 128):
        dv_ref[:, k : k + 128] = dvt_ref[k : k + 128, :].T.astype(BF16)
    dlog = scan_lanes(r1_ref[...] - q_ref[...], reverse=True) + jnp.sum(add_ref[...], 1, keepdims=True)
    s = s_ref[...]
    ds_ref[...] = q_ref[...] / s - dlog * (r_ref[...] * (1.0 / length))
    rates = jnp.sum(s * dlog, 1, keepdims=True) * (-1.0 / length)
    skips = jnp.sum(skip_ref[...], 1, keepdims=True)
    lane = lax.broadcasted_iota(jnp.int32, (heads, 128), 1)
    small_ref[...] = jnp.where(lane == 0, rates, jnp.where(lane == 1, skips, 0.0))


def grad_w_kernel(core, m0, m1, m2, m3, own, d1, d2, d3, e_ref, o0, o1, o2, o3):
    outs = (o0, o1, o2, o3)
    ms = [m[...].astype(BF16) for m in (m0, m1, m2, m3)]
    ds = (d1, d2, d3)
    me = core[0]
    for kd in range(2):
        at = me if kd == 0 else 1 - me
        acc = dot(ms[0], own[at])
        for k in range(3):
            piece = ds[k][...] if kd == 0 else e_ref[k]
            acc += dot(ms[k + 1], piece.astype(BF16))
        for r in range(SIDE):
            outs[r][at] = acc[:, r * 128 : (r + 1) * 128]


def gather_sum_kernel(a0, a1, a2, a3, b0, b1, b2, b3, keep_ref, send_ref):
    n = a0.shape[1]
    for at, (w, x, y, z) in ((0, (a0, a1, a2, a3)), (n, (b0, b1, b2, b3))):
        keep_ref[at : at + n, :] = w[0] + x[0] + y[0] + z[0]
        send_ref[at : at + n, :] = w[1] + x[1] + y[1] + z[1]


def finish_kernel(a_ref, b_ref, o_ref):
    o_ref[...] = (a_ref[...] + b_ref[...]).T


def body(values, b_proj, c_proj, step_sizes, decay_rates, skip_gain, w_out, d_out):
    tokens, channels = values.shape[1:]
    state = b_proj.shape[2]
    heads = decay_rates.shape[0]
    width = channels // heads
    shards = lax.axis_size("ctx")
    length = tokens * shards
    half = channels // 2
    sds = jax.ShapeDtypeStruct

    place = lax.axis_index("ctx")
    dp = lax.axis_index("dp")
    core = lax.rem(lax.axis_index("tensor"), 2)
    pos = jnp.stack([dp, place // SIDE, lax.rem(place, SIDE), core]).astype(jnp.int32)

    def shift(value, dx, dz):
        pairs = [
            (x * SIDE + z, ((x + dx) % SIDE) * SIDE + (z + dz) % SIDE)
            for x in range(SIDE)
            for z in range(SIDE)
        ]
        return lax.ppermute(value, "ctx", pairs)

    def other_core(value):
        return lax.ppermute(value, "tensor", [(0, 1), (1, 0), (2, 3), (3, 2)])

    def other_chip(value):
        return lax.ppermute(value, "tensor", [(0, 2), (2, 0), (1, 3), (3, 1)])

    def other_dp(value):
        return lax.ppermute(value, "dp", [(0, 1), (1, 0)])

    def spread(value):
        return lax.all_to_all(value, "ctx", 0, 0, tiled=True)

    v, b, c, steps, cot = values[0], b_proj[0], c_proj[0], step_sizes[0], d_out[0]
    rates = decay_rates[:, None]

    piece = sds((tokens, 4 * 128), F32)
    own = sds((2, tokens, 4 * 128), BF16)
    z1, z2, z3, x1, x2, x3, own_z, own_x = call(
        prep_kernel, (piece,) * 6 + (own, own), "prep", scalars=1, nbytes=7 << 20
    )(pos, cot)
    vt, ends, run = call(
        functools.partial(ends_kernel, length=length),
        (sds((channels, tokens), BF16), sds((heads, width + 8, state), F32), sds((heads, tokens), F32)),
        "ends",
        nbytes=2 << 20,
        flops=1 << 26,
    )(v, b, steps, rates)
    z1, z2, z3 = shift(z1, 0, 1), shift(z2, 0, 2), shift(z3, 0, 3)
    x1, x2, x3 = shift(x1, 1, 0), shift(x2, 2, 0), shift(x3, 3, 0)

    before, keep = call(
        before_kernel, (sds((shards, width, state), F32), sds((shards, 8, state), F32)), "before", nbytes=1 << 20
    )(spread(ends))
    state_in = spread(before)

    wide = pltpu.VMEM((heads, tokens, 128), F32)
    square = pltpu.VMEM((tokens, tokens), F32)
    mixed_a, mixed_b = call(
        mix_kernel, (sds((half, tokens), F32),) * 2, "mix", (wide, square), scalars=1, nbytes=4 << 20, flops=1 << 28
    )(skip_gain, vt, b, c, steps, run, state_in)

    a1, a2, a3 = shift(mixed_a, 0, 1), shift(mixed_a, 0, 2), shift(mixed_a, 0, 3)
    b1, b2, b3 = shift(mixed_b, 1, 0), shift(mixed_b, 2, 0), shift(mixed_b, 3, 0)

    swapped = other_core(jnp.stack([z1, z2, z3, x1, x2, x3]))
    up_t = lax.dot_general(w_out, cot, (((0,), (1,)), ((), ())), preferred_element_type=F32).astype(BF16)
    grad_ends = call(grad_ends_kernel, sds((heads, width, state), F32), "grad_ends", nbytes=2 << 20, flops=1 << 26)(
        up_t, c, run
    )
    after = call(after_kernel, sds((shards, width, state), F32), "after", nbytes=1 << 20)(spread(grad_ends), keep)
    grad_out = spread(after)

    out = (sds((2, half, 128), F32),) * 4
    flops = 2 * half * 4 * tokens * 1024
    pa = call(grad_w_kernel, out, "grad_w_a", scalars=1, flops=flops, nbytes=8 << 20)(
        core[None].astype(jnp.int32), mixed_a, a1, a2, a3, own_z, z1, z2, z3, swapped[:3]
    )
    pb = call(grad_w_kernel, out, "grad_w_b", scalars=1, flops=flops, nbytes=8 << 20)(
        core[None].astype(jnp.int32), mixed_b, b1, b2, b3, own_x, x1, x2, x3, swapped[3:]
    )
    ra = [pa[0]] + [shift(pa[k], k, 0) for k in range(1, SIDE)]
    rb = [pb[0]] + [shift(pb[k], 0, k) for k in range(1, SIDE)]

    dv, dbc, dsteps, small = call(
        functools.partial(back_kernel, length=length),
        (
            sds((tokens, channels), BF16),
            sds((2, tokens, state), F32),
            sds((heads, tokens), F32),
            sds((heads, 128), F32),
        ),
        "back",
        (
            wide, square, pltpu.VMEM((state, tokens), BF16), pltpu.VMEM((state, tokens), BF16),
            pltpu.VMEM((channels, tokens), BF16), pltpu.VMEM((channels, tokens), BF16),
            pltpu.VMEM((heads, tokens), F32), pltpu.VMEM((heads, tokens), F32),
            pltpu.VMEM((heads, tokens), F32), pltpu.VMEM((heads, tokens), F32),
            pltpu.VMEM((state, tokens), F32), pltpu.VMEM((state, tokens), F32),
            pltpu.VMEM((channels, tokens), F32),
        ),
        scalars=1,
        flops=1 << 30,
        nbytes=6 << 20,
    )(skip_gain, up_t, vt, b, c, steps, run, rates, state_in, grad_out, mixed_a, mixed_b)

    dbc = dbc + other_core(dbc)
    dbc = dbc + other_chip(dbc)
    small = spread(jnp.broadcast_to(small[None], (shards,) + small.shape)).sum(0)
    small = small + other_dp(small)

    kept, sent = call(gather_sum_kernel, (sds((channels, 128), F32),) * 2, "gather_sum", nbytes=5 << 20)(*ra, *rb)
    d_w = call(finish_kernel, sds((128, channels), F32), "finish", nbytes=2 << 20)(kept, other_dp(sent))
    return (dv[None], dbc[0][None], dbc[1][None], dsteps[None], small[:, 0], small[:, 1], d_w)


def solution(mesh):
    return jax.shard_map(
        body,
        mesh=mesh,
        in_specs=(
            P("dp", "ctx", "tensor"),
            P("dp", "ctx", None),
            P("dp", "ctx", None),
            P("dp", "tensor", "ctx"),
            P("tensor"),
            P("tensor"),
            P(None, "tensor"),
            P("dp", "ctx", None),
        ),
        out_specs=(
            P("dp", "ctx", "tensor"),
            P("dp", "ctx", None),
            P("dp", "ctx", None),
            P("dp", "tensor", "ctx"),
            P("tensor"),
            P("tensor"),
            P(("dp", "ctx"), "tensor"),
        ),
        check_vma=False,
    )
```

time: 495 us -> 207 us (0.42)
  waiting for transfers between devices: 232 us -> 38.3 us
  blocking collectives: 137 us -> 51.8 us
  starting transfers between devices: 0.34 us -> 51.6 us
  other arithmetic: 47.9 us -> 0.67 us
  Pallas kernels: 0 us -> 44.7 us
  matrix products: 43.2 us -> 6.57 us
  between operations: 14.8 us -> 0.86 us
    reduce_scatter x1 -> x0, waiting for transfers between devices: 103 us -> none  [body(): lax.psum_scatter(lax.dot_general(cotangent, mixed_bf, (((0,), (0,)), ((),...]
    all_gather x2 -> x0, waiting for transfers between devices: 95.6 us -> none  [prefix(): everything = jax.tree.map(lambda part: lax.all_gather(part, axis), value)]
    psum x1 -> x0, blocking collectives: 95.4 us -> none  [body(): d_rates, d_skip = lax.psum((grad_rates, grad_skip), ('dp', 'ctx'))]
    all_to_all x0 -> x3, blocking collectives: none -> 51.8 us  [spread(): return lax.all_to_all(value, 'ctx', 0, 0, tiled=True)]
    pallas_call x0 -> x11, Pallas kernels: none -> 44.7 us  [run(): pl.pallas_call(kernel, out_shape=outs, in_specs=specs, out_specs=jax.tree...]
    ppermute x0 -> x23, starting transfers between devices: none -> 43.5 us  [the longest x18 37.5 us: shift(): return lax.ppermute(value, 'ctx', pairs)]
    unnamed x1 -> x0, blocking collectives: 42.1 us -> none
    ppermute x0 -> x23, waiting for transfers between devices: none -> 38.3 us  [the longest x18 35 us: shift(): return lax.ppermute(value, 'ctx', pairs)]
  transfers between devices with their start and end apart: 4 -> 25, of which waited for: 4 -> 7; matrix products, arithmetic and copies ran while one was open for 7% -> 7% of each run, Pallas kernels for 0% -> 19%
where the time goes in v1:
time: 207 us
  blocking collectives  51.8 us (25%)
  starting transfers between devices  51.6 us (25%)
  Pallas kernels  44.7 us (22%)
  waiting for transfers between devices  38.3 us (19%)
  local copies, waits for them, and re-layouts  12.1 us (6%)
  matrix products  6.57 us (3%)
    all_to_all x3, blocking collectives, spread(): return lax.all_to_all(value, 'ctx', 0, 0, tiled=True)  51.8 us
    pallas_call x11, Pallas kernels, run(): pl.pallas_call(kernel, out_shape=outs, in_specs=specs, out_specs=jax.tree...  44.7 us
    ppermute x18, starting transfers between devices, shift(): return lax.ppermute(value, 'ctx', pairs)  37.5 us
    ppermute x18, waiting for transfers between devices, shift(): return lax.ppermute(value, 'ctx', pairs)  35 us
    all_to_all x2, starting transfers between devices, spread(): return lax.all_to_all(value, 'ctx', 0, 0, tiled=True)  8.15 us
    unnamed x39, local copies, waits for them, and re-layouts  7.01 us
    dot_general x1, matrix products, body(): lax.dot_general(w_out, cot, (((0,), (1,)), ((), ())), preferred_element_t...  6.57 us
    ppermute x2, starting transfers between devices, other_dp(): return lax.ppermute(value, 'dp', [(0, 1), (1, 0)])  5.11 us
  transfers between devices with their start and end apart: 25, of which 7 were waited for; matrix products, arithmetic and copies ran while one was open for 7% of the time, Pallas kernels for 19%

profile of v1, /device:TPU:0, one launch (start us, length us, event | category | flops | bytes accessed | tf_op | source)
XLA Modules:
  0.0 206.7 jit_solution(12694671791848582470)
XLA Ops:
  0.6 0.6 pad_add_fusion.pos
  1.2 4.3 %prep.1 = (f32[256,512]{1,0:T(8,128)}, f32[256,512]{1,0:T(8,128)}, f32[256,512]{1,0:T(8,128)}, f32[256,512]{1,0:T(8,128)}, f32[256,512]{1,0:T(8,128)}, /*index=5...) custom-call(s32[4]{0:T(128)} %pad_add_fusion.pos, bf16[256,4096]{1,0:T(8,128)(2,1)} %bitcast.27), custom_call_target="tpu_custom_call" | custom-call | bytes 7340032 | tf_op jit(solution)/shard_map/prep/pallas_call | solution.py:25
  5.5 2.0 collective-permute-start.6
  7.5 3.6 %collective-permute-start.7 = (f32[256,512]{1,0:T(8,128)}, f32[256,512]{1,0:T(8,128)S(1)}, u32[]{:S(2)}, u32[]{:S(2)}) collective-permute-start(f32[256,512]{1,0:T(8,128)} %get-tuple-element.49), channel_id=1, source_target_pairs={{0,8},{4,12},{8,0},{12,4},{16,24},{20,28},{24,16},{28,20},{32,40},... | collective-permute-start | bytes 1572872 | tf_op jit(solution)/shard_map/ppermute | solution.py:269
  11.1 1.0 collective-permute-start.8
  12.1 1.5 collective-permute-start.9
  13.6 2.7 %collective-permute-start.10 = (f32[256,512]{1,0:T(8,128)}, f32[256,512]{1,0:T(8,128)S(1)}, u32[]{:S(2)}, u32[]{:S(2)}) collective-permute-start(f32[256,512]{1,0:T(8,128)} %get-tuple-element.52), channel_id=1, source_target_pairs={{0,32},{4,36},{8,40},{12,44},{16,48},{20,52},{24,56},{28,60},{32,0... | collective-permute-start | bytes 1572872 | tf_op jit(solution)/shard_map/ppermute | solution.py:269
  16.3 5.4 %collective-permute-done.6.d1 = f32[256,512]{1,0:T(8,128)S(1)} collective-permute-done((f32[256,512]{1,0:T(8,128)}, f32[256,512]{1,0:T(8,128)S(1)}, u32[]{:S(2)}, u32[]{:S(2)}) %collective-permute-start.6) | collective-permute-done | bytes 524320 | tf_op jit(solution)/shard_map/ppermute | solution.py:269
  21.7 2.7 %collective-permute-start.11 = (f32[256,512]{1,0:T(8,128)}, f32[256,512]{1,0:T(8,128)S(1)}, u32[]{:S(2)}, u32[]{:S(2)}) collective-permute-start(f32[256,512]{1,0:T(8,128)} %get-tuple-element.53), channel_id=1, source_target_pairs={{0,48},{4,52},{8,56},{12,60},{16,0},{20,4},{24,8},{28,12},{32,16},... | collective-permute-start | bytes 1572872 | tf_op jit(solution)/shard_map/ppermute | solution.py:269
  24.5 0.9 bitcast_dynamic-update-slice_fusion.5
  25.4 8.8 %collective-permute-done.7.d2 = f32[256,512]{1,0:T(8,128)S(1)} collective-permute-done((f32[256,512]{1,0:T(8,128)}, f32[256,512]{1,0:T(8,128)S(1)}, u32[]{:S(2)}, u32[]{:S(2)}) %collective-permute-start.7) | collective-permute-done | bytes 524320 | tf_op jit(solution)/shard_map/ppermute | solution.py:269
  34.2 0.9 bitcast_dynamic-update-slice_fusion.4
  35.0 0.0 collective-permute-done.8.d3
  35.0 0.9 bitcast_dynamic-update-slice_fusion.3
  35.9 0.9 bitcast_dynamic-update-slice_fusion.2
  36.8 1.7 collective-permute-done.10.d2
  38.5 0.9 bitcast_dynamic-update-slice_fusion.1
  39.4 0.9 bitcast_dynamic-update-slice_fusion
  40.4 0.0 collective-permute-start.12
  40.4 0.0 copy-done.5
  40.4 0.7 copy.19.r_ref
  41.1 3.1 %ends.1 = (bf16[1024,256]{1,0:T(8,128)(2,1)}, f32[16,72,128]{2,1,0:T(8,128)}, f32[16,256]{1,0:T(8,128)}) custom-call(bf16[256,1024]{1,0:T(8,128)(2,1)} %bitcast.28, bf16[256,128]{1,0:T(8,128)(2,1)} %bitcast.29, f32[16,256]{1,0:T(8,128)} %bitcast.35, f32[16,1]{1,0:T(8,128)} %copy.19.r_ref), custom_call_target="tpu_custom_call" | custom-call | flops 67108864 | bytes 2097152 | tf_op jit(solution)/shard_map/ends/pallas_call | solution.py:25
  44.2 22.3 %all_to_all.25.e_ref = f32[16,72,128]{2,1,0:T(8,128)} all-to-all(f32[16,72,128]{2,1,0:T(8,128)} %get-tuple-element.38), channel_id=1, replica_groups=mesh['dp'=2,'ctx'=16,'tensor'=4] {'ctx'}, dimensions={0} | all-to-all | bytes 1179648 | tf_op jit(solution)/shard_map/all_to_all | solution.py:281
  66.5 1.9 before.1
  68.4 15.3 %all_to_all.26.sin_ref = f32[16,64,128]{2,1,0:T(8,128)} all-to-all(f32[16,64,128]{2,1,0:T(8,128)} %get-tuple-element.39), channel_id=1, replica_groups=mesh['dp'=2,'ctx'=16,'tensor'=4] {'ctx'}, dimensions={0} | all-to-all | bytes 1048576 | tf_op jit(solution)/shard_map/all_to_all | solution.py:281
  83.7 4.9 %mix.1 = (f32[512,256]{1,0:T(8,128)}, f32[512,256]{1,0:T(8,128)}) custom-call(f32[16]{0:T(128)} %g_ref.3, bf16[1024,256]{1,0:T(8,128)(2,1)} %get-tuple-element.36.vt_ref, bf16[256,128]{1,0:T(8,128)(2,1)} %bitcast.30, bf16[256,128]{1,0:T(8,128)(2,1)} %bitcast.32, f32[16,256]{1,0:T(8,128)} %bitcast.36, f32[16,256]{1,0:T(8,128)} %get-tuple-element.37.run_ref, ...), custom_call_target="tpu_custom_call" | custom-call | flops 268435456 | bytes 4194304 | tf_op jit(solution)/shard_map/mix/pallas_call | solution.py:25
  88.6 2.5 %collective-permute-start.17 = (f32[512,256]{1,0:T(8,128)}, f32[512,256]{1,0:T(8,128)}, u32[]{:S(2)}, u32[]{:S(2)}) collective-permute-start(f32[512,256]{1,0:T(8,128)} %get-tuple-element.42.mb_ref.m0), channel_id=1, source_target_pairs={{0,32},{4,36},{8,40},{12,44},{16,48},{20,52},{24,56},{28,60},{32,0... | collective-permute-start | bytes 1572872 | tf_op jit(solution)/shard_map/ppermute | solution.py:269
  91.2 1.2 collective-permute-start.18
  92.4 6.6 %convolution_convert_fusion.ut_ref = bf16[1024,256]{1,0:T(8,128)(2,1)} fusion(bf16[4096,1024]{1,0:T(8,128)(2,1)} %param.14, bf16[1,256,4096]{2,1,0:T(8,128)(2,1)S(1)} %copy-done.6), kind=kOutput, calls=%fused_computation | convolution fusion | flops 2147745792 | bytes 11010048 | tf_op jit(solution)/shard_map/dot_general | solution.py:316
  99.0 2.2 %grad_ends.1 = f32[16,64,128]{2,1,0:T(8,128)} custom-call(bf16[1024,256]{1,0:T(8,128)(2,1)} %convolution_convert_fusion.ut_ref, bf16[256,128]{1,0:T(8,128)(2,1)} %bitcast.33, f32[16,256]{1,0:T(8,128)} %get-tuple-element.37.run_ref), custom_call_target="tpu_custom_call" | custom-call | flops 67108864 | bytes 2097152 | tf_op jit(solution)/shard_map/grad_ends/pallas_call | solution.py:25
  101.1 4.4 %all-to-all-start.2 = ((f32[16,64,128]{2,1,0:T(8,128)}), f32[16,64,128]{2,1,0:T(8,128)}, u32[]{:S(2)}, u32[]{:S(2)}) async-start(f32[16,64,128]{2,1,0:T(8,128)} %grad_ends.1), calls=%async_computation.2 | async-start | bytes 1048576 | tf_op jit(solution)/shard_map/all_to_all | solution.py:281
  105.5 1.9 collective-permute-start.3
  107.4 2.7 %collective-permute-start.4 = (f32[512,256]{1,0:T(8,128)}, f32[512,256]{1,0:T(8,128)}, u32[]{:S(2)}, u32[]{:S(2)}) collective-permute-start(f32[512,256]{1,0:T(8,128)} %get-tuple-element.41.ma_ref.m0), channel_id=1, source_target_pairs={{0,8},{4,12},{8,0},{12,4},{16,24},{20,28},{24,16},{28,20},{32,40},... | collective-permute-start | bytes 1572872 | tf_op jit(solution)/shard_map/ppermute | solution.py:269
  110.1 6.9 %collective-permute-start.5 = (f32[512,256]{1,0:T(8,128)}, f32[512,256]{1,0:T(8,128)}, u32[]{:S(2)}, u32[]{:S(2)}) collective-permute-start(f32[512,256]{1,0:T(8,128)} %get-tuple-element.41.ma_ref.m0), channel_id=1, source_target_pairs={{0,12},{4,0},{8,4},{12,8},{16,28},{20,16},{24,20},{28,24},{32,44},... | collective-permute-start | bytes 1572872 | tf_op jit(solution)/shard_map/ppermute | solution.py:269
  117.0 2.1 fusion.1
  119.0 5.3 %grad_w_b.1 = (f32[2,512,128]{2,1,0:T(8,128)}, f32[2,512,128]{2,1,0:T(8,128)}, f32[2,512,128]{2,1,0:T(8,128)}, f32[2,512,128]{2,1,0:T(8,128)}) custom-call(s32[1]{0:T(128)} %bitcast.8.core, f32[512,256]{1,0:T(8,128)} %get-tuple-element.42.mb_ref.m0, f32[512,256]{1,0:T(8,128)} %collective-permute-done.16.m1, f32[512,256]{1,0:T(8,128)} %collective-permute-done.17.m2, ...), custom_call_target="tpu_custom_call" | custom-call | flops 1073741824 | bytes 8388608 | tf_op jit(solution)/shard_map/grad_w_b/pallas_call | solution.py:25
  124.4 0.9 collective-permute-start.19
  125.2 1.9 after.1
  127.1 3.8 %all-to-all-start.3 = ((f32[16,64,128]{2,1,0:T(8,128)}), f32[16,64,128]{2,1,0:T(8,128)S(1)}, u32[]{:S(2)}, u32[]{:S(2)}) async-start(f32[16,64,128]{2,1,0:T(8,128)} %after.1), calls=%async_computation.3 | async-start | bytes 1048576 | tf_op jit(solution)/shard_map/all_to_all | solution.py:281
  130.9 3.4 %collective-permute-start.20 = (f32[2,512,128]{2,1,0:T(8,128)}, f32[2,512,128]{2,1,0:T(8,128)S(1)}, u32[]{:S(2)}, u32[]{:S(2)}) collective-permute-start(f32[2,512,128]{2,1,0:T(8,128)} %get-tuple-element.61), channel_id=1, source_target_pairs={{0,8},{4,12},{8,0},{12,4},{16,24},{20,28},{24,16},{28,20},{32,40},... | collective-permute-start | bytes 1572872 | tf_op jit(solution)/shard_map/ppermute | solution.py:269
  134.3 0.0 collective-permute-done.3.m1
  134.3 1.2 collective-permute-start.21
  135.5 7.6 %collective-permute-done.4.m2 = f32[512,256]{1,0:T(8,128)} collective-permute-done((f32[512,256]{1,0:T(8,128)}, f32[512,256]{1,0:T(8,128)}, u32[]{:S(2)}, u32[]{:S(2)}) %collective-permute-start.4) | collective-permute-done | bytes 524320 | tf_op jit(solution)/shard_map/ppermute | solution.py:269
  143.1 5.7 %collective-permute-done.5.m3 = f32[512,256]{1,0:T(8,128)} collective-permute-done((f32[512,256]{1,0:T(8,128)}, f32[512,256]{1,0:T(8,128)}, u32[]{:S(2)}, u32[]{:S(2)}) %collective-permute-start.5) | collective-permute-done | bytes 524320 | tf_op jit(solution)/shard_map/ppermute | solution.py:269
  148.8 5.3 %grad_w_a.1 = (f32[2,512,128]{2,1,0:T(8,128)}, f32[2,512,128]{2,1,0:T(8,128)}, f32[2,512,128]{2,1,0:T(8,128)}, f32[2,512,128]{2,1,0:T(8,128)}) custom-call(s32[1]{0:T(128)} %bitcast.8.core, f32[512,256]{1,0:T(8,128)} %get-tuple-element.41.ma_ref.m0, f32[512,256]{1,0:T(8,128)} %collective-permute-done.3.m1, f32[512,256]{1,0:T(8,128)} %collective-permute-done.4.m2, ...), custom_call_target="tpu_custom_call" | custom-call | flops 1073741824 | bytes 8388608 | tf_op jit(solution)/shard_map/grad_w_a/pallas_call | solution.py:25
  154.1 0.0 collective-permute-start.14
  154.1 3.3 %collective-permute-start.15 = (f32[2,512,128]{2,1,0:T(8,128)}, f32[2,512,128]{2,1,0:T(8,128)}, u32[]{:S(2)}, u32[]{:S(2)}) collective-permute-start(f32[2,512,128]{2,1,0:T(8,128)} %get-tuple-element.57), channel_id=1, source_target_pairs={{0,48},{4,52},{8,56},{12,60},{16,0},{20,4},{24,8},{28,12},{32,16},... | collective-permute-start | bytes 1572872 | tf_op jit(solution)/shard_map/ppermute | solution.py:269
  157.4 0.8 copy-done.8
  158.2 10.4 %back.1 = (bf16[256,1024]{1,0:T(8,128)(2,1)}, f32[2,256,128]{2,1,0:T(8,128)}, f32[16,256]{1,0:T(8,128)}, f32[16,128]{1,0:T(8,128)}) custom-call(f32[16]{0:T(128)} %g_ref.3, bf16[1024,256]{1,0:T(8,128)(2,1)} %convolution_convert_fusion.ut_ref, bf16[1024,256]{1,0:T(8,128)(2,1)} %get-tuple-element.36.vt_ref, bf16[256,128]{1,0:T(8,128)(2,1)} %bitcast.31, ...), custom_call_target="tpu_custom_call" | custom-call | flops 1073741824 | bytes 6291456 | tf_op jit(solution)/shard_map/back/pallas_call | solution.py:25
  168.6 0.0 copy-start.15
  168.6 0.1 collective-permute-start
  168.8 5.7 %collective-permute-done.13.a1 = f32[2,512,128]{2,1,0:T(8,128)S(1)} collective-permute-done((f32[2,512,128]{2,1,0:T(8,128)}, f32[2,512,128]{2,1,0:T(8,128)S(1)}, u32[]{:S(2)}, u32[]{:S(2)}) %collective-permute-start.13) | collective-permute-done | bytes 524320 | tf_op jit(solution)/shard_map/ppermute | solution.py:269
  174.5 0.7 copy-done.12
  175.2 0.2 copy-done.13
  175.4 3.3 %gather_sum.1 = (f32[1024,128]{1,0:T(8,128)}, f32[1024,128]{1,0:T(8,128)}) custom-call(f32[2,512,128]{2,1,0:T(8,128)} %get-tuple-element.54.a0, f32[2,512,128]{2,1,0:T(8,128)} %copy-done.12, f32[2,512,128]{2,1,0:T(8,128)} %copy-done.13, f32[2,512,128]{2,1,0:T(8,128)} %collective-permute-done.15.a3, f32[2,512,128]{2,1,0:T(8,128)} %get-tuple-element.59.b0, ...), custom_call_target="tpu_custom_call" | custom-call | bytes 5242880 | tf_op jit(solution)/shard_map/gather_sum/pallas_call | solution.py:25
  178.7 3.2 %collective-permute-start.22 = (f32[1024,128]{1,0:T(8,128)}, f32[1024,128]{1,0:T(8,128)S(1)}, u32[]{:S(2)}, u32[]{:S(2)}) collective-permute-start(f32[1024,128]{1,0:T(8,128)} %get-tuple-element.64), channel_id=1, source_target_pairs={{0,64},{64,0},{1,65},{65,1},{2,66},{66,2},{3,67},{67,3},{4,68},{68... | collective-permute-start | bytes 1572872 | tf_op jit(solution)/shard_map/ppermute | solution.py:278
  181.9 0.8 collective-permute-start.1
  182.7 14.3 %all_to_all.27 = f32[16,16,128]{2,1,0:T(8,128)S(1)} all-to-all(f32[16,16,128]{2,1,0:T(8,128)S(1)} %broadcast_in_dim.22), channel_id=1, replica_groups=mesh['dp'=2,'ctx'=16,'tensor'=4] {'ctx'}, dimensions={0} | all-to-all | bytes 262144 | tf_op jit(solution)/shard_map/all_to_all | solution.py:281
  197.0 1.9 collective-permute-start.2
  198.9 3.3 %collective-permute-done.2 = f32[16,128]{1,0:T(8,128)S(1)} collective-permute-done((f32[16,128]{1,0:T(8,128)S(1)}, f32[16,128]{1,0:T(8,128)S(1)}, u32[]{:S(2)}, u32[]{:S(2)}) %collective-permute-start.2) | collective-permute-done | bytes 8224 | tf_op jit(solution)/shard_map/ppermute | solution.py:278
  202.2 0.7 slice_reduce_fusion
  202.9 0.7 fusion.2
  203.7 0.8 copy-done.7
  204.5 2.2 %finish.1 = f32[128,1024]{1,0:T(8,128)} custom-call(f32[1024,128]{1,0:T(8,128)} %get-tuple-element.63.a_ref, f32[1024,128]{1,0:T(8,128)} %copy-done.7), custom_call_target="tpu_custom_call" | custom-call | bytes 2097152 | tf_op jit(solution)/shard_map/finish/pallas_call | solution.py:25
  (51 shorter events, 0.2 us)
Async XLA Ops:
  5.5 16.2 %collective-permute-start.6 = (f32[256,512]{1,0:T(8,128)}, f32[256,512]{1,0:T(8,128)S(1)}, u32[]{:S(2)}, u32[]{:S(2)}) collective-permute-start(f32[256,512]{1,0:T(8,128)} %get-tuple-element.48), channel_id=1, source_target_pairs={{0,4},{4,8},{8,12},{12,0},{16,20},{20,24},{24,28},{28,16},{32,36},... | collective-permute-start | bytes 1572872 | tf_op jit(solution)/shard_map/ppermute | solution.py:269
  7.5 26.7 %collective-permute-start.7 = (f32[256,512]{1,0:T(8,128)}, f32[256,512]{1,0:T(8,128)S(1)}, u32[]{:S(2)}, u32[]{:S(2)}) collective-permute-start(f32[256,512]{1,0:T(8,128)} %get-tuple-element.49), channel_id=1, source_target_pairs={{0,8},{4,12},{8,0},{12,4},{16,24},{20,28},{24,16},{28,20},{32,40},... | collective-permute-start | bytes 1572872 | tf_op jit(solution)/shard_map/ppermute | solution.py:269
  11.1 24.0 %collective-permute-start.8 = (f32[256,512]{1,0:T(8,128)}, f32[256,512]{1,0:T(8,128)S(1)}, u32[]{:S(2)}, u32[]{:S(2)}) collective-permute-start(f32[256,512]{1,0:T(8,128)} %get-tuple-element.50), channel_id=1, source_target_pairs={{0,12},{4,0},{8,4},{12,8},{16,28},{20,16},{24,20},{28,24},{32,44},... | collective-permute-start | bytes 1572872 | tf_op jit(solution)/shard_map/ppermute | solution.py:269
  12.1 23.9 %collective-permute-start.9 = (f32[256,512]{1,0:T(8,128)}, f32[256,512]{1,0:T(8,128)S(1)}, u32[]{:S(2)}, u32[]{:S(2)}) collective-permute-start(f32[256,512]{1,0:T(8,128)} %get-tuple-element.51), channel_id=1, source_target_pairs={{0,16},{4,20},{8,24},{12,28},{16,32},{20,36},{24,40},{28,44},{32,4... | collective-permute-start | bytes 1572872 | tf_op jit(solution)/shard_map/ppermute | solution.py:269
  13.6 25.0 %collective-permute-start.10 = (f32[256,512]{1,0:T(8,128)}, f32[256,512]{1,0:T(8,128)S(1)}, u32[]{:S(2)}, u32[]{:S(2)}) collective-permute-start(f32[256,512]{1,0:T(8,128)} %get-tuple-element.52), channel_id=1, source_target_pairs={{0,32},{4,36},{8,40},{12,44},{16,48},{20,52},{24,56},{28,60},{32,0... | collective-permute-start | bytes 1572872 | tf_op jit(solution)/shard_map/ppermute | solution.py:269
  21.7 18.6 %copy-start = (f32[256,512]{1,0:T(8,128)}, f32[256,512]{1,0:T(8,128)S(1)}, u32[]{:S(2)}) copy-start(f32[256,512]{1,0:T(8,128)S(1)} %collective-permute-done.6.d1) | copy-start | bytes 1572868
  21.7 18.7 %copy-start.16 = (f32[16]{0:T(128)S(1)}, f32[16]{0:T(128)}, u32[]{:S(2)}) copy-start(f32[16]{0:T(128)} %param.12) | copy-start | bytes 196
  21.7 17.7 %collective-permute-start.11 = (f32[256,512]{1,0:T(8,128)}, f32[256,512]{1,0:T(8,128)S(1)}, u32[]{:S(2)}, u32[]{:S(2)}) collective-permute-start(f32[256,512]{1,0:T(8,128)} %get-tuple-element.53), channel_id=1, source_target_pairs={{0,48},{4,52},{8,56},{12,60},{16,0},{20,4},{24,8},{28,12},{32,16},... | collective-permute-start | bytes 1572872 | tf_op jit(solution)/shard_map/ppermute | solution.py:269
  34.2 6.2 %copy-start.1 = (f32[256,512]{1,0:T(8,128)}, f32[256,512]{1,0:T(8,128)S(1)}, u32[]{:S(2)}) copy-start(f32[256,512]{1,0:T(8,128)S(1)} %collective-permute-done.7.d2) | copy-start | bytes 1572868
  35.0 5.3 %copy-start.2 = (f32[256,512]{1,0:T(8,128)}, f32[256,512]{1,0:T(8,128)S(1)}, u32[]{:S(2)}) copy-start(f32[256,512]{1,0:T(8,128)S(1)} %collective-permute-done.8.d3) | copy-start | bytes 1572868
  35.9 4.5 %copy-start.3 = (f32[256,512]{1,0:T(8,128)}, f32[256,512]{1,0:T(8,128)S(1)}, u32[]{:S(2)}) copy-start(f32[256,512]{1,0:T(8,128)S(1)} %collective-permute-done.9.d1) | copy-start | bytes 1572868
  38.5 1.9 copy-start.4
  39.4 1.0 copy-start.5
  40.4 69.7 %collective-permute-start.12 = (f32[6,256,512]{2,1,0:T(8,128)}, f32[6,256,512]{2,1,0:T(8,128)S(1)}, u32[]{:S(2)}, u32[]{:S(2)}) collective-permute-start(f32[6,256,512]{2,1,0:T(8,128)} %bitcast_dynamic-update-slice_fusion), channel_id=1, source_target_pairs={{0,1},{1,0},{2,3},{3,2},{4,5},{5,4},{6,7},{7,6},{8,9},{9,8},{10,11... | collective-permute-start | bytes 9437192 | tf_op jit(solution)/shard_map/ppermute | solution.py:272
  41.1 51.3 %copy-start.6 = (bf16[1,256,4096]{2,1,0:T(8,128)(2,1)S(1)}, bf16[1,256,4096]{2,1,0:T(8,128)(2,1)}, u32[]{:S(2)}) copy-start(bf16[1,256,4096]{2,1,0:T(8,128)(2,1)} %param.15) | copy-start | bytes 6291460
  88.6 18.8 %collective-permute-start.16 = (f32[512,256]{1,0:T(8,128)}, f32[512,256]{1,0:T(8,128)}, u32[]{:S(2)}, u32[]{:S(2)}) collective-permute-start(f32[512,256]{1,0:T(8,128)} %get-tuple-element.42.mb_ref.m0), channel_id=1, source_target_pairs={{0,16},{4,20},{8,24},{12,28},{16,32},{20,36},{24,40},{28,44},{32,4... | collective-permute-start | bytes 1572872 | tf_op jit(solution)/shard_map/ppermute | solution.py:269
  88.6 30.4 %collective-permute-start.17 = (f32[512,256]{1,0:T(8,128)}, f32[512,256]{1,0:T(8,128)}, u32[]{:S(2)}, u32[]{:S(2)}) collective-permute-start(f32[512,256]{1,0:T(8,128)} %get-tuple-element.42.mb_ref.m0), channel_id=1, source_target_pairs={{0,32},{4,36},{8,40},{12,44},{16,48},{20,52},{24,56},{28,60},{32,0... | collective-permute-start | bytes 1572872 | tf_op jit(solution)/shard_map/ppermute | solution.py:269
  91.2 27.9 %collective-permute-start.18 = (f32[512,256]{1,0:T(8,128)}, f32[512,256]{1,0:T(8,128)}, u32[]{:S(2)}, u32[]{:S(2)}) collective-permute-start(f32[512,256]{1,0:T(8,128)} %get-tuple-element.42.mb_ref.m0), channel_id=1, source_target_pairs={{0,48},{4,52},{8,56},{12,60},{16,0},{20,4},{24,8},{28,12},{32,16},... | collective-permute-start | bytes 1572872 | tf_op jit(solution)/shard_map/ppermute | solution.py:269
  101.1 24.1 %all-to-all-start.2 = ((f32[16,64,128]{2,1,0:T(8,128)}), f32[16,64,128]{2,1,0:T(8,128)}, u32[]{:S(2)}, u32[]{:S(2)}) async-start(f32[16,64,128]{2,1,0:T(8,128)} %grad_ends.1), calls=%async_computation.2 | async-start | bytes 1048576 | tf_op jit(solution)/shard_map/all_to_all | solution.py:281
  105.5 28.8 %collective-permute-start.3 = (f32[512,256]{1,0:T(8,128)}, f32[512,256]{1,0:T(8,128)}, u32[]{:S(2)}, u32[]{:S(2)}) collective-permute-start(f32[512,256]{1,0:T(8,128)} %get-tuple-element.41.ma_ref.m0), channel_id=1, source_target_pairs={{0,4},{4,8},{8,12},{12,0},{16,20},{20,24},{24,28},{28,16},{32,36},... | collective-permute-start | bytes 1572872 | tf_op jit(solution)/shard_map/ppermute | solution.py:269
  107.4 35.7 %collective-permute-start.4 = (f32[512,256]{1,0:T(8,128)}, f32[512,256]{1,0:T(8,128)}, u32[]{:S(2)}, u32[]{:S(2)}) collective-permute-start(f32[512,256]{1,0:T(8,128)} %get-tuple-element.41.ma_ref.m0), channel_id=1, source_target_pairs={{0,8},{4,12},{8,0},{12,4},{16,24},{20,28},{24,16},{28,20},{32,40},... | collective-permute-start | bytes 1572872 | tf_op jit(solution)/shard_map/ppermute | solution.py:269
  110.1 38.7 %collective-permute-start.5 = (f32[512,256]{1,0:T(8,128)}, f32[512,256]{1,0:T(8,128)}, u32[]{:S(2)}, u32[]{:S(2)}) collective-permute-start(f32[512,256]{1,0:T(8,128)} %get-tuple-element.41.ma_ref.m0), channel_id=1, source_target_pairs={{0,12},{4,0},{8,4},{12,8},{16,28},{20,16},{24,20},{28,24},{32,44},... | collective-permute-start | bytes 1572872 | tf_op jit(solution)/shard_map/ppermute | solution.py:269
  124.4 29.7 %collective-permute-start.19 = (f32[2,512,128]{2,1,0:T(8,128)}, f32[2,512,128]{2,1,0:T(8,128)S(1)}, u32[]{:S(2)}, u32[]{:S(2)}) collective-permute-start(f32[2,512,128]{2,1,0:T(8,128)} %get-tuple-element.60), channel_id=1, source_target_pairs={{0,4},{4,8},{8,12},{12,0},{16,20},{20,24},{24,28},{28,16},{32,36},... | collective-permute-start | bytes 1572872 | tf_op jit(solution)/shard_map/ppermute | solution.py:269
  127.1 30.3 %all-to-all-start.3 = ((f32[16,64,128]{2,1,0:T(8,128)}), f32[16,64,128]{2,1,0:T(8,128)S(1)}, u32[]{:S(2)}, u32[]{:S(2)}) async-start(f32[16,64,128]{2,1,0:T(8,128)} %after.1), calls=%async_computation.3 | async-start | bytes 1048576 | tf_op jit(solution)/shard_map/all_to_all | solution.py:281
  130.9 37.8 %collective-permute-start.20 = (f32[2,512,128]{2,1,0:T(8,128)}, f32[2,512,128]{2,1,0:T(8,128)S(1)}, u32[]{:S(2)}, u32[]{:S(2)}) collective-permute-start(f32[2,512,128]{2,1,0:T(8,128)} %get-tuple-element.61), channel_id=1, source_target_pairs={{0,8},{4,12},{8,0},{12,4},{16,24},{20,28},{24,16},{28,20},{32,40},... | collective-permute-start | bytes 1572872 | tf_op jit(solution)/shard_map/ppermute | solution.py:269
  134.3 34.4 %collective-permute-start.21 = (f32[2,512,128]{2,1,0:T(8,128)}, f32[2,512,128]{2,1,0:T(8,128)S(1)}, u32[]{:S(2)}, u32[]{:S(2)}) collective-permute-start(f32[2,512,128]{2,1,0:T(8,128)} %get-tuple-element.62), channel_id=1, source_target_pairs={{0,12},{4,0},{8,4},{12,8},{16,28},{20,16},{24,20},{28,24},{32,44},... | collective-permute-start | bytes 1572872 | tf_op jit(solution)/shard_map/ppermute | solution.py:269
  154.1 20.3 %collective-permute-start.13 = (f32[2,512,128]{2,1,0:T(8,128)}, f32[2,512,128]{2,1,0:T(8,128)S(1)}, u32[]{:S(2)}, u32[]{:S(2)}) collective-permute-start(f32[2,512,128]{2,1,0:T(8,128)} %get-tuple-element.55), channel_id=1, source_target_pairs={{0,16},{4,20},{8,24},{12,28},{16,32},{20,36},{24,40},{28,44},{32,4... | collective-permute-start | bytes 1572872 | tf_op jit(solution)/shard_map/ppermute | solution.py:269
  154.1 20.3 %collective-permute-start.14 = (f32[2,512,128]{2,1,0:T(8,128)}, f32[2,512,128]{2,1,0:T(8,128)S(1)}, u32[]{:S(2)}, u32[]{:S(2)}) collective-permute-start(f32[2,512,128]{2,1,0:T(8,128)} %get-tuple-element.56), channel_id=1, source_target_pairs={{0,32},{4,36},{8,40},{12,44},{16,48},{20,52},{24,56},{28,60},{32,0... | collective-permute-start | bytes 1572872 | tf_op jit(solution)/shard_map/ppermute | solution.py:269
  154.1 20.3 %copy-start.9 = (f32[2,512,128]{2,1,0:T(8,128)}, f32[2,512,128]{2,1,0:T(8,128)S(1)}, u32[]{:S(2)}) copy-start(f32[2,512,128]{2,1,0:T(8,128)S(1)} %collective-permute-done.19.b1) | copy-start | bytes 1572868
  154.1 20.3 %collective-permute-start.15 = (f32[2,512,128]{2,1,0:T(8,128)}, f32[2,512,128]{2,1,0:T(8,128)}, u32[]{:S(2)}, u32[]{:S(2)}) collective-permute-start(f32[2,512,128]{2,1,0:T(8,128)} %get-tuple-element.57), channel_id=1, source_target_pairs={{0,48},{4,52},{8,56},{12,60},{16,0},{20,4},{24,8},{28,12},{32,16},... | collective-permute-start | bytes 1572872 | tf_op jit(solution)/shard_map/ppermute | solution.py:269
  157.4 0.8 copy-start.8
  168.6 13.3 %copy-start.14 = (f32[2,256,128]{2,1,0:T(8,128)S(1)}, f32[2,256,128]{2,1,0:T(8,128)}, u32[]{:S(2)}) copy-start(f32[2,256,128]{2,1,0:T(8,128)} %get-tuple-element.44) | copy-start | bytes 786436
  168.6 14.1 %copy-start.15 = (f32[16,128]{1,0:T(8,128)S(1)}, f32[16,128]{1,0:T(8,128)}, u32[]{:S(2)}) copy-start(f32[16,128]{1,0:T(8,128)} %get-tuple-element.46) | copy-start | bytes 24580
  168.6 5.8 %copy-start.10 = (f32[2,512,128]{2,1,0:T(8,128)}, f32[2,512,128]{2,1,0:T(8,128)S(1)}, u32[]{:S(2)}) copy-start(f32[2,512,128]{2,1,0:T(8,128)S(1)} %collective-permute-done.20.b2) | copy-start | bytes 1572868
  168.6 13.2 %collective-permute-start = (f32[2,256,128]{2,1,0:T(8,128)}, f32[2,256,128]{2,1,0:T(8,128)S(1)}, u32[]{:S(2)}, u32[]{:S(2)}) collective-permute-start(f32[2,256,128]{2,1,0:T(8,128)} %get-tuple-element.44), channel_id=1, source_target_pairs={{0,1},{1,0},{2,3},{3,2},{4,5},{5,4},{6,7},{7,6},{8,9},{9,8},{10,11... | collective-permute-start | bytes 786440 | tf_op jit(solution)/shard_map/ppermute | solution.py:272
  168.7 5.7 %copy-start.11 = (f32[2,512,128]{2,1,0:T(8,128)}, f32[2,512,128]{2,1,0:T(8,128)S(1)}, u32[]{:S(2)}) copy-start(f32[2,512,128]{2,1,0:T(8,128)S(1)} %collective-permute-done.21.b3) | copy-start | bytes 1572868
  174.4 0.8 copy-start.12
  174.4 1.0 copy-start.13
  178.7 25.0 %collective-permute-start.22 = (f32[1024,128]{1,0:T(8,128)}, f32[1024,128]{1,0:T(8,128)S(1)}, u32[]{:S(2)}, u32[]{:S(2)}) collective-permute-start(f32[1024,128]{1,0:T(8,128)} %get-tuple-element.64), channel_id=1, source_target_pairs={{0,64},{64,0},{1,65},{65,1},{2,66},{66,2},{3,67},{67,3},{4,68},{68... | collective-permute-start | bytes 1572872 | tf_op jit(solution)/shard_map/ppermute | solution.py:278
  181.9 21.0 %collective-permute-start.1 = (f32[2,256,128]{2,1,0:T(8,128)S(1)}, f32[2,256,128]{2,1,0:T(8,128)S(1)}, u32[]{:S(2)}, u32[]{:S(2)}) collective-permute-start(f32[2,256,128]{2,1,0:T(8,128)S(1)} %add.10), channel_id=1, source_target_pairs={{0,2},{2,0},{1,3},{3,1},{4,6},{6,4},{5,7},{7,5},{8,10},{10,8},{9,1... | collective-permute-start | bytes 786440 | tf_op jit(solution)/shard_map/ppermute | solution.py:275
  197.0 5.2 %collective-permute-start.2 = (f32[16,128]{1,0:T(8,128)S(1)}, f32[16,128]{1,0:T(8,128)S(1)}, u32[]{:S(2)}, u32[]{:S(2)}) collective-permute-start(f32[16,128]{1,0:T(8,128)S(1)} %reduce_sum.9), channel_id=1, source_target_pairs={{0,64},{64,0},{1,65},{65,1},{2,66},{66,2},{3,67},{67,3},{4,68},{68... | collective-permute-start | bytes 24584 | tf_op jit(solution)/shard_map/ppermute | solution.py:278
  203.6 0.8 copy-start.7

commit v2 on v1

--- a/solution.py
+++ b/solution.py
@@ -70,43 +70,43 @@
             ox[kd, :, cols] = column(d, x, z + r)
 
 
-def ends_kernel(v_ref, b_ref, s_ref, r_ref, vt_ref, end_ref, run_ref, *, length):
+def ends_kernel(ut_ref, v_ref, b_ref, c_ref, s_ref, r_ref, vt_ref, end_ref, run_ref, *, length):
     heads, tokens = s_ref.shape
     width = v_ref.shape[1] // heads
     run = scan_lanes(s_ref[...] * (r_ref[...] * (-1.0 / length)))
     run_ref[...] = run
     last = run[:, tokens - 1 :]
+    grow = jnp.exp(run)
     tail = jnp.exp(last - run) * s_ref[...]
     total = jnp.exp(last)
     b = b_ref[...]
+    c = c_ref[...]
     per = 128 // width
     for h in range(0, heads, per):
         vt = v_ref[:, h * width : (h + per) * width].astype(F32).T
         vt_ref[h * width : (h + per) * width, :] = vt.astype(BF16)
         for k in range(per):
-            scaled = vt[k * width : (k + 1) * width] * tail[h + k : h + k + 1]
-            end_ref[h + k, :width, :] = dot(scaled.astype(BF16), b)
-            end_ref[h + k, width:, :] = jnp.broadcast_to(total[h + k : h + k + 1], (8, 128))
-
-
-def before_kernel(e_ref, o_ref, keep_ref):
+            at = h + k
+            scaled = vt[k * width : (k + 1) * width] * tail[at : at + 1]
+            end_ref[at, :width, :] = dot(scaled.astype(BF16), b)
+            scaled = ut_ref[at * width : (at + 1) * width, :].astype(F32) * grow[at : at + 1]
+            end_ref[at, width : 2 * width, :] = dot(scaled.astype(BF16), c)
+            end_ref[at, 2 * width :, :] = jnp.broadcast_to(total[at : at + 1], (8, 128))
+
+
+def across_kernel(e_ref, o_ref):
     shards, rows, _ = o_ref.shape
-    state = jnp.zeros(o_ref.shape[1:], F32)
+    width = rows // 2
+    state = jnp.zeros((width, o_ref.shape[2]), F32)
     for k in range(shards):
-        o_ref[k] = state
-        decay = e_ref[k, rows:, :]
-        keep_ref[k] = decay
+        o_ref[k, :width, :] = state
         if k < shards - 1:
-            state = state * decay[0:1] + e_ref[k, :rows, :]
-
-
-def after_kernel(e_ref, keep_ref, o_ref):
-    shards = o_ref.shape[0]
-    state = jnp.zeros(o_ref.shape[1:], F32)
+            state = state * e_ref[k, rows : rows + 1, :] + e_ref[k, :width, :]
+    state = jnp.zeros((width, o_ref.shape[2]), F32)
     for k in reversed(range(shards)):
-        o_ref[k] = state
+        o_ref[k, width:, :] = state
         if k:
-            state = state * keep_ref[k, 0:1] + e_ref[k]
+            state = state * e_ref[k, rows : rows + 1, :] + e_ref[k, width:rows, :]
 
 
 def columns_of(run, wide_ref):
@@ -123,7 +123,7 @@
     return jnp.exp(jnp.where(i >= j, between, NEG)) * steps
 
 
-def mix_kernel(g_ref, vt_ref, b_ref, c_ref, s_ref, run_ref, sin_ref, ma_ref, mb_ref, wide_ref, g2_ref):
+def mix_kernel(g_ref, vt_ref, b_ref, c_ref, s_ref, run_ref, st_ref, ma_ref, mb_ref, wide_ref, g2_ref):
     heads, tokens = s_ref.shape
     width = vt_ref.shape[0] // heads
     columns_of(run_ref[...], wide_ref)
@@ -136,7 +136,7 @@
         at = pl.ds(pl.multiple_of(h * width, width), width)
         v = vt_ref[at, :]
         inside = dot(v, mix, 1, 1)
-        carried = dot(sin_ref[h].astype(BF16), c_ref[...], 1, 1) * jnp.exp(row)
+        carried = dot(st_ref[h, :width, :].astype(BF16), c_ref[...], 1, 1) * jnp.exp(row)
         to = pl.ds(pl.multiple_of((h - base) * width, width), width)
         out_ref[to, :] = inside + carried + g_ref[h] * v.astype(F32)
 
@@ -144,17 +144,8 @@
     lax.fori_loop(half, heads, lambda h, _: head(h, mb_ref, half), None, unroll=2)
 
 
-def grad_ends_kernel(ut_ref, c_ref, run_ref, o_ref):
-    heads, width, _ = o_ref.shape
-    grow = jnp.exp(run_ref[...])
-    c = c_ref[...]
-    for h in range(heads):
-        scaled = ut_ref[h * width : (h + 1) * width, :].astype(F32) * grow[h : h + 1]
-        o_ref[h] = dot(scaled.astype(BF16), c)
-
-
 def back_kernel(
-    g_ref, ut_ref, vt_ref, b_ref, c_ref, s_ref, run_ref, r_ref, sin_ref, gs_ref, ma_ref, mb_ref,
+    g_ref, ut_ref, vt_ref, b_ref, c_ref, s_ref, run_ref, r_ref, st_ref, ma_ref, mb_ref,
     dv_ref, dbc_ref, ds_ref, small_ref,
     wide_ref, g2_ref, ct_ref, bt_ref, ue_ref, vw_ref, r1_ref, q_ref, add_ref, skip_ref, dbt_ref, dct_ref, dvt_ref,
     *, length,
@@ -185,7 +176,7 @@
         tail = jnp.exp(last - row) * steps
         ue_ref[at, :] = (uf * jnp.exp(row)).astype(BF16)
         vw_ref[at, :] = (vf * tail).astype(BF16)
-        gs = gs_ref[h]
+        gs = st_ref[h, width:, :]
         far = dot(gs.astype(BF16), bt_ref[...]) * tail
         near = dot(u, mix)
         both = near + far
@@ -194,7 +185,7 @@
         out = mixed_ref[pl.ds(pl.multiple_of((h - base) * width, width), width), :] - gain * vf
         r1_ref[pl.ds(h, 1), :] = jnp.sum(uf * out, 0, keepdims=True)
         q_ref[pl.ds(h, 1), :] = jnp.sum(vf * both, 0, keepdims=True)
-        kept = jnp.sum(sin_ref[h] * gs, 0, keepdims=True) * jnp.exp(last)
+        kept = jnp.sum(st_ref[h, :width, :] * gs, 0, keepdims=True) * jnp.exp(last)
         add_ref[pl.ds(h, 1), :] = jnp.sum(vf * far, 0, keepdims=True) + jnp.concatenate(
             [kept, jnp.zeros((1, tokens - 128), F32)], 1
         )
@@ -203,9 +194,9 @@
     lax.fori_loop(0, half, lambda h, _: head(h, ma_ref, 0), None, unroll=2)
     lax.fori_loop(half, heads, lambda h, _: head(h, mb_ref, half), None, unroll=2)
 
-    states = sin_ref.shape[0] * sin_ref.shape[1]
-    sin_t = sin_ref[...].reshape(states, 128).T.astype(BF16)
-    gs_t = gs_ref[...].reshape(states, 128).T.astype(BF16)
+    states = heads * width
+    sin_t = st_ref[:, :width, :].reshape(states, 128).T.astype(BF16)
+    gs_t = st_ref[:, width:, :].reshape(states, 128).T.astype(BF16)
     dbc_ref[0] = (dbt_ref[...] + dot(gs_t, vw_ref[...])).T
     dbc_ref[1] = (dct_ref[...] + dot(sin_t, ue_ref[...])).T
     for k in range(0, heads * width, 128):
@@ -216,33 +207,34 @@
     rates = jnp.sum(s * dlog, 1, keepdims=True) * (-1.0 / length)
     skips = jnp.sum(skip_ref[...], 1, keepdims=True)
     lane = lax.broadcasted_iota(jnp.int32, (heads, 128), 1)
-    small_ref[...] = jnp.where(lane == 0, rates, jnp.where(lane == 1, skips, 0.0))
-
-
-def grad_w_kernel(core, m0, m1, m2, m3, own, d1, d2, d3, e_ref, o0, o1, o2, o3):
+    head_of = lax.broadcasted_iota(jnp.int32, (heads, 128), 0)
+    packed = jnp.where(lane == head_of, rates, jnp.where(lane == head_of + heads, skips, 0.0))
+    small_ref[...] = jnp.sum(packed, 0, keepdims=True)
+
+
+def grad_w_kernel(core, m0, m1, m2, m3, own, d1, d2, d3, e1, e2, e3, o0, o1, o2, o3):
     outs = (o0, o1, o2, o3)
     ms = [m[...].astype(BF16) for m in (m0, m1, m2, m3)]
-    ds = (d1, d2, d3)
+    ds = ((d1, d2, d3), (e1, e2, e3))
     me = core[0]
     for kd in range(2):
         at = me if kd == 0 else 1 - me
         acc = dot(ms[0], own[at])
         for k in range(3):
-            piece = ds[k][...] if kd == 0 else e_ref[k]
-            acc += dot(ms[k + 1], piece.astype(BF16))
+            acc += dot(ms[k + 1], ds[kd][k][...].astype(BF16))
         for r in range(SIDE):
             outs[r][at] = acc[:, r * 128 : (r + 1) * 128]
 
 
-def gather_sum_kernel(a0, a1, a2, a3, b0, b1, b2, b3, keep_ref, send_ref):
-    n = a0.shape[1]
-    for at, (w, x, y, z) in ((0, (a0, a1, a2, a3)), (n, (b0, b1, b2, b3))):
-        keep_ref[at : at + n, :] = w[0] + x[0] + y[0] + z[0]
-        send_ref[at : at + n, :] = w[1] + x[1] + y[1] + z[1]
-
-
-def finish_kernel(a_ref, b_ref, o_ref):
-    o_ref[...] = (a_ref[...] + b_ref[...]).T
+def gather_sum_kernel(a0, a1, a2, a3, keep_ref, send_ref):
+    keep_ref[...] = a0[0] + a1[0] + a2[0] + a3[0]
+    send_ref[...] = a0[1] + a1[1] + a2[1] + a3[1]
+
+
+def finish_kernel(a0, a1, b0, b1, o_ref):
+    n = a0.shape[0]
+    o_ref[:, :n] = (a0[...] + a1[...]).T
+    o_ref[:, n:] = (b0[...] + b1[...]).T
 
 
 def body(values, b_proj, c_proj, step_sizes, decay_rates, skip_gain, w_out, d_out):
@@ -283,53 +275,41 @@
     v, b, c, steps, cot = values[0], b_proj[0], c_proj[0], step_sizes[0], d_out[0]
     rates = decay_rates[:, None]
 
+    def later(value, *first):
+        return lax.optimization_barrier((value,) + first)[0]
+
     piece = sds((tokens, 4 * 128), F32)
     own = sds((2, tokens, 4 * 128), BF16)
     z1, z2, z3, x1, x2, x3, own_z, own_x = call(
         prep_kernel, (piece,) * 6 + (own, own), "prep", scalars=1, nbytes=7 << 20
     )(pos, cot)
+    z3, x3, z1, x1 = shift(z3, 0, 3), shift(x3, 3, 0), shift(z1, 0, 1), shift(x1, 1, 0)
+
+    up_t = lax.dot_general(w_out, later(cot, own_z), (((0,), (1,)), ((), ())), preferred_element_type=F32).astype(BF16)
     vt, ends, run = call(
         functools.partial(ends_kernel, length=length),
-        (sds((channels, tokens), BF16), sds((heads, width + 8, state), F32), sds((heads, tokens), F32)),
+        (sds((channels, tokens), BF16), sds((heads, 2 * width + 8, state), F32), sds((heads, tokens), F32)),
         "ends",
-        nbytes=2 << 20,
-        flops=1 << 26,
-    )(v, b, steps, rates)
-    z1, z2, z3 = shift(z1, 0, 1), shift(z2, 0, 2), shift(z3, 0, 3)
-    x1, x2, x3 = shift(x1, 1, 0), shift(x2, 2, 0), shift(x3, 3, 0)
-
-    before, keep = call(
-        before_kernel, (sds((shards, width, state), F32), sds((shards, 8, state), F32)), "before", nbytes=1 << 20
-    )(spread(ends))
-    state_in = spread(before)
+        nbytes=4 << 20,
+        flops=1 << 27,
+    )(up_t, v, b, c, steps, rates)
+    z2, x2 = shift(later(z2, run), 0, 2), shift(later(x2, run), 2, 0)
+    ends = later(ends, z1, z3, x1, x3)
+    across = call(across_kernel, sds((shards, 2 * width, state), F32), "across", nbytes=2 << 20)(spread(ends))
+    states = spread(across)
+    sent = [z1, z2, z3, x1, x2, x3]
 
     wide = pltpu.VMEM((heads, tokens, 128), F32)
     square = pltpu.VMEM((tokens, tokens), F32)
     mixed_a, mixed_b = call(
         mix_kernel, (sds((half, tokens), F32),) * 2, "mix", (wide, square), scalars=1, nbytes=4 << 20, flops=1 << 28
-    )(skip_gain, vt, b, c, steps, run, state_in)
-
-    a1, a2, a3 = shift(mixed_a, 0, 1), shift(mixed_a, 0, 2), shift(mixed_a, 0, 3)
-    b1, b2, b3 = shift(mixed_b, 1, 0), shift(mixed_b, 2, 0), shift(mixed_b, 3, 0)
-
-    swapped = other_core(jnp.stack([z1, z2, z3, x1, x2, x3]))
-    up_t = lax.dot_general(w_out, cot, (((0,), (1,)), ((), ())), preferred_element_type=F32).astype(BF16)
-    grad_ends = call(grad_ends_kernel, sds((heads, width, state), F32), "grad_ends", nbytes=2 << 20, flops=1 << 26)(
-        up_t, c, run
-    )
-    after = call(after_kernel, sds((shards, width, state), F32), "after", nbytes=1 << 20)(spread(grad_ends), keep)
-    grad_out = spread(after)
-
-    out = (sds((2, half, 128), F32),) * 4
-    flops = 2 * half * 4 * tokens * 1024
-    pa = call(grad_w_kernel, out, "grad_w_a", scalars=1, flops=flops, nbytes=8 << 20)(
-        core[None].astype(jnp.int32), mixed_a, a1, a2, a3, own_z, z1, z2, z3, swapped[:3]
-    )
-    pb = call(grad_w_kernel, out, "grad_w_b", scalars=1, flops=flops, nbytes=8 << 20)(
-        core[None].astype(jnp.int32), mixed_b, b1, b2, b3, own_x, x1, x2, x3, swapped[3:]
-    )
-    ra = [pa[0]] + [shift(pa[k], k, 0) for k in range(1, SIDE)]
-    rb = [pb[0]] + [shift(pb[k], 0, k) for k in range(1, SIDE)]
+    )(skip_gain, vt, b, c, steps, run, states)
+
+    swapped = [other_core(p) for p in lax.optimization_barrier((*sent, across))[:6]]
+    ready = lax.optimization_barrier((mixed_a, mixed_b, *swapped))
+    mixed_a, mixed_b, swapped = ready[0], ready[1], ready[2:]
+    b1, b3 = shift(mixed_b, 1, 0), shift(mixed_b, 3, 0)
+    a1, a3, a2 = shift(mixed_a, 0, 1), shift(mixed_a, 0, 3), shift(mixed_a, 0, 2)
 
     dv, dbc, dsteps, small = call(
         functools.partial(back_kernel, length=length),
@@ -337,7 +317,7 @@
             sds((tokens, channels), BF16),
             sds((2, tokens, state), F32),
             sds((heads, tokens), F32),
-            sds((heads, 128), F32),
+            sds((1, 128), F32),
         ),
         "back",
         (
@@ -351,16 +331,34 @@
         scalars=1,
         flops=1 << 30,
         nbytes=6 << 20,
-    )(skip_gain, up_t, vt, b, c, steps, run, rates, state_in, grad_out, mixed_a, mixed_b)
+    )(skip_gain, up_t, vt, b, c, steps, run, rates, states, mixed_a, mixed_b)
+
+    b2 = shift(later(mixed_b, b1, b3, small), 2, 0)
+    small = spread(jnp.broadcast_to(small[None], (shards,) + small.shape)).sum(0)
+
+    out = (sds((2, half, 128), F32),) * 4
+    flops = 2 * half * 4 * tokens * 1024
+    me = core[None].astype(jnp.int32)
+    pa = call(grad_w_kernel, out, "grad_w_a", scalars=1, flops=flops, nbytes=8 << 20)(
+        me, later(mixed_a, small), a1, a2, a3, own_z, *sent[:3], *swapped[:3]
+    )
+    ra = [pa[0]] + [shift(pa[k], k, 0) for k in range(1, SIDE)]
+    pb = call(grad_w_kernel, out, "grad_w_b", scalars=1, flops=flops, nbytes=8 << 20)(
+        me, later(mixed_b, pa[0]), b1, b2, b3, own_x, *sent[3:], *swapped[3:]
+    )
+    rb = [pb[0]] + [shift(pb[k], 0, k) for k in range(1, SIDE)]
 
     dbc = dbc + other_core(dbc)
     dbc = dbc + other_chip(dbc)
-    small = spread(jnp.broadcast_to(small[None], (shards,) + small.shape)).sum(0)
     small = small + other_dp(small)
 
-    kept, sent = call(gather_sum_kernel, (sds((channels, 128), F32),) * 2, "gather_sum", nbytes=5 << 20)(*ra, *rb)
-    d_w = call(finish_kernel, sds((128, channels), F32), "finish", nbytes=2 << 20)(kept, other_dp(sent))
-    return (dv[None], dbc[0][None], dbc[1][None], dsteps[None], small[:, 0], small[:, 1], d_w)
+    pair = (sds((half, 128), F32),) * 2
+    kept_a, away_a = call(gather_sum_kernel, pair, "gather_sum_a", nbytes=3 << 20)(*ra)
+    away_a = other_dp(away_a)
+    kept_b, away_b = call(gather_sum_kernel, pair, "gather_sum_b", nbytes=3 << 20)(*rb)
+    away_b = other_dp(away_b)
+    d_w = call(finish_kernel, sds((128, channels), F32), "finish", nbytes=2 << 20)(kept_a, away_a, kept_b, away_b)
+    return (dv[None], dbc[0][None], dbc[1][None], dsteps[None], small[0, :heads], small[0, heads : 2 * heads], d_w)
 
 
 def solution(mesh):

time: 207 us -> 179 us (0.86)
  blocking collectives: 51.8 us -> 0 us
  waiting for transfers between devices: 38.3 us -> 59.4 us
  starting transfers between devices: 51.6 us -> 58.3 us
  local copies, waits for them, and re-layouts: 12.1 us -> 8.65 us
    all_to_all x3 -> x0, blocking collectives: 51.8 us -> none  [spread(): return lax.all_to_all(value, 'ctx', 0, 0, tiled=True)]
    all_to_all x2 -> x3, waiting for transfers between devices: 0.01 us -> 33.6 us  [spread(): return lax.all_to_all(value, 'ctx', 0, 0, tiled=True)]
    ppermute x18, waiting for transfers between devices: 35 us -> 18.6 us  [shift(): return lax.ppermute(value, 'ctx', pairs)]
    all_to_all x2 -> x3, starting transfers between devices: 8.15 us -> 18.2 us  [spread(): return lax.all_to_all(value, 'ctx', 0, 0, tiled=True)]
    ppermute x18, starting transfers between devices: 37.5 us -> 30.5 us  [shift(): return lax.ppermute(value, 'ctx', pairs)]
    ppermute x2 -> x3, waiting for transfers between devices: 3.32 us -> 7.3 us  [other_dp(): return lax.ppermute(value, 'dp', [(0, 1), (1, 0)])]
    slice x2 -> x0, local copies, waits for them, and re-layouts: 2.76 us -> none  [the longest x1 2.06 us: body(): swapped[3:]]
    ppermute x2 -> x3, starting transfers between devices: 5.11 us -> 6.75 us  [other_dp(): return lax.ppermute(value, 'dp', [(0, 1), (1, 0)])]
  transfers between devices with their start and end apart: 25 -> 32, of which waited for: 7 -> 9; matrix products, arithmetic and copies ran while one was open for 7% -> 6% of each run, Pallas kernels for 19% -> 21%
where the time goes in v2:
time: 179 us
  waiting for transfers between devices  59.4 us (33%)
  starting transfers between devices  58.3 us (33%)
  Pallas kernels  43.1 us (24%)
  local copies, waits for them, and re-layouts  8.65 us (5%)
  matrix products  7.53 us (4%)
    pallas_call x10, Pallas kernels, run(): pl.pallas_call(kernel, out_shape=outs, in_specs=specs, out_specs=jax.tree...  43.1 us
    all_to_all x3, waiting for transfers between devices, spread(): return lax.all_to_all(value, 'ctx', 0, 0, tiled=True)  33.6 us
    ppermute x18, starting transfers between devices, shift(): return lax.ppermute(value, 'ctx', pairs)  30.5 us
    ppermute x18, waiting for transfers between devices, shift(): return lax.ppermute(value, 'ctx', pairs)  18.6 us
    all_to_all x3, starting transfers between devices, spread(): return lax.all_to_all(value, 'ctx', 0, 0, tiled=True)  18.2 us
    dot_general x1, matrix products, body(): lax.dot_general(w_out, later(cot, own_z), (((0,), (1,)), ((), ())), prefe...  7.53 us
    ppermute x3, waiting for transfers between devices, other_dp(): return lax.ppermute(value, 'dp', [(0, 1), (1, 0)])  7.3 us
    ppermute x3, starting transfers between devices, other_dp(): return lax.ppermute(value, 'dp', [(0, 1), (1, 0)])  6.75 us
  transfers between devices with their start and end apart: 32, of which 9 were waited for; matrix products, arithmetic and copies ran while one was open for 6% of the time, Pallas kernels for 21%

profile of v2, /device:TPU:0, one launch (start us, length us, event | category | flops | bytes accessed | tf_op | source)
XLA Modules:
  0.0 178.6 jit_solution(17084828671478649501)
XLA Ops:
  0.6 0.0 copy-start.2
  0.7 0.6 pad_add_fusion.pos
  1.3 4.3 %prep.1 = (f32[256,512]{1,0:T(8,128)}, f32[256,512]{1,0:T(8,128)}, f32[256,512]{1,0:T(8,128)}, f32[256,512]{1,0:T(8,128)}, f32[256,512]{1,0:T(8,128)}, /*index=5...) custom-call(s32[4]{0:T(128)} %pad_add_fusion.pos, bf16[256,4096]{1,0:T(8,128)(2,1)} %bitcast.24), custom_call_target="tpu_custom_call" | custom-call | bytes 7340032 | tf_op jit(solution)/shard_map/prep/pallas_call | solution.py:25
  5.5 2.0 %collective-permute-start = (f32[256,512]{1,0:T(8,128)}, f32[256,512]{1,0:T(8,128)}, u32[]{:S(2)}, u32[]{:S(2)}) collective-permute-start(f32[256,512]{1,0:T(8,128)} %get-tuple-element.62), channel_id=1, source_target_pairs={{0,4},{4,8},{8,12},{12,0},{16,20},{20,24},{24,28},{28,16},{32,36},... | collective-permute-start | bytes 1572872 | tf_op jit(solution)/shard_map/ppermute | solution.py:261
  7.5 2.1 %collective-permute-start.1 = (f32[256,512]{1,0:T(8,128)}, f32[256,512]{1,0:T(8,128)}, u32[]{:S(2)}, u32[]{:S(2)}) collective-permute-start(f32[256,512]{1,0:T(8,128)} %get-tuple-element.63), channel_id=1, source_target_pairs={{0,12},{4,0},{8,4},{12,8},{16,28},{20,16},{24,20},{28,24},{32,44},... | collective-permute-start | bytes 1572872 | tf_op jit(solution)/shard_map/ppermute | solution.py:261
  9.7 1.5 collective-permute-start.2
  11.1 1.8 collective-permute-start.3
  12.9 0.7 copy.22.r_ref
  13.6 7.5 %fusion.ut_ref = bf16[1024,256]{1,0:T(8,128)(2,1)} fusion(bf16[256,4096]{1,0:T(8,128)(2,1)S(1)} %bitcast.25, bf16[4096,1024]{1,0:T(8,128)(2,1)} %param.14), kind=kOutput, calls=%fused_computation.1 | convolution fusion | flops 2147745792 | bytes 11010048 | tf_op jit(solution)/shard_map/dot_general | solution.py:288
  21.1 3.6 %ends.1 = (bf16[1024,256]{1,0:T(8,128)(2,1)}, f32[16,136,128]{2,1,0:T(8,128)}, f32[16,256]{1,0:T(8,128)}) custom-call(bf16[1024,256]{1,0:T(8,128)(2,1)} %fusion.ut_ref, bf16[256,1024]{1,0:T(8,128)(2,1)} %bitcast.26, bf16[256,128]{1,0:T(8,128)(2,1)} %bitcast.27, bf16[256,128]{1,0:T(8,128)(2,1)} %bitcast.30, f32[16,256]{1,0:T(8,128)} %bitcast.33, ...), custom_call_target="tpu_custom_call" | custom-call | flops 134217728 | bytes 4194304 | tf_op jit(solution)/shard_map/ends/pallas_call | solution.py:25
  24.7 5.3 %all-to-all-start = ((f32[16,136,128]{2,1,0:T(8,128)}), f32[16,136,128]{2,1,0:T(8,128)S(1)}, u32[]{:S(2)}, u32[]{:S(2)}) async-start(f32[16,136,128]{2,1,0:T(8,128)} %get-tuple-element.66), calls=%async_computation | async-start | bytes 2228224 | tf_op jit(solution)/shard_map/all_to_all | solution.py:273
  30.0 3.4 %collective-permute-start.4 = (f32[256,512]{1,0:T(8,128)}, f32[256,512]{1,0:T(8,128)}, u32[]{:S(2)}, u32[]{:S(2)}) collective-permute-start(f32[256,512]{1,0:T(8,128)} %get-tuple-element.70), channel_id=1, source_target_pairs={{0,8},{4,12},{8,0},{12,4},{16,24},{20,28},{24,16},{28,20},{32,40},... | collective-permute-start | bytes 1572872 | tf_op jit(solution)/shard_map/ppermute | solution.py:261
  33.4 3.0 %collective-permute-start.5 = (f32[256,512]{1,0:T(8,128)}, f32[256,512]{1,0:T(8,128)S(1)}, u32[]{:S(2)}, u32[]{:S(2)}) collective-permute-start(f32[256,512]{1,0:T(8,128)} %get-tuple-element.72), channel_id=1, source_target_pairs={{0,32},{4,36},{8,40},{12,44},{16,48},{20,52},{24,56},{28,60},{32,0... | collective-permute-start | bytes 1572872 | tf_op jit(solution)/shard_map/ppermute | solution.py:261
  36.4 12.4 %all-to-all-done.e_ref = f32[16,136,128]{2,1,0:T(8,128)S(1)} async-done(((f32[16,136,128]{2,1,0:T(8,128)}), f32[16,136,128]{2,1,0:T(8,128)S(1)}, u32[]{:S(2)}, u32[]{:S(2)}) %all-to-all-start) | async-done | bytes 1114144 | tf_op jit(solution)/shard_map/all_to_all | solution.py:273
  48.8 1.0 copy-done
  49.8 2.4 %across.1 = f32[16,128,128]{2,1,0:T(8,128)} custom-call(f32[16,136,128]{2,1,0:T(8,128)} %copy-done), custom_call_target="tpu_custom_call" | custom-call | bytes 2097152 | tf_op jit(solution)/shard_map/across/pallas_call | solution.py:25
  52.2 4.4 %collective-permute-done.4.d2 = f32[256,512]{1,0:T(8,128)} collective-permute-done((f32[256,512]{1,0:T(8,128)}, f32[256,512]{1,0:T(8,128)}, u32[]{:S(2)}, u32[]{:S(2)}) %collective-permute-start.4) | collective-permute-done | bytes 524320 | tf_op jit(solution)/shard_map/ppermute | solution.py:261
  56.6 6.5 %all-to-all-start.1 = ((f32[16,128,128]{2,1,0:T(8,128)}), f32[16,128,128]{2,1,0:T(8,128)S(1)}, u32[]{:S(2)}, u32[]{:S(2)}) async-start(f32[16,128,128]{2,1,0:T(8,128)} %across.1), calls=%async_computation.1 | async-start | bytes 2097152 | tf_op jit(solution)/shard_map/all_to_all | solution.py:273
  63.1 0.3 collective-permute-start.7
  63.4 0.3 collective-permute-start.8
  63.7 0.2 collective-permute-start.9
  63.9 0.3 collective-permute-start.10
  64.2 0.2 collective-permute-start.11
  64.4 17.1 %all-to-all-done.1.st_ref = f32[16,128,128]{2,1,0:T(8,128)S(1)} async-done(((f32[16,128,128]{2,1,0:T(8,128)}), f32[16,128,128]{2,1,0:T(8,128)S(1)}, u32[]{:S(2)}, u32[]{:S(2)}) %all-to-all-start.1) | async-done | bytes 1048608 | tf_op jit(solution)/shard_map/all_to_all | solution.py:273
  81.6 1.1 copy-done.1
  82.6 5.1 %mix.1 = (f32[512,256]{1,0:T(8,128)}, f32[512,256]{1,0:T(8,128)}) custom-call(f32[16]{0:T(128)} %g_ref.3, bf16[1024,256]{1,0:T(8,128)(2,1)} %get-tuple-element.59.vt_ref, bf16[256,128]{1,0:T(8,128)(2,1)} %bitcast.28, bf16[256,128]{1,0:T(8,128)(2,1)} %bitcast.31, f32[16,256]{1,0:T(8,128)} %bitcast.34, f32[16,256]{1,0:T(8,128)} %get-tuple-element.60.run_ref, ...), custom_call_target="tpu_custom_call" | custom-call | flops 268435456 | bytes 4194304 | tf_op jit(solution)/shard_map/mix/pallas_call | solution.py:25
  87.8 1.0 collective-permute-start.23
  88.8 1.1 collective-permute-start.22
  89.9 0.2 collective-permute-start.17
  90.1 2.4 %collective-permute-start.16 = (f32[512,256]{1,0:T(8,128)}, f32[512,256]{1,0:T(8,128)S(1)}, u32[]{:S(2)}, u32[]{:S(2)}) collective-permute-start(f32[512,256]{1,0:T(8,128)} %get-tuple-element.85.ma_ref.m0), channel_id=1, source_target_pairs={{0,8},{4,12},{8,0},{12,4},{16,24},{20,28},{24,16},{28,20},{32,40},... | collective-permute-start | bytes 1572872 | tf_op jit(solution)/shard_map/ppermute | solution.py:261
  92.6 10.4 %back.1 = (bf16[256,1024]{1,0:T(8,128)(2,1)}, f32[2,256,128]{2,1,0:T(8,128)}, f32[16,256]{1,0:T(8,128)}, f32[1,128]{1,0:T(1,128)}) custom-call(f32[16]{0:T(128)} %g_ref.3, bf16[1024,256]{1,0:T(8,128)(2,1)} %fusion.ut_ref, bf16[1024,256]{1,0:T(8,128)(2,1)} %get-tuple-element.59.vt_ref, bf16[256,128]{1,0:T(8,128)(2,1)} %bitcast.29, bf16[256,128]{1,0:T(8,128)(2,1)} %bitcast.32, ...), custom_call_target="tpu_custom_call" | custom-call | flops 1073741824 | bytes 6291456 | tf_op jit(solution)/shard_map/back/pallas_call | solution.py:25
  103.0 1.3 broadcast_in_dim.22
  104.2 6.4 %all-to-all-start.2 = ((f32[16,1,128]{2,1,0:T(1,128)}), f32[16,1,128]{2,1,0:T(1,128)S(1)}, u32[]{:S(2)}, u32[]{:S(2)}) async-start(f32[16,1,128]{2,1,0:T(1,128)} %broadcast_in_dim.22), calls=%async_computation.2 | async-start | bytes 16384 | tf_op jit(solution)/shard_map/all_to_all | solution.py:273
  110.7 3.5 %collective-permute-start.24 = (f32[512,256]{1,0:T(8,128)S(1)}, f32[512,256]{1,0:T(8,128)S(1)}, u32[]{:S(2)}, u32[]{:S(2)}) collective-permute-start(f32[512,256]{1,0:T(8,128)S(1)} %copy-done.6), channel_id=1, source_target_pairs={{0,32},{4,36},{8,40},{12,44},{16,48},{20,52},{24,56},{28,60},{32,0... | collective-permute-start | bytes 1572872 | tf_op jit(solution)/shard_map/ppermute | solution.py:261
  114.2 4.0 %all-to-all-done.2 = f32[16,1,128]{2,1,0:T(1,128)S(1)} async-done(((f32[16,1,128]{2,1,0:T(1,128)}), f32[16,1,128]{2,1,0:T(1,128)S(1)}, u32[]{:S(2)}, u32[]{:S(2)}) %all-to-all-start.2) | async-done | bytes 8224 | tf_op jit(solution)/shard_map/all_to_all | solution.py:273
  118.3 0.8 copy-done.10
  119.1 0.2 copy-done.11
  119.3 5.2 %grad_w_a.1 = (f32[2,512,128]{2,1,0:T(8,128)}, f32[2,512,128]{2,1,0:T(8,128)}, f32[2,512,128]{2,1,0:T(8,128)}, f32[2,512,128]{2,1,0:T(8,128)}) custom-call(s32[1]{0:T(128)} %bitcast.4.core, f32[512,256]{1,0:T(8,128)} %get-tuple-element.85.ma_ref.m0, f32[512,256]{1,0:T(8,128)} %collective-permute-done.15.m1, f32[512,256]{1,0:T(8,128)} %copy-done.11, ...), custom_call_target="tpu_custom_call" | custom-call | flops 1073741824 | bytes 8388608 | tf_op jit(solution)/shard_map/grad_w_a/pallas_call | solution.py:25
  124.5 0.6 collective-permute-start.18
  125.1 2.1 %collective-permute-start.19 = (f32[2,512,128]{2,1,0:T(8,128)}, f32[2,512,128]{2,1,0:T(8,128)S(1)}, u32[]{:S(2)}, u32[]{:S(2)}) collective-permute-start(f32[2,512,128]{2,1,0:T(8,128)} %get-tuple-element.91), channel_id=1, source_target_pairs={{0,32},{4,36},{8,40},{12,44},{16,48},{20,52},{24,56},{28,60},{32,0... | collective-permute-start | bytes 1572872 | tf_op jit(solution)/shard_map/ppermute | solution.py:261
  127.2 3.2 %collective-permute-start.14 = (f32[1,128]{1,0:T(1,128)S(1)}, f32[1,128]{1,0:T(1,128)S(1)}, u32[]{:S(2)}, u32[]{:S(2)}) collective-permute-start(f32[1,128]{1,0:T(1,128)S(1)} %bitcast.38), channel_id=1, source_target_pairs={{0,64},{64,0},{1,65},{65,1},{2,66},{66,2},{3,67},{67,3},{4,68},{68... | collective-permute-start | bytes 1544 | tf_op jit(solution)/shard_map/ppermute | solution.py:270
  130.4 1.2 collective-permute-start.20
  131.5 5.2 %grad_w_b.1 = (f32[2,512,128]{2,1,0:T(8,128)}, f32[2,512,128]{2,1,0:T(8,128)}, f32[2,512,128]{2,1,0:T(8,128)}, f32[2,512,128]{2,1,0:T(8,128)}) custom-call(s32[1]{0:T(128)} %bitcast.4.core, f32[512,256]{1,0:T(8,128)} %get-tuple-element.96.mb_ref.m0, f32[512,256]{1,0:T(8,128)} %copy-done.8, f32[512,256]{1,0:T(8,128)} %copy-done.9, f32[512,256]{1,0:T(8,128)} %copy-done.7, ...), custom_call_target="tpu_custom_call" | custom-call | flops 1073741824 | bytes 8388608 | tf_op jit(solution)/shard_map/grad_w_b/pallas_call | solution.py:25
  136.8 0.6 collective-permute-start.25
  137.3 2.1 %collective-permute-start.26 = (f32[2,512,128]{2,1,0:T(8,128)}, f32[2,512,128]{2,1,0:T(8,128)S(1)}, u32[]{:S(2)}, u32[]{:S(2)}) collective-permute-start(f32[2,512,128]{2,1,0:T(8,128)} %get-tuple-element.103), channel_id=1, source_target_pairs={{0,8},{4,12},{8,0},{12,4},{16,24},{20,28},{24,16},{28,20},{32,40},... | collective-permute-start | bytes 1572872 | tf_op jit(solution)/shard_map/ppermute | solution.py:261
  139.4 2.0 %collective-permute-start.27 = (f32[2,512,128]{2,1,0:T(8,128)}, f32[2,512,128]{2,1,0:T(8,128)S(1)}, u32[]{:S(2)}, u32[]{:S(2)}) collective-permute-start(f32[2,512,128]{2,1,0:T(8,128)} %get-tuple-element.104), channel_id=1, source_target_pairs={{0,12},{4,0},{8,4},{12,8},{16,28},{20,16},{24,20},{28,24},{32,44},... | collective-permute-start | bytes 1572872 | tf_op jit(solution)/shard_map/ppermute | solution.py:261
  141.4 7.2 %collective-permute-done.19.a2 = f32[2,512,128]{2,1,0:T(8,128)S(1)} collective-permute-done((f32[2,512,128]{2,1,0:T(8,128)}, f32[2,512,128]{2,1,0:T(8,128)S(1)}, u32[]{:S(2)}, u32[]{:S(2)}) %collective-permute-start.19) | collective-permute-done | bytes 524320 | tf_op jit(solution)/shard_map/ppermute | solution.py:261
  148.6 1.6 collective-permute-start.13
  150.2 2.2 %collective-permute-done.20.a3 = f32[2,512,128]{2,1,0:T(8,128)S(1)} collective-permute-done((f32[2,512,128]{2,1,0:T(8,128)}, f32[2,512,128]{2,1,0:T(8,128)S(1)}, u32[]{:S(2)}, u32[]{:S(2)}) %collective-permute-start.20) | collective-permute-done | bytes 524320 | tf_op jit(solution)/shard_map/ppermute | solution.py:261
  152.4 0.8 copy-done.14
  153.3 2.4 %gather_sum_a.1 = (f32[512,128]{1,0:T(8,128)}, f32[512,128]{1,0:T(8,128)}) custom-call(f32[2,512,128]{2,1,0:T(8,128)} %get-tuple-element.89.a0, f32[2,512,128]{2,1,0:T(8,128)} %copy-done.12, f32[2,512,128]{2,1,0:T(8,128)} %copy-done.13, f32[2,512,128]{2,1,0:T(8,128)} %copy-done.14), custom_call_target="tpu_custom_call" | custom-call | bytes 3145728 | tf_op jit(solution)/shard_map/gather_sum_a/pallas_call | solution.py:25
  155.6 3.2 %collective-permute-start.21 = (f32[512,128]{1,0:T(8,128)}, f32[512,128]{1,0:T(8,128)S(1)}, u32[]{:S(2)}, u32[]{:S(2)}) collective-permute-start(f32[512,128]{1,0:T(8,128)} %get-tuple-element.94), channel_id=1, source_target_pairs={{0,64},{64,0},{1,65},{65,1},{2,66},{66,2},{3,67},{67,3},{4,68},{68... | collective-permute-start | bytes 786440 | tf_op jit(solution)/shard_map/ppermute | solution.py:270
  158.8 4.1 %collective-permute-done.25.a1 = f32[2,512,128]{2,1,0:T(8,128)S(1)} collective-permute-done((f32[2,512,128]{2,1,0:T(8,128)}, f32[2,512,128]{2,1,0:T(8,128)S(1)}, u32[]{:S(2)}, u32[]{:S(2)}) %collective-permute-start.25) | collective-permute-done | bytes 524320 | tf_op jit(solution)/shard_map/ppermute | solution.py:261
  162.9 0.6 collective-permute-done.27.a3
  163.6 0.2 copy-done.15
  163.7 0.2 copy-done.16
  163.9 0.4 copy-done.17
  164.4 2.4 %gather_sum_b.1 = (f32[512,128]{1,0:T(8,128)}, f32[512,128]{1,0:T(8,128)}) custom-call(f32[2,512,128]{2,1,0:T(8,128)} %get-tuple-element.101.a0, f32[2,512,128]{2,1,0:T(8,128)} %copy-done.15, f32[2,512,128]{2,1,0:T(8,128)} %copy-done.16, f32[2,512,128]{2,1,0:T(8,128)} %copy-done.17), custom_call_target="tpu_custom_call" | custom-call | bytes 3145728 | tf_op jit(solution)/shard_map/gather_sum_b/pallas_call | solution.py:25
  166.7 0.4 collective-permute-start.28
  167.1 0.6 slice_bitcast_fusion
  167.7 0.7 fusion.1
  168.4 7.3 %collective-permute-done.28.b1 = f32[512,128]{1,0:T(8,128)S(1)} collective-permute-done((f32[512,128]{1,0:T(8,128)}, f32[512,128]{1,0:T(8,128)S(1)}, u32[]{:S(2)}, u32[]{:S(2)}) %collective-permute-start.28) | collective-permute-done | bytes 262176 | tf_op jit(solution)/shard_map/ppermute | solution.py:270
  175.7 0.7 copy-done.20
  176.4 2.2 %finish.1 = f32[128,1024]{1,0:T(8,128)} custom-call(f32[512,128]{1,0:T(8,128)} %get-tuple-element.93.a0, f32[512,128]{1,0:T(8,128)} %copy-done.19, f32[512,128]{1,0:T(8,128)} %get-tuple-element.105.b0, f32[512,128]{1,0:T(8,128)} %copy-done.20), custom_call_target="tpu_custom_call" | custom-call | bytes 2097152 | tf_op jit(solution)/shard_map/finish/pallas_call | solution.py:25
  (64 shorter events, 0.2 us)
Async XLA Ops:
  0.6 13.0 %copy-start.2 = (bf16[1,256,4096]{2,1,0:T(8,128)(2,1)S(1)}, bf16[1,256,4096]{2,1,0:T(8,128)(2,1)}, u32[]{:S(2)}) copy-start(bf16[1,256,4096]{2,1,0:T(8,128)(2,1)} %param.15) | copy-start | bytes 6291460
  0.6 12.3 %copy-start.21 = (f32[16]{0:T(128)S(1)}, f32[16]{0:T(128)}, u32[]{:S(2)}) copy-start(f32[16]{0:T(128)} %param.12) | copy-start | bytes 196
  5.5 19.1 %collective-permute-start = (f32[256,512]{1,0:T(8,128)}, f32[256,512]{1,0:T(8,128)}, u32[]{:S(2)}, u32[]{:S(2)}) collective-permute-start(f32[256,512]{1,0:T(8,128)} %get-tuple-element.62), channel_id=1, source_target_pairs={{0,4},{4,8},{8,12},{12,0},{16,20},{20,24},{24,28},{28,16},{32,36},... | collective-permute-start | bytes 1572872 | tf_op jit(solution)/shard_map/ppermute | solution.py:261
  7.5 17.1 %collective-permute-start.1 = (f32[256,512]{1,0:T(8,128)}, f32[256,512]{1,0:T(8,128)}, u32[]{:S(2)}, u32[]{:S(2)}) collective-permute-start(f32[256,512]{1,0:T(8,128)} %get-tuple-element.63), channel_id=1, source_target_pairs={{0,12},{4,0},{8,4},{12,8},{16,28},{20,16},{24,20},{28,24},{32,44},... | collective-permute-start | bytes 1572872 | tf_op jit(solution)/shard_map/ppermute | solution.py:261
  9.7 15.0 %collective-permute-start.2 = (f32[256,512]{1,0:T(8,128)}, f32[256,512]{1,0:T(8,128)S(1)}, u32[]{:S(2)}, u32[]{:S(2)}) collective-permute-start(f32[256,512]{1,0:T(8,128)} %get-tuple-element.64), channel_id=1, source_target_pairs={{0,16},{4,20},{8,24},{12,28},{16,32},{20,36},{24,40},{28,44},{32,4... | collective-permute-start | bytes 1572872 | tf_op jit(solution)/shard_map/ppermute | solution.py:261
  11.1 13.6 %collective-permute-start.3 = (f32[256,512]{1,0:T(8,128)}, f32[256,512]{1,0:T(8,128)S(1)}, u32[]{:S(2)}, u32[]{:S(2)}) collective-permute-start(f32[256,512]{1,0:T(8,128)} %get-tuple-element.65), channel_id=1, source_target_pairs={{0,48},{4,52},{8,56},{12,60},{16,0},{20,4},{24,8},{28,12},{32,16},... | collective-permute-start | bytes 1572872 | tf_op jit(solution)/shard_map/ppermute | solution.py:261
  24.7 39.0 %copy-start.3 = (f32[256,512]{1,0:T(8,128)}, f32[256,512]{1,0:T(8,128)S(1)}, u32[]{:S(2)}) copy-start(f32[256,512]{1,0:T(8,128)S(1)} %collective-permute-done.2.d1) | copy-start | bytes 1572868
  24.7 39.5 %copy-start.4 = (f32[256,512]{1,0:T(8,128)}, f32[256,512]{1,0:T(8,128)S(1)}, u32[]{:S(2)}) copy-start(f32[256,512]{1,0:T(8,128)S(1)} %collective-permute-done.3.d3) | copy-start | bytes 1572868
  24.7 24.1 %all-to-all-start = ((f32[16,136,128]{2,1,0:T(8,128)}), f32[16,136,128]{2,1,0:T(8,128)S(1)}, u32[]{:S(2)}, u32[]{:S(2)}) async-start(f32[16,136,128]{2,1,0:T(8,128)} %get-tuple-element.66), calls=%async_computation | async-start | bytes 2228224 | tf_op jit(solution)/shard_map/all_to_all | solution.py:273
  30.0 26.6 %collective-permute-start.4 = (f32[256,512]{1,0:T(8,128)}, f32[256,512]{1,0:T(8,128)}, u32[]{:S(2)}, u32[]{:S(2)}) collective-permute-start(f32[256,512]{1,0:T(8,128)} %get-tuple-element.70), channel_id=1, source_target_pairs={{0,8},{4,12},{8,0},{12,4},{16,24},{20,28},{24,16},{28,20},{32,40},... | collective-permute-start | bytes 1572872 | tf_op jit(solution)/shard_map/ppermute | solution.py:261
  33.4 23.2 %collective-permute-start.5 = (f32[256,512]{1,0:T(8,128)}, f32[256,512]{1,0:T(8,128)S(1)}, u32[]{:S(2)}, u32[]{:S(2)}) collective-permute-start(f32[256,512]{1,0:T(8,128)} %get-tuple-element.72), channel_id=1, source_target_pairs={{0,32},{4,36},{8,40},{12,44},{16,48},{20,52},{24,56},{28,60},{32,0... | collective-permute-start | bytes 1572872 | tf_op jit(solution)/shard_map/ppermute | solution.py:261
  48.8 1.0 copy-start
  56.6 46.4 %copy-start.5 = (f32[256,512]{1,0:T(8,128)}, f32[256,512]{1,0:T(8,128)S(1)}, u32[]{:S(2)}) copy-start(f32[256,512]{1,0:T(8,128)S(1)} %collective-permute-done.5.d2) | copy-start | bytes 1572868
  56.6 7.6 %collective-permute-start.6 = (f32[256,512]{1,0:T(8,128)}, f32[256,512]{1,0:T(8,128)}, u32[]{:S(2)}, u32[]{:S(2)}) collective-permute-start(f32[256,512]{1,0:T(8,128)} %collective-permute-done.d1), channel_id=1, source_target_pairs={{0,1},{1,0},{2,3},{3,2},{4,5},{5,4},{6,7},{7,6},{8,9},{9,8},{10,11... | collective-permute-start | bytes 1572872 | tf_op jit(solution)/shard_map/ppermute | solution.py:264
  56.6 25.0 %all-to-all-start.1 = ((f32[16,128,128]{2,1,0:T(8,128)}), f32[16,128,128]{2,1,0:T(8,128)S(1)}, u32[]{:S(2)}, u32[]{:S(2)}) async-start(f32[16,128,128]{2,1,0:T(8,128)} %across.1), calls=%async_computation.1 | async-start | bytes 2097152 | tf_op jit(solution)/shard_map/all_to_all | solution.py:273
  63.1 24.7 %collective-permute-start.7 = (f32[256,512]{1,0:T(8,128)}, f32[256,512]{1,0:T(8,128)}, u32[]{:S(2)}, u32[]{:S(2)}) collective-permute-start(f32[256,512]{1,0:T(8,128)} %collective-permute-done.4.d2), channel_id=1, source_target_pairs={{0,1},{1,0},{2,3},{3,2},{4,5},{5,4},{6,7},{7,6},{8,9},{9,8},{10,11... | collective-permute-start | bytes 1572872 | tf_op jit(solution)/shard_map/ppermute | solution.py:264
  63.4 24.4 %collective-permute-start.8 = (f32[256,512]{1,0:T(8,128)}, f32[256,512]{1,0:T(8,128)}, u32[]{:S(2)}, u32[]{:S(2)}) collective-permute-start(f32[256,512]{1,0:T(8,128)} %collective-permute-done.1.d3), channel_id=1, source_target_pairs={{0,1},{1,0},{2,3},{3,2},{4,5},{5,4},{6,7},{7,6},{8,9},{9,8},{10,11... | collective-permute-start | bytes 1572872 | tf_op jit(solution)/shard_map/ppermute | solution.py:264
  63.7 24.1 %collective-permute-start.9 = (f32[256,512]{1,0:T(8,128)S(1)}, f32[256,512]{1,0:T(8,128)}, u32[]{:S(2)}, u32[]{:S(2)}) collective-permute-start(f32[256,512]{1,0:T(8,128)S(1)} %collective-permute-done.2.d1), channel_id=1, source_target_pairs={{0,1},{1,0},{2,3},{3,2},{4,5},{5,4},{6,7},{7,6},{8,9},{9,8},{10,11... | collective-permute-start | bytes 1572872 | tf_op jit(solution)/shard_map/ppermute | solution.py:264
  63.9 23.9 %collective-permute-start.10 = (f32[256,512]{1,0:T(8,128)S(1)}, f32[256,512]{1,0:T(8,128)}, u32[]{:S(2)}, u32[]{:S(2)}) collective-permute-start(f32[256,512]{1,0:T(8,128)S(1)} %collective-permute-done.5.d2), channel_id=1, source_target_pairs={{0,1},{1,0},{2,3},{3,2},{4,5},{5,4},{6,7},{7,6},{8,9},{9,8},{10,11... | collective-permute-start | bytes 1572872 | tf_op jit(solution)/shard_map/ppermute | solution.py:264
  64.2 23.6 %collective-permute-start.11 = (f32[256,512]{1,0:T(8,128)S(1)}, f32[256,512]{1,0:T(8,128)}, u32[]{:S(2)}, u32[]{:S(2)}) collective-permute-start(f32[256,512]{1,0:T(8,128)S(1)} %collective-permute-done.3.d3), channel_id=1, source_target_pairs={{0,1},{1,0},{2,3},{3,2},{4,5},{5,4},{6,7},{7,6},{8,9},{9,8},{10,11... | collective-permute-start | bytes 1572872 | tf_op jit(solution)/shard_map/ppermute | solution.py:264
  81.6 1.1 copy-start.1
  87.8 22.9 %copy-start.6 = (f32[512,256]{1,0:T(8,128)S(1)}, f32[512,256]{1,0:T(8,128)}, u32[]{:S(2)}) copy-start(f32[512,256]{1,0:T(8,128)} %get-tuple-element.96.mb_ref.m0) | copy-start | bytes 1572868
  87.8 22.9 %collective-permute-start.23 = (f32[512,256]{1,0:T(8,128)}, f32[512,256]{1,0:T(8,128)S(1)}, u32[]{:S(2)}, u32[]{:S(2)}) collective-permute-start(f32[512,256]{1,0:T(8,128)} %get-tuple-element.96.mb_ref.m0), channel_id=1, source_target_pairs={{0,48},{4,52},{8,56},{12,60},{16,0},{20,4},{24,8},{28,12},{32,16},... | collective-permute-start | bytes 1572872 | tf_op jit(solution)/shard_map/ppermute | solution.py:261
  88.8 21.9 %collective-permute-start.22 = (f32[512,256]{1,0:T(8,128)}, f32[512,256]{1,0:T(8,128)S(1)}, u32[]{:S(2)}, u32[]{:S(2)}) collective-permute-start(f32[512,256]{1,0:T(8,128)} %get-tuple-element.96.mb_ref.m0), channel_id=1, source_target_pairs={{0,16},{4,20},{8,24},{12,28},{16,32},{20,36},{24,40},{28,44},{32,4... | collective-permute-start | bytes 1572872 | tf_op jit(solution)/shard_map/ppermute | solution.py:261
  89.9 28.4 %collective-permute-start.17 = (f32[512,256]{1,0:T(8,128)}, f32[512,256]{1,0:T(8,128)S(1)}, u32[]{:S(2)}, u32[]{:S(2)}) collective-permute-start(f32[512,256]{1,0:T(8,128)} %get-tuple-element.85.ma_ref.m0), channel_id=1, source_target_pairs={{0,12},{4,0},{8,4},{12,8},{16,28},{20,16},{24,20},{28,24},{32,44},... | collective-permute-start | bytes 1572872 | tf_op jit(solution)/shard_map/ppermute | solution.py:261
  90.1 28.2 %collective-permute-start.16 = (f32[512,256]{1,0:T(8,128)}, f32[512,256]{1,0:T(8,128)S(1)}, u32[]{:S(2)}, u32[]{:S(2)}) collective-permute-start(f32[512,256]{1,0:T(8,128)} %get-tuple-element.85.ma_ref.m0), channel_id=1, source_target_pairs={{0,8},{4,12},{8,0},{12,4},{16,24},{20,28},{24,16},{28,20},{32,40},... | collective-permute-start | bytes 1572872 | tf_op jit(solution)/shard_map/ppermute | solution.py:261
  92.6 25.8 %collective-permute-start.15 = (f32[512,256]{1,0:T(8,128)}, f32[512,256]{1,0:T(8,128)}, u32[]{:S(2)}, u32[]{:S(2)}) collective-permute-start(f32[512,256]{1,0:T(8,128)} %get-tuple-element.85.ma_ref.m0), channel_id=1, source_target_pairs={{0,4},{4,8},{8,12},{12,0},{16,20},{20,24},{24,28},{28,16},{32,36},... | collective-permute-start | bytes 1572872 | tf_op jit(solution)/shard_map/ppermute | solution.py:261
  104.2 14.0 %all-to-all-start.2 = ((f32[16,1,128]{2,1,0:T(1,128)}), f32[16,1,128]{2,1,0:T(1,128)S(1)}, u32[]{:S(2)}, u32[]{:S(2)}) async-start(f32[16,1,128]{2,1,0:T(1,128)} %broadcast_in_dim.22), calls=%async_computation.2 | async-start | bytes 16384 | tf_op jit(solution)/shard_map/all_to_all | solution.py:273
  110.7 13.8 %copy-start.7 = (f32[512,256]{1,0:T(8,128)}, f32[512,256]{1,0:T(8,128)S(1)}, u32[]{:S(2)}) copy-start(f32[512,256]{1,0:T(8,128)S(1)} %collective-permute-done.23.m3) | copy-start | bytes 1572868
  110.7 13.8 %copy-start.8 = (f32[512,256]{1,0:T(8,128)}, f32[512,256]{1,0:T(8,128)S(1)}, u32[]{:S(2)}) copy-start(f32[512,256]{1,0:T(8,128)S(1)} %collective-permute-done.22.m1) | copy-start | bytes 1572868
  110.7 19.6 %collective-permute-start.24 = (f32[512,256]{1,0:T(8,128)S(1)}, f32[512,256]{1,0:T(8,128)S(1)}, u32[]{:S(2)}, u32[]{:S(2)}) collective-permute-start(f32[512,256]{1,0:T(8,128)S(1)} %copy-done.6), channel_id=1, source_target_pairs={{0,32},{4,36},{8,40},{12,44},{16,48},{20,52},{24,56},{28,60},{32,0... | collective-permute-start | bytes 1572872 | tf_op jit(solution)/shard_map/ppermute | solution.py:261
  118.3 6.8 %copy-start.18 = (f32[2,256,128]{2,1,0:T(8,128)S(1)}, f32[2,256,128]{2,1,0:T(8,128)}, u32[]{:S(2)}) copy-start(f32[2,256,128]{2,1,0:T(8,128)} %get-tuple-element.82) | copy-start | bytes 786436
  118.3 0.8 copy-start.10
  118.3 0.9 copy-start.11
  124.5 15.0 %collective-permute-start.18 = (f32[2,512,128]{2,1,0:T(8,128)}, f32[2,512,128]{2,1,0:T(8,128)S(1)}, u32[]{:S(2)}, u32[]{:S(2)}) collective-permute-start(f32[2,512,128]{2,1,0:T(8,128)} %get-tuple-element.90), channel_id=1, source_target_pairs={{0,16},{4,20},{8,24},{12,28},{16,32},{20,36},{24,40},{28,44},{32,4... | collective-permute-start | bytes 1572872 | tf_op jit(solution)/shard_map/ppermute | solution.py:261
  125.1 12.2 %collective-permute-start.12 = (f32[2,256,128]{2,1,0:T(8,128)S(1)}, f32[2,256,128]{2,1,0:T(8,128)S(1)}, u32[]{:S(2)}, u32[]{:S(2)}) collective-permute-start(f32[2,256,128]{2,1,0:T(8,128)S(1)} %copy-done.18), channel_id=1, source_target_pairs={{0,1},{1,0},{2,3},{3,2},{4,5},{5,4},{6,7},{7,6},{8,9},{9,8},{10,11... | collective-permute-start | bytes 786440 | tf_op jit(solution)/shard_map/ppermute | solution.py:264
  125.1 23.5 %collective-permute-start.19 = (f32[2,512,128]{2,1,0:T(8,128)}, f32[2,512,128]{2,1,0:T(8,128)S(1)}, u32[]{:S(2)}, u32[]{:S(2)}) collective-permute-start(f32[2,512,128]{2,1,0:T(8,128)} %get-tuple-element.91), channel_id=1, source_target_pairs={{0,32},{4,36},{8,40},{12,44},{16,48},{20,52},{24,56},{28,60},{32,0... | collective-permute-start | bytes 1572872 | tf_op jit(solution)/shard_map/ppermute | solution.py:261
  127.2 9.6 %collective-permute-start.14 = (f32[1,128]{1,0:T(1,128)S(1)}, f32[1,128]{1,0:T(1,128)S(1)}, u32[]{:S(2)}, u32[]{:S(2)}) collective-permute-start(f32[1,128]{1,0:T(1,128)S(1)} %bitcast.38), channel_id=1, source_target_pairs={{0,64},{64,0},{1,65},{65,1},{2,66},{66,2},{3,67},{67,3},{4,68},{68... | collective-permute-start | bytes 1544 | tf_op jit(solution)/shard_map/ppermute | solution.py:270
  130.4 1.2 copy-start.9
  130.4 22.1 %collective-permute-start.20 = (f32[2,512,128]{2,1,0:T(8,128)}, f32[2,512,128]{2,1,0:T(8,128)S(1)}, u32[]{:S(2)}, u32[]{:S(2)}) collective-permute-start(f32[2,512,128]{2,1,0:T(8,128)} %get-tuple-element.92), channel_id=1, source_target_pairs={{0,48},{4,52},{8,56},{12,60},{16,0},{20,4},{24,8},{28,12},{32,16},... | collective-permute-start | bytes 1572872 | tf_op jit(solution)/shard_map/ppermute | solution.py:261
  136.8 26.2 %collective-permute-start.25 = (f32[2,512,128]{2,1,0:T(8,128)}, f32[2,512,128]{2,1,0:T(8,128)S(1)}, u32[]{:S(2)}, u32[]{:S(2)}) collective-permute-start(f32[2,512,128]{2,1,0:T(8,128)} %get-tuple-element.102), channel_id=1, source_target_pairs={{0,4},{4,8},{8,12},{12,0},{16,20},{20,24},{24,28},{28,16},{32,36},... | collective-permute-start | bytes 1572872 | tf_op jit(solution)/shard_map/ppermute | solution.py:261
  137.3 25.6 %collective-permute-start.26 = (f32[2,512,128]{2,1,0:T(8,128)}, f32[2,512,128]{2,1,0:T(8,128)S(1)}, u32[]{:S(2)}, u32[]{:S(2)}) collective-permute-start(f32[2,512,128]{2,1,0:T(8,128)} %get-tuple-element.103), channel_id=1, source_target_pairs={{0,8},{4,12},{8,0},{12,4},{16,24},{20,28},{24,16},{28,20},{32,40},... | collective-permute-start | bytes 1572872 | tf_op jit(solution)/shard_map/ppermute | solution.py:261
  139.4 13.0 %copy-start.12 = (f32[2,512,128]{2,1,0:T(8,128)}, f32[2,512,128]{2,1,0:T(8,128)S(1)}, u32[]{:S(2)}) copy-start(f32[2,512,128]{2,1,0:T(8,128)S(1)} %collective-permute-done.18.a1) | copy-start | bytes 1572868
  139.4 24.1 %collective-permute-start.27 = (f32[2,512,128]{2,1,0:T(8,128)}, f32[2,512,128]{2,1,0:T(8,128)S(1)}, u32[]{:S(2)}, u32[]{:S(2)}) collective-permute-start(f32[2,512,128]{2,1,0:T(8,128)} %get-tuple-element.104), channel_id=1, source_target_pairs={{0,12},{4,0},{8,4},{12,8},{16,28},{20,16},{24,20},{28,24},{32,44},... | collective-permute-start | bytes 1572872 | tf_op jit(solution)/shard_map/ppermute | solution.py:261
  148.6 3.8 %copy-start.13 = (f32[2,512,128]{2,1,0:T(8,128)}, f32[2,512,128]{2,1,0:T(8,128)S(1)}, u32[]{:S(2)}) copy-start(f32[2,512,128]{2,1,0:T(8,128)S(1)} %collective-permute-done.19.a2) | copy-start | bytes 1572868
  148.6 19.1 %collective-permute-start.13 = (f32[2,256,128]{2,1,0:T(8,128)S(1)}, f32[2,256,128]{2,1,0:T(8,128)S(1)}, u32[]{:S(2)}, u32[]{:S(2)}) collective-permute-start(f32[2,256,128]{2,1,0:T(8,128)S(1)} %add.10), channel_id=1, source_target_pairs={{0,2},{2,0},{1,3},{3,1},{4,6},{6,4},{5,7},{7,5},{8,10},{10,8},{9,1... | collective-permute-start | bytes 786440 | tf_op jit(solution)/shard_map/ppermute | solution.py:267
  152.4 0.8 copy-start.14
  155.6 12.8 %collective-permute-start.21 = (f32[512,128]{1,0:T(8,128)}, f32[512,128]{1,0:T(8,128)S(1)}, u32[]{:S(2)}, u32[]{:S(2)}) collective-permute-start(f32[512,128]{1,0:T(8,128)} %get-tuple-element.94), channel_id=1, source_target_pairs={{0,64},{64,0},{1,65},{65,1},{2,66},{66,2},{3,67},{67,3},{4,68},{68... | collective-permute-start | bytes 786440 | tf_op jit(solution)/shard_map/ppermute | solution.py:270
  162.9 0.8 copy-start.15
  162.9 1.0 copy-start.16
  163.6 0.8 copy-start.17
  166.7 9.0 %collective-permute-start.28 = (f32[512,128]{1,0:T(8,128)}, f32[512,128]{1,0:T(8,128)S(1)}, u32[]{:S(2)}, u32[]{:S(2)}) collective-permute-start(f32[512,128]{1,0:T(8,128)} %get-tuple-element.106), channel_id=1, source_target_pairs={{0,64},{64,0},{1,65},{65,1},{2,66},{66,2},{3,67},{67,3},{4,68},{68... | collective-permute-start | bytes 786440 | tf_op jit(solution)/shard_map/ppermute | solution.py:270
  168.4 7.3 %copy-start.19 = (f32[512,128]{1,0:T(8,128)}, f32[512,128]{1,0:T(8,128)S(1)}, u32[]{:S(2)}) copy-start(f32[512,128]{1,0:T(8,128)S(1)} %collective-permute-done.21.a1) | copy-start | bytes 786436
  175.7 0.7 copy-start.20

commit v3 on v2

--- a/solution.py
+++ b/solution.py
@@ -123,25 +123,31 @@
     return jnp.exp(jnp.where(i >= j, between, NEG)) * steps
 
 
-def mix_kernel(g_ref, vt_ref, b_ref, c_ref, s_ref, run_ref, st_ref, ma_ref, mb_ref, wide_ref, g2_ref):
+def inside_kernel(g_ref, vt_ref, b_ref, c_ref, s_ref, run_ref, o_ref, wide_ref, g2_ref):
     heads, tokens = s_ref.shape
     width = vt_ref.shape[0] // heads
     columns_of(run_ref[...], wide_ref)
     g2_ref[...] = dot(c_ref[...], b_ref[...], 1, 1)
-    half = heads // 2
-
-    def head(h, out_ref, base):
+
+    def head(h, _):
         row = run_ref[pl.ds(h, 1), :]
         mix = (weights_of(wide_ref[h], row, s_ref[pl.ds(h, 1), :], tokens) * g2_ref[...]).astype(BF16)
         at = pl.ds(pl.multiple_of(h * width, width), width)
         v = vt_ref[at, :]
-        inside = dot(v, mix, 1, 1)
-        carried = dot(st_ref[h, :width, :].astype(BF16), c_ref[...], 1, 1) * jnp.exp(row)
-        to = pl.ds(pl.multiple_of((h - base) * width, width), width)
-        out_ref[to, :] = inside + carried + g_ref[h] * v.astype(F32)
-
-    lax.fori_loop(0, half, lambda h, _: head(h, ma_ref, 0), None, unroll=2)
-    lax.fori_loop(half, heads, lambda h, _: head(h, mb_ref, half), None, unroll=2)
+        o_ref[at, :] = dot(v, mix, 1, 1) + g_ref[h] * v.astype(F32)
+
+    lax.fori_loop(0, heads, head, None, unroll=2)
+
+
+def mix_kernel(in_ref, c_ref, run_ref, st_ref, ma_ref, mb_ref):
+    heads = run_ref.shape[0]
+    width = in_ref.shape[0] // heads
+    half = heads // 2
+    c = c_ref[...]
+    for h in range(heads):
+        carried = dot(st_ref[h, :width, :].astype(BF16), c, 1, 1) * jnp.exp(run_ref[h : h + 1, :])
+        out_ref, to = (ma_ref, h) if h < half else (mb_ref, h - half)
+        out_ref[to * width : (to + 1) * width, :] = in_ref[h * width : (h + 1) * width, :] + carried
 
 
 def back_kernel(
@@ -297,17 +303,18 @@
     ends = later(ends, z1, z3, x1, x3)
     across = call(across_kernel, sds((shards, 2 * width, state), F32), "across", nbytes=2 << 20)(spread(ends))
     states = spread(across)
-    sent = [z1, z2, z3, x1, x2, x3]
 
     wide = pltpu.VMEM((heads, tokens, 128), F32)
     square = pltpu.VMEM((tokens, tokens), F32)
-    mixed_a, mixed_b = call(
-        mix_kernel, (sds((half, tokens), F32),) * 2, "mix", (wide, square), scalars=1, nbytes=4 << 20, flops=1 << 28
-    )(skip_gain, vt, b, c, steps, run, states)
-
-    swapped = [other_core(p) for p in lax.optimization_barrier((*sent, across))[:6]]
-    ready = lax.optimization_barrier((mixed_a, mixed_b, *swapped))
-    mixed_a, mixed_b, swapped = ready[0], ready[1], ready[2:]
+    inside = call(
+        inside_kernel, sds((channels, tokens), F32), "inside", (wide, square), scalars=1, nbytes=4 << 20, flops=1 << 28
+    )(skip_gain, vt, b, c, steps, later(run, across))
+    swapped = [other_core(p) for p in lax.optimization_barrier((z1, z2, z3, x1, x3, inside, x2))[:5]]
+    mixed_a, mixed_b = call(mix_kernel, (sds((half, tokens), F32),) * 2, "mix", nbytes=4 << 20, flops=1 << 27)(
+        inside, c, run, states
+    )
+    mixed_a, mixed_b, *swapped = lax.optimization_barrier((mixed_a, mixed_b, *swapped))
+    sent = [z1, z2, z3, x1, x2, x3]
     b1, b3 = shift(mixed_b, 1, 0), shift(mixed_b, 3, 0)
     a1, a3, a2 = shift(mixed_a, 0, 1), shift(mixed_a, 0, 3), shift(mixed_a, 0, 2)
 
@@ -334,7 +341,9 @@
     )(skip_gain, up_t, vt, b, c, steps, run, rates, states, mixed_a, mixed_b)
 
     b2 = shift(later(mixed_b, b1, b3, small), 2, 0)
+    small = later(small, b1, b3)
     small = spread(jnp.broadcast_to(small[None], (shards,) + small.shape)).sum(0)
+    swapped.insert(4, other_core(later(x2, small)))
 
     out = (sds((2, half, 128), F32),) * 4
     flops = 2 * half * 4 * tokens * 1024
@@ -348,6 +357,7 @@
     )
     rb = [pb[0]] + [shift(pb[k], 0, k) for k in range(1, SIDE)]
 
+    dbc = later(dbc, pa[0])
     dbc = dbc + other_core(dbc)
     dbc = dbc + other_chip(dbc)
     small = small + other_dp(small)

time: 179 us -> 173 us (0.966)
  waiting for transfers between devices: 59.4 us -> 44.2 us
  starting transfers between devices: 58.3 us -> 65.1 us
  Pallas kernels: 43.1 us -> 45.6 us
    all_to_all x3, waiting for transfers between devices: 33.6 us -> 23.3 us  [spread(): return lax.all_to_all(value, 'ctx', 0, 0, tiled=True)]
    all_to_all x3, starting transfers between devices: 18.2 us -> 22.9 us  [spread(): return lax.all_to_all(value, 'ctx', 0, 0, tiled=True)]
    ppermute x3, waiting for transfers between devices: 7.3 us -> 4.21 us  [other_dp(): return lax.ppermute(value, 'dp', [(0, 1), (1, 0)])]
    ppermute x3, starting transfers between devices: 6.75 us -> 9.29 us  [other_dp(): return lax.ppermute(value, 'dp', [(0, 1), (1, 0)])]
    pallas_call x10 -> x11, Pallas kernels: 43.1 us -> 45.6 us  [run(): pl.pallas_call(kernel, out_shape=outs, in_specs=specs, out_specs=jax.tree...]
    ppermute x18, waiting for transfers between devices: 18.6 us -> 16.6 us  [shift(): return lax.ppermute(value, 'ctx', pairs)]
  transfers between devices with their start and end apart: 32 -> 32, of which waited for: 9 -> 7; matrix products, arithmetic and copies ran while one was open for 6% -> 6% of each run, Pallas kernels for 21% -> 23%
where the time goes in v3:
time: 173 us; the launch traced here: 172 us
  starting transfers between devices  65.1 us (38%)
  Pallas kernels  45.6 us (26%)
  waiting for transfers between devices  44.2 us (26%)
  local copies, waits for them, and re-layouts  8.46 us (5%)
  matrix products  7.53 us (4%)
    pallas_call x11, Pallas kernels, run(): pl.pallas_call(kernel, out_shape=outs, in_specs=specs, out_specs=jax.tree...  45.6 us
    ppermute x18, starting transfers between devices, shift(): return lax.ppermute(value, 'ctx', pairs)  29.7 us
    all_to_all x3, waiting for transfers between devices, spread(): return lax.all_to_all(value, 'ctx', 0, 0, tiled=True)  23.3 us
    all_to_all x3, starting transfers between devices, spread(): return lax.all_to_all(value, 'ctx', 0, 0, tiled=True)  22.9 us
    ppermute x18, waiting for transfers between devices, shift(): return lax.ppermute(value, 'ctx', pairs)  16.6 us
    ppermute x3, starting transfers between devices, other_dp(): return lax.ppermute(value, 'dp', [(0, 1), (1, 0)])  9.29 us
    dot_general x1, matrix products, body(): lax.dot_general(w_out, later(cot, own_z), (((0,), (1,)), ((), ())), prefe...  7.53 us
    unnamed x44, local copies, waits for them, and re-layouts  5.19 us
  transfers between devices with their start and end apart: 32, of which 7 were waited for; matrix products, arithmetic and copies ran while one was open for 6% of the time, Pallas kernels for 23%

profile of v3, /device:TPU:0, one launch (start us, length us, event | category | flops | bytes accessed | tf_op | source)
XLA Modules:
  0.0 172.5 jit_solution(13218723479223526021)
XLA Ops:
  0.6 0.0 copy-start.2
  0.7 0.6 pad_add_fusion.pos
  1.3 4.3 %prep.1 = (f32[256,512]{1,0:T(8,128)}, f32[256,512]{1,0:T(8,128)}, f32[256,512]{1,0:T(8,128)}, f32[256,512]{1,0:T(8,128)}, f32[256,512]{1,0:T(8,128)}, /*index=5...) custom-call(s32[4]{0:T(128)} %pad_add_fusion.pos, bf16[256,4096]{1,0:T(8,128)(2,1)} %bitcast.24), custom_call_target="tpu_custom_call" | custom-call | bytes 7340032 | tf_op jit(solution)/shard_map/prep/pallas_call | solution.py:25
  5.5 2.0 %collective-permute-start = (f32[256,512]{1,0:T(8,128)}, f32[256,512]{1,0:T(8,128)}, u32[]{:S(2)}, u32[]{:S(2)}) collective-permute-start(f32[256,512]{1,0:T(8,128)} %get-tuple-element.64), channel_id=1, source_target_pairs={{0,4},{4,8},{8,12},{12,0},{16,20},{20,24},{24,28},{28,16},{32,36},... | collective-permute-start | bytes 1572872 | tf_op jit(solution)/shard_map/ppermute | solution.py:267
  7.5 2.1 %collective-permute-start.1 = (f32[256,512]{1,0:T(8,128)}, f32[256,512]{1,0:T(8,128)}, u32[]{:S(2)}, u32[]{:S(2)}) collective-permute-start(f32[256,512]{1,0:T(8,128)} %get-tuple-element.65), channel_id=1, source_target_pairs={{0,12},{4,0},{8,4},{12,8},{16,28},{20,16},{24,20},{28,24},{32,44},... | collective-permute-start | bytes 1572872 | tf_op jit(solution)/shard_map/ppermute | solution.py:267
  9.7 1.5 collective-permute-start.2
  11.1 1.8 %collective-permute-start.3 = (f32[256,512]{1,0:T(8,128)}, f32[256,512]{1,0:T(8,128)S(1)}, u32[]{:S(2)}, u32[]{:S(2)}) collective-permute-start(f32[256,512]{1,0:T(8,128)} %get-tuple-element.67), channel_id=1, source_target_pairs={{0,48},{4,52},{8,56},{12,60},{16,0},{20,4},{24,8},{28,12},{32,16},... | collective-permute-start | bytes 1572872 | tf_op jit(solution)/shard_map/ppermute | solution.py:267
  12.9 0.7 copy.22.r_ref
  13.6 7.5 %fusion.ut_ref = bf16[1024,256]{1,0:T(8,128)(2,1)} fusion(bf16[256,4096]{1,0:T(8,128)(2,1)S(1)} %bitcast.25, bf16[4096,1024]{1,0:T(8,128)(2,1)} %param.14), kind=kOutput, calls=%fused_computation.1 | convolution fusion | flops 2147745792 | bytes 11010048 | tf_op jit(solution)/shard_map/dot_general | solution.py:294
  21.1 3.5 %ends.1 = (bf16[1024,256]{1,0:T(8,128)(2,1)}, f32[16,136,128]{2,1,0:T(8,128)}, f32[16,256]{1,0:T(8,128)}) custom-call(bf16[1024,256]{1,0:T(8,128)(2,1)} %fusion.ut_ref, bf16[256,1024]{1,0:T(8,128)(2,1)} %bitcast.30, bf16[256,128]{1,0:T(8,128)(2,1)} %bitcast.31, bf16[256,128]{1,0:T(8,128)(2,1)} %bitcast.26, f32[16,256]{1,0:T(8,128)} %bitcast.34, ...), custom_call_target="tpu_custom_call" | custom-call | flops 134217728 | bytes 4194304 | tf_op jit(solution)/shard_map/ends/pallas_call | solution.py:25
  24.6 5.4 %all-to-all-start = ((f32[16,136,128]{2,1,0:T(8,128)}), f32[16,136,128]{2,1,0:T(8,128)S(1)}, u32[]{:S(2)}, u32[]{:S(2)}) async-start(f32[16,136,128]{2,1,0:T(8,128)} %get-tuple-element.68), calls=%async_computation | async-start | bytes 2228224 | tf_op jit(solution)/shard_map/all_to_all | solution.py:279
  30.0 3.4 %collective-permute-start.4 = (f32[256,512]{1,0:T(8,128)}, f32[256,512]{1,0:T(8,128)}, u32[]{:S(2)}, u32[]{:S(2)}) collective-permute-start(f32[256,512]{1,0:T(8,128)} %get-tuple-element.73), channel_id=1, source_target_pairs={{0,8},{4,12},{8,0},{12,4},{16,24},{20,28},{24,16},{28,20},{32,40},... | collective-permute-start | bytes 1572872 | tf_op jit(solution)/shard_map/ppermute | solution.py:267
  33.4 3.0 %collective-permute-start.5 = (f32[256,512]{1,0:T(8,128)}, f32[256,512]{1,0:T(8,128)S(1)}, u32[]{:S(2)}, u32[]{:S(2)}) collective-permute-start(f32[256,512]{1,0:T(8,128)} %get-tuple-element.75), channel_id=1, source_target_pairs={{0,32},{4,36},{8,40},{12,44},{16,48},{20,52},{24,56},{28,60},{32,0... | collective-permute-start | bytes 1572872 | tf_op jit(solution)/shard_map/ppermute | solution.py:267
  36.4 12.4 %all-to-all-done.e_ref = f32[16,136,128]{2,1,0:T(8,128)S(1)} async-done(((f32[16,136,128]{2,1,0:T(8,128)}), f32[16,136,128]{2,1,0:T(8,128)S(1)}, u32[]{:S(2)}, u32[]{:S(2)}) %all-to-all-start) | async-done | bytes 1114144 | tf_op jit(solution)/shard_map/all_to_all | solution.py:279
  48.8 1.0 copy-done
  49.8 2.4 %across.1 = f32[16,128,128]{2,1,0:T(8,128)} custom-call(f32[16,136,128]{2,1,0:T(8,128)} %copy-done), custom_call_target="tpu_custom_call" | custom-call | bytes 2097152 | tf_op jit(solution)/shard_map/across/pallas_call | solution.py:25
  52.2 10.7 %all-to-all-start.1 = ((f32[16,128,128]{2,1,0:T(8,128)}), f32[16,128,128]{2,1,0:T(8,128)S(1)}, u32[]{:S(2)}, u32[]{:S(2)}) async-start(f32[16,128,128]{2,1,0:T(8,128)} %across.1), calls=%async_computation.1 | async-start | bytes 2097152 | tf_op jit(solution)/shard_map/all_to_all | solution.py:279
  62.9 4.7 %inside.1.in_ref = f32[1024,256]{1,0:T(8,128)} custom-call(f32[16]{0:T(128)} %g_ref.3, bf16[1024,256]{1,0:T(8,128)(2,1)} %get-tuple-element.61.vt_ref, bf16[256,128]{1,0:T(8,128)(2,1)} %bitcast.32, bf16[256,128]{1,0:T(8,128)(2,1)} %bitcast.27, f32[16,256]{1,0:T(8,128)} %bitcast.35, f32[16,256]{1,0:T(8,128)} %get-tuple-element.69.run_ref), custom_call_target="tpu_custom_call" | custom-call | flops 268435456 | bytes 4194304 | tf_op jit(solution)/shard_map/inside/pallas_call | solution.py:25
  67.7 0.1 collective-permute-start.6
  67.8 0.5 collective-permute-start.7
  68.3 0.1 collective-permute-start.8
  68.4 0.4 collective-permute-start.9
  68.8 0.1 collective-permute-start.10
  68.9 7.0 %all-to-all-done.1.st_ref = f32[16,128,128]{2,1,0:T(8,128)S(1)} async-done(((f32[16,128,128]{2,1,0:T(8,128)}), f32[16,128,128]{2,1,0:T(8,128)S(1)}, u32[]{:S(2)}, u32[]{:S(2)}) %all-to-all-start.1) | async-done | bytes 1048608 | tf_op jit(solution)/shard_map/all_to_all | solution.py:279
  75.8 1.1 copy-done.1
  76.9 2.9 %mix.1 = (f32[512,256]{1,0:T(8,128)}, f32[512,256]{1,0:T(8,128)}) custom-call(f32[1024,256]{1,0:T(8,128)} %inside.1.in_ref, bf16[256,128]{1,0:T(8,128)(2,1)} %bitcast.28, f32[16,256]{1,0:T(8,128)} %get-tuple-element.69.run_ref, f32[16,128,128]{2,1,0:T(8,128)} %copy-done.1), custom_call_target="tpu_custom_call" | custom-call | flops 134217728 | bytes 4194304 | tf_op jit(solution)/shard_map/mix/pallas_call | solution.py:25
  79.9 1.3 collective-permute-start.12
  81.2 0.8 collective-permute-start.11
  82.0 0.9 collective-permute-start.15
  82.8 1.8 %collective-permute-start.14 = (f32[512,256]{1,0:T(8,128)}, f32[512,256]{1,0:T(8,128)}, u32[]{:S(2)}, u32[]{:S(2)}) collective-permute-start(f32[512,256]{1,0:T(8,128)} %get-tuple-element.87.ma_ref.m0), channel_id=1, source_target_pairs={{0,8},{4,12},{8,0},{12,4},{16,24},{20,28},{24,16},{28,20},{32,40},... | collective-permute-start | bytes 1572872 | tf_op jit(solution)/shard_map/ppermute | solution.py:267
  84.6 0.0 collective-permute-start.13
  84.6 10.4 %back.1 = (bf16[256,1024]{1,0:T(8,128)(2,1)}, f32[2,256,128]{2,1,0:T(8,128)}, f32[16,256]{1,0:T(8,128)}, f32[1,128]{1,0:T(1,128)}) custom-call(f32[16]{0:T(128)} %g_ref.3, bf16[1024,256]{1,0:T(8,128)(2,1)} %fusion.ut_ref, bf16[1024,256]{1,0:T(8,128)(2,1)} %get-tuple-element.61.vt_ref, bf16[256,128]{1,0:T(8,128)(2,1)} %bitcast.33, bf16[256,128]{1,0:T(8,128)(2,1)} %bitcast.29, ...), custom_call_target="tpu_custom_call" | custom-call | flops 1073741824 | bytes 6291456 | tf_op jit(solution)/shard_map/back/pallas_call | solution.py:25
  95.0 1.3 broadcast_in_dim.21
  96.3 6.8 %all-to-all-start.2 = ((f32[16,1,128]{2,1,0:T(1,128)}), f32[16,1,128]{2,1,0:T(1,128)S(1)}, u32[]{:S(2)}, u32[]{:S(2)}) async-start(f32[16,1,128]{2,1,0:T(1,128)} %broadcast_in_dim.21), calls=%async_computation.2 | async-start | bytes 16384 | tf_op jit(solution)/shard_map/all_to_all | solution.py:279
  103.2 3.5 %collective-permute-start.23 = (f32[512,256]{1,0:T(8,128)S(1)}, f32[512,256]{1,0:T(8,128)S(1)}, u32[]{:S(2)}, u32[]{:S(2)}) collective-permute-start(f32[512,256]{1,0:T(8,128)S(1)} %copy-done.6), channel_id=1, source_target_pairs={{0,32},{4,36},{8,40},{12,44},{16,48},{20,52},{24,56},{28,60},{32,0... | collective-permute-start | bytes 1572872 | tf_op jit(solution)/shard_map/ppermute | solution.py:267
  106.7 4.0 %all-to-all-done.2 = f32[16,1,128]{2,1,0:T(1,128)S(1)} async-done(((f32[16,1,128]{2,1,0:T(1,128)}), f32[16,1,128]{2,1,0:T(1,128)S(1)}, u32[]{:S(2)}, u32[]{:S(2)}) %all-to-all-start.2) | async-done | bytes 8224 | tf_op jit(solution)/shard_map/all_to_all | solution.py:279
  110.7 0.1 collective-permute-start.24
  110.8 0.0 copy-start.10
  110.8 0.8 copy-done.10
  111.6 5.3 %grad_w_a.1 = (f32[2,512,128]{2,1,0:T(8,128)}, f32[2,512,128]{2,1,0:T(8,128)}, f32[2,512,128]{2,1,0:T(8,128)}, f32[2,512,128]{2,1,0:T(8,128)}) custom-call(s32[1]{0:T(128)} %bitcast.4.core, f32[512,256]{1,0:T(8,128)} %get-tuple-element.87.ma_ref.m0, f32[512,256]{1,0:T(8,128)} %collective-permute-done.13.m1, f32[512,256]{1,0:T(8,128)} %collective-permute-done.14.m2, ...), custom_call_target="tpu_custom_call" | custom-call | flops 1073741824 | bytes 8388608 | tf_op jit(solution)/shard_map/grad_w_a/pallas_call | solution.py:25
  116.9 0.7 collective-permute-start.19
  117.6 0.2 collective-permute-start.16
  117.8 2.1 %collective-permute-start.20 = (f32[2,512,128]{2,1,0:T(8,128)}, f32[2,512,128]{2,1,0:T(8,128)S(1)}, u32[]{:S(2)}, u32[]{:S(2)}) collective-permute-start(f32[2,512,128]{2,1,0:T(8,128)} %get-tuple-element.95), channel_id=1, source_target_pairs={{0,32},{4,36},{8,40},{12,44},{16,48},{20,52},{24,56},{28,60},{32,0... | collective-permute-start | bytes 1572872 | tf_op jit(solution)/shard_map/ppermute | solution.py:267
  119.9 3.2 %collective-permute-start.18 = (f32[1,128]{1,0:T(1,128)S(1)}, f32[1,128]{1,0:T(1,128)S(1)}, u32[]{:S(2)}, u32[]{:S(2)}) collective-permute-start(f32[1,128]{1,0:T(1,128)S(1)} %bitcast.39), channel_id=1, source_target_pairs={{0,64},{64,0},{1,65},{65,1},{2,66},{66,2},{3,67},{67,3},{4,68},{68... | collective-permute-start | bytes 1544 | tf_op jit(solution)/shard_map/ppermute | solution.py:276
  123.1 1.1 collective-permute-start.21
  124.2 5.2 %grad_w_b.1 = (f32[2,512,128]{2,1,0:T(8,128)}, f32[2,512,128]{2,1,0:T(8,128)}, f32[2,512,128]{2,1,0:T(8,128)}, f32[2,512,128]{2,1,0:T(8,128)}) custom-call(s32[1]{0:T(128)} %bitcast.4.core, f32[512,256]{1,0:T(8,128)} %get-tuple-element.100.mb_ref.m0, f32[512,256]{1,0:T(8,128)} %copy-done.8, f32[512,256]{1,0:T(8,128)} %copy-done.9, f32[512,256]{1,0:T(8,128)} %copy-done.7, ...), custom_call_target="tpu_custom_call" | custom-call | flops 1073741824 | bytes 8388608 | tf_op jit(solution)/shard_map/grad_w_b/pallas_call | solution.py:25
  129.4 0.6 collective-permute-start.25
  130.0 2.1 %collective-permute-start.26 = (f32[2,512,128]{2,1,0:T(8,128)}, f32[2,512,128]{2,1,0:T(8,128)S(1)}, u32[]{:S(2)}, u32[]{:S(2)}) collective-permute-start(f32[2,512,128]{2,1,0:T(8,128)} %get-tuple-element.107), channel_id=1, source_target_pairs={{0,8},{4,12},{8,0},{12,4},{16,24},{20,28},{24,16},{28,20},{32,40},... | collective-permute-start | bytes 1572872 | tf_op jit(solution)/shard_map/ppermute | solution.py:267
  132.1 11.8 %collective-permute-done.19.a1 = f32[2,512,128]{2,1,0:T(8,128)S(1)} collective-permute-done((f32[2,512,128]{2,1,0:T(8,128)}, f32[2,512,128]{2,1,0:T(8,128)S(1)}, u32[]{:S(2)}, u32[]{:S(2)}) %collective-permute-start.19) | collective-permute-done | bytes 524320 | tf_op jit(solution)/shard_map/ppermute | solution.py:267
  143.9 1.2 collective-permute-start.27
  145.1 1.7 collective-permute-start.17
  146.8 0.8 copy-done.14
  147.6 2.4 %gather_sum_a.1 = (f32[512,128]{1,0:T(8,128)}, f32[512,128]{1,0:T(8,128)}) custom-call(f32[2,512,128]{2,1,0:T(8,128)} %get-tuple-element.91.a0, f32[2,512,128]{2,1,0:T(8,128)} %copy-done.12, f32[2,512,128]{2,1,0:T(8,128)} %copy-done.13, f32[2,512,128]{2,1,0:T(8,128)} %copy-done.14), custom_call_target="tpu_custom_call" | custom-call | bytes 3145728 | tf_op jit(solution)/shard_map/gather_sum_a/pallas_call | solution.py:25
  150.0 2.9 %collective-permute-start.22 = (f32[512,128]{1,0:T(8,128)}, f32[512,128]{1,0:T(8,128)S(1)}, u32[]{:S(2)}, u32[]{:S(2)}) collective-permute-start(f32[512,128]{1,0:T(8,128)} %get-tuple-element.98), channel_id=1, source_target_pairs={{0,64},{64,0},{1,65},{65,1},{2,66},{66,2},{3,67},{67,3},{4,68},{68... | collective-permute-start | bytes 786440 | tf_op jit(solution)/shard_map/ppermute | solution.py:276
  152.9 2.5 %collective-permute-done.25.a1 = f32[2,512,128]{2,1,0:T(8,128)S(1)} collective-permute-done((f32[2,512,128]{2,1,0:T(8,128)}, f32[2,512,128]{2,1,0:T(8,128)S(1)}, u32[]{:S(2)}, u32[]{:S(2)}) %collective-permute-start.25) | collective-permute-done | bytes 524320 | tf_op jit(solution)/shard_map/ppermute | solution.py:267
  155.4 2.3 %collective-permute-done.27.a3 = f32[2,512,128]{2,1,0:T(8,128)S(1)} collective-permute-done((f32[2,512,128]{2,1,0:T(8,128)}, f32[2,512,128]{2,1,0:T(8,128)S(1)}, u32[]{:S(2)}, u32[]{:S(2)}) %collective-permute-start.27) | collective-permute-done | bytes 524320 | tf_op jit(solution)/shard_map/ppermute | solution.py:267
  157.7 0.8 copy-done.17
  158.4 2.4 %gather_sum_b.1 = (f32[512,128]{1,0:T(8,128)}, f32[512,128]{1,0:T(8,128)}) custom-call(f32[2,512,128]{2,1,0:T(8,128)} %get-tuple-element.105.a0, f32[2,512,128]{2,1,0:T(8,128)} %copy-done.15, f32[2,512,128]{2,1,0:T(8,128)} %copy-done.16, f32[2,512,128]{2,1,0:T(8,128)} %copy-done.17), custom_call_target="tpu_custom_call" | custom-call | bytes 3145728 | tf_op jit(solution)/shard_map/gather_sum_b/pallas_call | solution.py:25
  160.8 3.2 %collective-permute-start.28 = (f32[512,128]{1,0:T(8,128)}, f32[512,128]{1,0:T(8,128)S(1)}, u32[]{:S(2)}, u32[]{:S(2)}) collective-permute-start(f32[512,128]{1,0:T(8,128)} %get-tuple-element.110), channel_id=1, source_target_pairs={{0,64},{64,0},{1,65},{65,1},{2,66},{66,2},{3,67},{67,3},{4,68},{68... | collective-permute-start | bytes 786440 | tf_op jit(solution)/shard_map/ppermute | solution.py:276
  164.0 0.6 slice_bitcast_fusion
  164.6 0.7 fusion.1
  165.4 4.2 %collective-permute-done.28.b1 = f32[512,128]{1,0:T(8,128)S(1)} collective-permute-done((f32[512,128]{1,0:T(8,128)}, f32[512,128]{1,0:T(8,128)S(1)}, u32[]{:S(2)}, u32[]{:S(2)}) %collective-permute-start.28) | collective-permute-done | bytes 262176 | tf_op jit(solution)/shard_map/ppermute | solution.py:276
  169.6 0.7 copy-done.20
  170.3 2.2 %finish.1 = f32[128,1024]{1,0:T(8,128)} custom-call(f32[512,128]{1,0:T(8,128)} %get-tuple-element.97.a0, f32[512,128]{1,0:T(8,128)} %copy-done.19, f32[512,128]{1,0:T(8,128)} %get-tuple-element.109.b0, f32[512,128]{1,0:T(8,128)} %copy-done.20), custom_call_target="tpu_custom_call" | custom-call | bytes 2097152 | tf_op jit(solution)/shard_map/finish/pallas_call | solution.py:25
  (65 shorter events, 0.2 us)
Async XLA Ops:
  0.6 13.0 %copy-start.2 = (bf16[1,256,4096]{2,1,0:T(8,128)(2,1)S(1)}, bf16[1,256,4096]{2,1,0:T(8,128)(2,1)}, u32[]{:S(2)}) copy-start(bf16[1,256,4096]{2,1,0:T(8,128)(2,1)} %param.15) | copy-start | bytes 6291460
  0.6 12.3 %copy-start.21 = (f32[16]{0:T(128)S(1)}, f32[16]{0:T(128)}, u32[]{:S(2)}) copy-start(f32[16]{0:T(128)} %param.12) | copy-start | bytes 196
  5.5 19.0 %collective-permute-start = (f32[256,512]{1,0:T(8,128)}, f32[256,512]{1,0:T(8,128)}, u32[]{:S(2)}, u32[]{:S(2)}) collective-permute-start(f32[256,512]{1,0:T(8,128)} %get-tuple-element.64), channel_id=1, source_target_pairs={{0,4},{4,8},{8,12},{12,0},{16,20},{20,24},{24,28},{28,16},{32,36},... | collective-permute-start | bytes 1572872 | tf_op jit(solution)/shard_map/ppermute | solution.py:267
  7.5 17.1 %collective-permute-start.1 = (f32[256,512]{1,0:T(8,128)}, f32[256,512]{1,0:T(8,128)}, u32[]{:S(2)}, u32[]{:S(2)}) collective-permute-start(f32[256,512]{1,0:T(8,128)} %get-tuple-element.65), channel_id=1, source_target_pairs={{0,12},{4,0},{8,4},{12,8},{16,28},{20,16},{24,20},{28,24},{32,44},... | collective-permute-start | bytes 1572872 | tf_op jit(solution)/shard_map/ppermute | solution.py:267
  9.7 14.9 %collective-permute-start.2 = (f32[256,512]{1,0:T(8,128)}, f32[256,512]{1,0:T(8,128)S(1)}, u32[]{:S(2)}, u32[]{:S(2)}) collective-permute-start(f32[256,512]{1,0:T(8,128)} %get-tuple-element.66), channel_id=1, source_target_pairs={{0,16},{4,20},{8,24},{12,28},{16,32},{20,36},{24,40},{28,44},{32,4... | collective-permute-start | bytes 1572872 | tf_op jit(solution)/shard_map/ppermute | solution.py:267
  11.1 13.5 %collective-permute-start.3 = (f32[256,512]{1,0:T(8,128)}, f32[256,512]{1,0:T(8,128)S(1)}, u32[]{:S(2)}, u32[]{:S(2)}) collective-permute-start(f32[256,512]{1,0:T(8,128)} %get-tuple-element.67), channel_id=1, source_target_pairs={{0,48},{4,52},{8,56},{12,60},{16,0},{20,4},{24,8},{28,12},{32,16},... | collective-permute-start | bytes 1572872 | tf_op jit(solution)/shard_map/ppermute | solution.py:267
  24.6 43.8 %copy-start.3 = (f32[256,512]{1,0:T(8,128)}, f32[256,512]{1,0:T(8,128)S(1)}, u32[]{:S(2)}) copy-start(f32[256,512]{1,0:T(8,128)S(1)} %collective-permute-done.2.d1) | copy-start | bytes 1572868
  24.6 44.2 %copy-start.4 = (f32[256,512]{1,0:T(8,128)}, f32[256,512]{1,0:T(8,128)S(1)}, u32[]{:S(2)}) copy-start(f32[256,512]{1,0:T(8,128)S(1)} %collective-permute-done.3.d3) | copy-start | bytes 1572868
  24.6 24.2 %all-to-all-start = ((f32[16,136,128]{2,1,0:T(8,128)}), f32[16,136,128]{2,1,0:T(8,128)S(1)}, u32[]{:S(2)}, u32[]{:S(2)}) async-start(f32[16,136,128]{2,1,0:T(8,128)} %get-tuple-element.68), calls=%async_computation | async-start | bytes 2228224 | tf_op jit(solution)/shard_map/all_to_all | solution.py:279
  30.0 37.7 %collective-permute-start.4 = (f32[256,512]{1,0:T(8,128)}, f32[256,512]{1,0:T(8,128)}, u32[]{:S(2)}, u32[]{:S(2)}) collective-permute-start(f32[256,512]{1,0:T(8,128)} %get-tuple-element.73), channel_id=1, source_target_pairs={{0,8},{4,12},{8,0},{12,4},{16,24},{20,28},{24,16},{28,20},{32,40},... | collective-permute-start | bytes 1572872 | tf_op jit(solution)/shard_map/ppermute | solution.py:267
  33.4 34.2 %collective-permute-start.5 = (f32[256,512]{1,0:T(8,128)}, f32[256,512]{1,0:T(8,128)S(1)}, u32[]{:S(2)}, u32[]{:S(2)}) collective-permute-start(f32[256,512]{1,0:T(8,128)} %get-tuple-element.75), channel_id=1, source_target_pairs={{0,32},{4,36},{8,40},{12,44},{16,48},{20,52},{24,56},{28,60},{32,0... | collective-permute-start | bytes 1572872 | tf_op jit(solution)/shard_map/ppermute | solution.py:267
  48.8 1.0 copy-start
  52.2 23.7 %all-to-all-start.1 = ((f32[16,128,128]{2,1,0:T(8,128)}), f32[16,128,128]{2,1,0:T(8,128)S(1)}, u32[]{:S(2)}, u32[]{:S(2)}) async-start(f32[16,128,128]{2,1,0:T(8,128)} %across.1), calls=%async_computation.1 | async-start | bytes 2097152 | tf_op jit(solution)/shard_map/all_to_all | solution.py:279
  67.7 56.5 %copy-start.5 = (f32[256,512]{1,0:T(8,128)}, f32[256,512]{1,0:T(8,128)S(1)}, u32[]{:S(2)}) copy-start(f32[256,512]{1,0:T(8,128)S(1)} %collective-permute-done.5.d2) | copy-start | bytes 1572868
  67.7 12.1 %collective-permute-start.6 = (f32[256,512]{1,0:T(8,128)}, f32[256,512]{1,0:T(8,128)}, u32[]{:S(2)}, u32[]{:S(2)}) collective-permute-start(f32[256,512]{1,0:T(8,128)} %collective-permute-done.d1), channel_id=1, source_target_pairs={{0,1},{1,0},{2,3},{3,2},{4,5},{5,4},{6,7},{7,6},{8,9},{9,8},{10,11... | collective-permute-start | bytes 1572872 | tf_op jit(solution)/shard_map/ppermute | solution.py:270
  67.8 12.1 %collective-permute-start.7 = (f32[256,512]{1,0:T(8,128)}, f32[256,512]{1,0:T(8,128)}, u32[]{:S(2)}, u32[]{:S(2)}) collective-permute-start(f32[256,512]{1,0:T(8,128)} %collective-permute-done.4.d2), channel_id=1, source_target_pairs={{0,1},{1,0},{2,3},{3,2},{4,5},{5,4},{6,7},{7,6},{8,9},{9,8},{10,11... | collective-permute-start | bytes 1572872 | tf_op jit(solution)/shard_map/ppermute | solution.py:270
  68.3 11.6 %collective-permute-start.8 = (f32[256,512]{1,0:T(8,128)}, f32[256,512]{1,0:T(8,128)}, u32[]{:S(2)}, u32[]{:S(2)}) collective-permute-start(f32[256,512]{1,0:T(8,128)} %collective-permute-done.1.d3), channel_id=1, source_target_pairs={{0,1},{1,0},{2,3},{3,2},{4,5},{5,4},{6,7},{7,6},{8,9},{9,8},{10,11... | collective-permute-start | bytes 1572872 | tf_op jit(solution)/shard_map/ppermute | solution.py:270
  68.4 11.5 %collective-permute-start.9 = (f32[256,512]{1,0:T(8,128)S(1)}, f32[256,512]{1,0:T(8,128)}, u32[]{:S(2)}, u32[]{:S(2)}) collective-permute-start(f32[256,512]{1,0:T(8,128)S(1)} %collective-permute-done.2.d1), channel_id=1, source_target_pairs={{0,1},{1,0},{2,3},{3,2},{4,5},{5,4},{6,7},{7,6},{8,9},{9,8},{10,11... | collective-permute-start | bytes 1572872 | tf_op jit(solution)/shard_map/ppermute | solution.py:270
  68.8 11.1 %collective-permute-start.10 = (f32[256,512]{1,0:T(8,128)S(1)}, f32[256,512]{1,0:T(8,128)}, u32[]{:S(2)}, u32[]{:S(2)}) collective-permute-start(f32[256,512]{1,0:T(8,128)S(1)} %collective-permute-done.3.d3), channel_id=1, source_target_pairs={{0,1},{1,0},{2,3},{3,2},{4,5},{5,4},{6,7},{7,6},{8,9},{9,8},{10,11... | collective-permute-start | bytes 1572872 | tf_op jit(solution)/shard_map/ppermute | solution.py:270
  75.8 1.1 copy-start.1
  79.8 23.3 %copy-start.6 = (f32[512,256]{1,0:T(8,128)S(1)}, f32[512,256]{1,0:T(8,128)}, u32[]{:S(2)}) copy-start(f32[512,256]{1,0:T(8,128)} %get-tuple-element.100.mb_ref.m0) | copy-start | bytes 1572868
  79.9 15.1 %collective-permute-start.12 = (f32[512,256]{1,0:T(8,128)}, f32[512,256]{1,0:T(8,128)S(1)}, u32[]{:S(2)}, u32[]{:S(2)}) collective-permute-start(f32[512,256]{1,0:T(8,128)} %get-tuple-element.100.mb_ref.m0), channel_id=1, source_target_pairs={{0,48},{4,52},{8,56},{12,60},{16,0},{20,4},{24,8},{28,12},{32,16},... | collective-permute-start | bytes 1572872 | tf_op jit(solution)/shard_map/ppermute | solution.py:267
  81.2 13.8 %collective-permute-start.11 = (f32[512,256]{1,0:T(8,128)}, f32[512,256]{1,0:T(8,128)S(1)}, u32[]{:S(2)}, u32[]{:S(2)}) collective-permute-start(f32[512,256]{1,0:T(8,128)} %get-tuple-element.100.mb_ref.m0), channel_id=1, source_target_pairs={{0,16},{4,20},{8,24},{12,28},{16,32},{20,36},{24,40},{28,44},{32,4... | collective-permute-start | bytes 1572872 | tf_op jit(solution)/shard_map/ppermute | solution.py:267
  82.0 28.8 %collective-permute-start.15 = (f32[512,256]{1,0:T(8,128)}, f32[512,256]{1,0:T(8,128)S(1)}, u32[]{:S(2)}, u32[]{:S(2)}) collective-permute-start(f32[512,256]{1,0:T(8,128)} %get-tuple-element.87.ma_ref.m0), channel_id=1, source_target_pairs={{0,12},{4,0},{8,4},{12,8},{16,28},{20,16},{24,20},{28,24},{32,44},... | collective-permute-start | bytes 1572872 | tf_op jit(solution)/shard_map/ppermute | solution.py:267
  82.8 28.0 %collective-permute-start.14 = (f32[512,256]{1,0:T(8,128)}, f32[512,256]{1,0:T(8,128)}, u32[]{:S(2)}, u32[]{:S(2)}) collective-permute-start(f32[512,256]{1,0:T(8,128)} %get-tuple-element.87.ma_ref.m0), channel_id=1, source_target_pairs={{0,8},{4,12},{8,0},{12,4},{16,24},{20,28},{24,16},{28,20},{32,40},... | collective-permute-start | bytes 1572872 | tf_op jit(solution)/shard_map/ppermute | solution.py:267
  84.6 26.2 %collective-permute-start.13 = (f32[512,256]{1,0:T(8,128)}, f32[512,256]{1,0:T(8,128)}, u32[]{:S(2)}, u32[]{:S(2)}) collective-permute-start(f32[512,256]{1,0:T(8,128)} %get-tuple-element.87.ma_ref.m0), channel_id=1, source_target_pairs={{0,4},{4,8},{8,12},{12,0},{16,20},{20,24},{24,28},{28,16},{32,36},... | collective-permute-start | bytes 1572872 | tf_op jit(solution)/shard_map/ppermute | solution.py:267
  95.0 21.8 %copy-start.7 = (f32[512,256]{1,0:T(8,128)}, f32[512,256]{1,0:T(8,128)S(1)}, u32[]{:S(2)}) copy-start(f32[512,256]{1,0:T(8,128)S(1)} %collective-permute-done.12.m3) | copy-start | bytes 1572868
  95.0 21.8 %copy-start.8 = (f32[512,256]{1,0:T(8,128)}, f32[512,256]{1,0:T(8,128)S(1)}, u32[]{:S(2)}) copy-start(f32[512,256]{1,0:T(8,128)S(1)} %collective-permute-done.11.m1) | copy-start | bytes 1572868
  96.3 14.3 %all-to-all-start.2 = ((f32[16,1,128]{2,1,0:T(1,128)}), f32[16,1,128]{2,1,0:T(1,128)S(1)}, u32[]{:S(2)}, u32[]{:S(2)}) async-start(f32[16,1,128]{2,1,0:T(1,128)} %broadcast_in_dim.21), calls=%async_computation.2 | async-start | bytes 16384 | tf_op jit(solution)/shard_map/all_to_all | solution.py:279
  103.2 16.7 %collective-permute-start.23 = (f32[512,256]{1,0:T(8,128)S(1)}, f32[512,256]{1,0:T(8,128)S(1)}, u32[]{:S(2)}, u32[]{:S(2)}) collective-permute-start(f32[512,256]{1,0:T(8,128)S(1)} %copy-done.6), channel_id=1, source_target_pairs={{0,32},{4,36},{8,40},{12,44},{16,48},{20,52},{24,56},{28,60},{32,0... | collective-permute-start | bytes 1572872 | tf_op jit(solution)/shard_map/ppermute | solution.py:267
  110.7 6.9 %copy-start.18 = (f32[2,256,128]{2,1,0:T(8,128)S(1)}, f32[2,256,128]{2,1,0:T(8,128)}, u32[]{:S(2)}) copy-start(f32[2,256,128]{2,1,0:T(8,128)} %get-tuple-element.92) | copy-start | bytes 786436
  110.7 12.4 %collective-permute-start.24 = (f32[256,512]{1,0:T(8,128)S(1)}, f32[256,512]{1,0:T(8,128)S(1)}, u32[]{:S(2)}, u32[]{:S(2)}) collective-permute-start(f32[256,512]{1,0:T(8,128)S(1)} %collective-permute-done.5.d2), channel_id=1, source_target_pairs={{0,1},{1,0},{2,3},{3,2},{4,5},{5,4},{6,7},{7,6},{8,9},{9,8},{10,11... | collective-permute-start | bytes 1572872 | tf_op jit(solution)/shard_map/ppermute | solution.py:270
  110.8 0.8 copy-start.10
  116.9 27.0 %collective-permute-start.19 = (f32[2,512,128]{2,1,0:T(8,128)}, f32[2,512,128]{2,1,0:T(8,128)S(1)}, u32[]{:S(2)}, u32[]{:S(2)}) collective-permute-start(f32[2,512,128]{2,1,0:T(8,128)} %get-tuple-element.94), channel_id=1, source_target_pairs={{0,16},{4,20},{8,24},{12,28},{16,32},{20,36},{24,40},{28,44},{32,4... | collective-permute-start | bytes 1572872 | tf_op jit(solution)/shard_map/ppermute | solution.py:267
  117.6 12.4 %collective-permute-start.16 = (f32[2,256,128]{2,1,0:T(8,128)S(1)}, f32[2,256,128]{2,1,0:T(8,128)S(1)}, u32[]{:S(2)}, u32[]{:S(2)}) collective-permute-start(f32[2,256,128]{2,1,0:T(8,128)S(1)} %copy-done.18), channel_id=1, source_target_pairs={{0,1},{1,0},{2,3},{3,2},{4,5},{5,4},{6,7},{7,6},{8,9},{9,8},{10,11... | collective-permute-start | bytes 786440 | tf_op jit(solution)/shard_map/ppermute | solution.py:270
  117.8 27.4 %collective-permute-start.20 = (f32[2,512,128]{2,1,0:T(8,128)}, f32[2,512,128]{2,1,0:T(8,128)S(1)}, u32[]{:S(2)}, u32[]{:S(2)}) collective-permute-start(f32[2,512,128]{2,1,0:T(8,128)} %get-tuple-element.95), channel_id=1, source_target_pairs={{0,32},{4,36},{8,40},{12,44},{16,48},{20,52},{24,56},{28,60},{32,0... | collective-permute-start | bytes 1572872 | tf_op jit(solution)/shard_map/ppermute | solution.py:267
  119.9 4.3 %copy-start.9 = (f32[512,256]{1,0:T(8,128)}, f32[512,256]{1,0:T(8,128)S(1)}, u32[]{:S(2)}) copy-start(f32[512,256]{1,0:T(8,128)S(1)} %collective-permute-done.23.m2) | copy-start | bytes 1572868
  119.9 9.6 %collective-permute-start.18 = (f32[1,128]{1,0:T(1,128)S(1)}, f32[1,128]{1,0:T(1,128)S(1)}, u32[]{:S(2)}, u32[]{:S(2)}) collective-permute-start(f32[1,128]{1,0:T(1,128)S(1)} %bitcast.39), channel_id=1, source_target_pairs={{0,64},{64,0},{1,65},{65,1},{2,66},{66,2},{3,67},{67,3},{4,68},{68... | collective-permute-start | bytes 1544 | tf_op jit(solution)/shard_map/ppermute | solution.py:276
  123.1 1.1 copy-start.11
  123.1 23.7 %collective-permute-start.21 = (f32[2,512,128]{2,1,0:T(8,128)}, f32[2,512,128]{2,1,0:T(8,128)S(1)}, u32[]{:S(2)}, u32[]{:S(2)}) collective-permute-start(f32[2,512,128]{2,1,0:T(8,128)} %get-tuple-element.96), channel_id=1, source_target_pairs={{0,48},{4,52},{8,56},{12,60},{16,0},{20,4},{24,8},{28,12},{32,16},... | collective-permute-start | bytes 1572872 | tf_op jit(solution)/shard_map/ppermute | solution.py:267
  129.4 26.0 %collective-permute-start.25 = (f32[2,512,128]{2,1,0:T(8,128)}, f32[2,512,128]{2,1,0:T(8,128)S(1)}, u32[]{:S(2)}, u32[]{:S(2)}) collective-permute-start(f32[2,512,128]{2,1,0:T(8,128)} %get-tuple-element.106), channel_id=1, source_target_pairs={{0,4},{4,8},{8,12},{12,0},{16,20},{20,24},{24,28},{28,16},{32,36},... | collective-permute-start | bytes 1572872 | tf_op jit(solution)/shard_map/ppermute | solution.py:267
  130.0 25.4 %collective-permute-start.26 = (f32[2,512,128]{2,1,0:T(8,128)}, f32[2,512,128]{2,1,0:T(8,128)S(1)}, u32[]{:S(2)}, u32[]{:S(2)}) collective-permute-start(f32[2,512,128]{2,1,0:T(8,128)} %get-tuple-element.107), channel_id=1, source_target_pairs={{0,8},{4,12},{8,0},{12,4},{16,24},{20,28},{24,16},{28,20},{32,40},... | collective-permute-start | bytes 1572872 | tf_op jit(solution)/shard_map/ppermute | solution.py:267
  143.9 2.9 %copy-start.12 = (f32[2,512,128]{2,1,0:T(8,128)}, f32[2,512,128]{2,1,0:T(8,128)S(1)}, u32[]{:S(2)}) copy-start(f32[2,512,128]{2,1,0:T(8,128)S(1)} %collective-permute-done.19.a1) | copy-start | bytes 1572868
  143.9 13.7 %collective-permute-start.27 = (f32[2,512,128]{2,1,0:T(8,128)}, f32[2,512,128]{2,1,0:T(8,128)S(1)}, u32[]{:S(2)}, u32[]{:S(2)}) collective-permute-start(f32[2,512,128]{2,1,0:T(8,128)} %get-tuple-element.108), channel_id=1, source_target_pairs={{0,12},{4,0},{8,4},{12,8},{16,28},{20,16},{24,20},{28,24},{32,44},... | collective-permute-start | bytes 1572872 | tf_op jit(solution)/shard_map/ppermute | solution.py:267
  145.1 1.7 copy-start.13
  145.1 19.5 %collective-permute-start.17 = (f32[2,256,128]{2,1,0:T(8,128)S(1)}, f32[2,256,128]{2,1,0:T(8,128)S(1)}, u32[]{:S(2)}, u32[]{:S(2)}) collective-permute-start(f32[2,256,128]{2,1,0:T(8,128)S(1)} %add.10), channel_id=1, source_target_pairs={{0,2},{2,0},{1,3},{3,1},{4,6},{6,4},{5,7},{7,5},{8,10},{10,8},{9,1... | collective-permute-start | bytes 786440 | tf_op jit(solution)/shard_map/ppermute | solution.py:273
  146.8 0.8 copy-start.14
  150.0 15.4 %collective-permute-start.22 = (f32[512,128]{1,0:T(8,128)}, f32[512,128]{1,0:T(8,128)S(1)}, u32[]{:S(2)}, u32[]{:S(2)}) collective-permute-start(f32[512,128]{1,0:T(8,128)} %get-tuple-element.98), channel_id=1, source_target_pairs={{0,64},{64,0},{1,65},{65,1},{2,66},{66,2},{3,67},{67,3},{4,68},{68... | collective-permute-start | bytes 786440 | tf_op jit(solution)/shard_map/ppermute | solution.py:276
  155.4 2.3 %copy-start.15 = (f32[2,512,128]{2,1,0:T(8,128)}, f32[2,512,128]{2,1,0:T(8,128)S(1)}, u32[]{:S(2)}) copy-start(f32[2,512,128]{2,1,0:T(8,128)S(1)} %collective-permute-done.25.a1) | copy-start | bytes 1572868
  155.4 2.3 %copy-start.16 = (f32[2,512,128]{2,1,0:T(8,128)}, f32[2,512,128]{2,1,0:T(8,128)S(1)}, u32[]{:S(2)}) copy-start(f32[2,512,128]{2,1,0:T(8,128)S(1)} %collective-permute-done.26.a2) | copy-start | bytes 1572868
  157.6 0.8 copy-start.17
  160.8 8.7 %collective-permute-start.28 = (f32[512,128]{1,0:T(8,128)}, f32[512,128]{1,0:T(8,128)S(1)}, u32[]{:S(2)}, u32[]{:S(2)}) collective-permute-start(f32[512,128]{1,0:T(8,128)} %get-tuple-element.110), channel_id=1, source_target_pairs={{0,64},{64,0},{1,65},{65,1},{2,66},{66,2},{3,67},{67,3},{4,68},{68... | collective-permute-start | bytes 786440 | tf_op jit(solution)/shard_map/ppermute | solution.py:276
  165.4 4.2 %copy-start.19 = (f32[512,128]{1,0:T(8,128)}, f32[512,128]{1,0:T(8,128)S(1)}, u32[]{:S(2)}) copy-start(f32[512,128]{1,0:T(8,128)S(1)} %collective-permute-done.22.a1) | copy-start | bytes 786436
  169.6 0.7 copy-start.20

commit v4 on v3

--- a/solution.py
+++ b/solution.py
@@ -49,25 +49,35 @@
     return x
 
 
-def prep_kernel(pos, d_ref, z1, z2, z3, x1, x2, x3, oz, ox):
+def piece_of(pos, d_ref):
     dp, x, z, core = pos[0], pos[1], pos[2], pos[3]
 
-    def column(d, xx, zz):
-        at = (d * SIDE + lax.rem(xx, SIDE)) * SIDE + lax.rem(zz, SIDE)
+    def column(d, dx, dz):
+        at = (d * SIDE + lax.rem(x + dx, SIDE)) * SIDE + lax.rem(z + dz, SIDE)
         return d_ref[:, pl.ds(pl.multiple_of(at * 128, 128), 128)]
 
-    mine = lax.rem(dp + core, 2)
-    for k, (zr, xr) in enumerate(((z1, x1), (z2, x2), (z3, x3)), 1):
+    return column, dp, lax.rem(dp + core, 2)
+
+
+def near_kernel(pos, d_ref, z1, z3, x1, x3):
+    column, _, mine = piece_of(pos, d_ref)
+    for k, zr, xr in ((1, z1, x1), (3, z3, x3)):
         for r in range(SIDE):
             cols = slice(r * 128, (r + 1) * 128)
-            zr[:, cols] = column(mine, x + r, z + k).astype(F32)
-            xr[:, cols] = column(mine, x + k, z + r).astype(F32)
-    for kd in range(2):
-        d = lax.rem(dp + kd, 2)
-        for r in range(SIDE):
-            cols = slice(r * 128, (r + 1) * 128)
-            oz[kd, :, cols] = column(d, x + r, z)
-            ox[kd, :, cols] = column(d, x, z + r)
+            zr[:, cols] = column(mine, r, k).astype(F32)
+            xr[:, cols] = column(mine, k, r).astype(F32)
+
+
+def far_kernel(pos, d_ref, z2, x2, oz, ox):
+    column, dp, mine = piece_of(pos, d_ref)
+    for r in range(SIDE):
+        cols = slice(r * 128, (r + 1) * 128)
+        z2[:, cols] = column(mine, r, 2).astype(F32)
+        x2[:, cols] = column(mine, 2, r).astype(F32)
+        for kd in range(2):
+            d = lax.rem(dp + kd, 2)
+            oz[kd, :, cols] = column(d, r, 0)
+            ox[kd, :, cols] = column(d, 0, r)
 
 
 def ends_kernel(ut_ref, v_ref, b_ref, c_ref, s_ref, r_ref, vt_ref, end_ref, run_ref, *, length):
@@ -286,12 +296,11 @@
 
     piece = sds((tokens, 4 * 128), F32)
     own = sds((2, tokens, 4 * 128), BF16)
-    z1, z2, z3, x1, x2, x3, own_z, own_x = call(
-        prep_kernel, (piece,) * 6 + (own, own), "prep", scalars=1, nbytes=7 << 20
-    )(pos, cot)
+    z1, z3, x1, x3 = call(near_kernel, (piece,) * 4, "near", scalars=1, nbytes=4 << 20)(pos, cot)
+    placed = later(cot, z1)
     z3, x3, z1, x1 = shift(z3, 0, 3), shift(x3, 3, 0), shift(z1, 0, 1), shift(x1, 1, 0)
 
-    up_t = lax.dot_general(w_out, later(cot, own_z), (((0,), (1,)), ((), ())), preferred_element_type=F32).astype(BF16)
+    up_t = lax.dot_general(w_out, placed, (((0,), (1,)), ((), ())), preferred_element_type=F32).astype(BF16)
     vt, ends, run = call(
         functools.partial(ends_kernel, length=length),
         (sds((channels, tokens), BF16), sds((heads, 2 * width + 8, state), F32), sds((heads, tokens), F32)),
@@ -299,7 +308,10 @@
         nbytes=4 << 20,
         flops=1 << 27,
     )(up_t, v, b, c, steps, rates)
-    z2, x2 = shift(later(z2, run), 0, 2), shift(later(x2, run), 2, 0)
+    z2, x2, own_z, own_x = call(far_kernel, (piece, piece, own, own), "far", scalars=1, nbytes=5 << 20)(
+        pos, later(cot, run)
+    )
+    z2, x2 = shift(z2, 0, 2), shift(x2, 2, 0)
     ends = later(ends, z1, z3, x1, x3)
     across = call(across_kernel, sds((shards, 2 * width, state), F32), "across", nbytes=2 << 20)(spread(ends))
     states = spread(across)

time: 173 us -> 167 us (0.965)
  starting transfers between devices: 65.1 us -> 57 us
  Pallas kernels: 45.6 us -> 47.9 us
    all_to_all x3, starting transfers between devices: 22.9 us -> 14.5 us  [spread(): return lax.all_to_all(value, 'ctx', 0, 0, tiled=True)]
    all_to_all x3, waiting for transfers between devices: 23.3 us -> 20.4 us  [spread(): return lax.all_to_all(value, 'ctx', 0, 0, tiled=True)]
    ppermute x18, waiting for transfers between devices: 16.6 us -> 19.3 us  [shift(): return lax.ppermute(value, 'ctx', pairs)]
    pallas_call x11 -> x12, Pallas kernels: 45.6 us -> 47.9 us  [run(): pl.pallas_call(kernel, out_shape=outs, in_specs=specs, out_specs=jax.tree...]
  transfers between devices with their start and end apart: 32 -> 32, of which waited for: 7 -> 8; matrix products, arithmetic and copies ran while one was open for 6% -> 7% of each run, Pallas kernels for 23% -> 26%
where the time goes in v4:
time: 167 us; the launch traced here: 166 us
  starting transfers between devices  57 us (34%)
  Pallas kernels  47.9 us (29%)
  waiting for transfers between devices  43.9 us (26%)
  local copies, waits for them, and re-layouts  8.43 us (5%)
  matrix products  7.53 us (5%)
    pallas_call x12, Pallas kernels, run(): pl.pallas_call(kernel, out_shape=outs, in_specs=specs, out_specs=jax.tree...  47.9 us
    ppermute x18, starting transfers between devices, shift(): return lax.ppermute(value, 'ctx', pairs)  30 us
    all_to_all x3, waiting for transfers between devices, spread(): return lax.all_to_all(value, 'ctx', 0, 0, tiled=True)  20.4 us
    ppermute x18, waiting for transfers between devices, shift(): return lax.ppermute(value, 'ctx', pairs)  19.3 us
    all_to_all x3, starting transfers between devices, spread(): return lax.all_to_all(value, 'ctx', 0, 0, tiled=True)  14.5 us
    ppermute x3, starting transfers between devices, other_dp(): return lax.ppermute(value, 'dp', [(0, 1), (1, 0)])  9.3 us
    dot_general x1, matrix products, body(): lax.dot_general(w_out, placed, (((0,), (1,)), ((), ())), preferred_elemen...  7.53 us
    unnamed x44, local copies, waits for them, and re-layouts  5.15 us
  transfers between devices with their start and end apart: 32, of which 8 were waited for; matrix products, arithmetic and copies ran while one was open for 7% of the time, Pallas kernels for 26%

profile of v4, /device:TPU:0, one launch (start us, length us, event | category | flops | bytes accessed | tf_op | source)
XLA Modules:
  0.0 166.4 jit_solution(8421940145897258548)
XLA Ops:
  0.6 0.0 copy-start
  0.7 0.7 pad_add_fusion.pos
  1.3 3.2 %near.1 = (f32[256,512]{1,0:T(8,128)}, f32[256,512]{1,0:T(8,128)}, f32[256,512]{1,0:T(8,128)}, f32[256,512]{1,0:T(8,128)}) custom-call(s32[4]{0:T(128)} %pad_add_fusion.pos, bf16[256,4096]{1,0:T(8,128)(2,1)} %bitcast.24), custom_call_target="tpu_custom_call" | custom-call | bytes 4194304 | tf_op jit(solution)/shard_map/near/pallas_call | solution.py:25
  4.5 4.1 %collective-permute-start.1 = (f32[256,512]{1,0:T(8,128)}, f32[256,512]{1,0:T(8,128)}, u32[]{:S(2)}, u32[]{:S(2)}) collective-permute-start(f32[256,512]{1,0:T(8,128)} %get-tuple-element.63), channel_id=1, source_target_pairs={{0,12},{4,0},{8,4},{12,8},{16,28},{20,16},{24,20},{28,24},{32,44},... | collective-permute-start | bytes 1572872 | tf_op jit(solution)/shard_map/ppermute | solution.py:277
  8.7 1.5 collective-permute-start.2
  10.1 1.8 %collective-permute-start.3 = (f32[256,512]{1,0:T(8,128)}, f32[256,512]{1,0:T(8,128)S(1)}, u32[]{:S(2)}, u32[]{:S(2)}) collective-permute-start(f32[256,512]{1,0:T(8,128)} %get-tuple-element.65), channel_id=1, source_target_pairs={{0,48},{4,52},{8,56},{12,60},{16,0},{20,4},{24,8},{28,12},{32,16},... | collective-permute-start | bytes 1572872 | tf_op jit(solution)/shard_map/ppermute | solution.py:277
  11.9 0.7 copy.22.r_ref
  12.6 7.5 %fusion.ut_ref = bf16[1024,256]{1,0:T(8,128)(2,1)} fusion(bf16[256,4096]{1,0:T(8,128)(2,1)S(1)} %bitcast.26, bf16[4096,1024]{1,0:T(8,128)(2,1)} %param.14), kind=kOutput, calls=%fused_computation.1 | convolution fusion | flops 2147745792 | bytes 11010048 | tf_op jit(solution)/shard_map/dot_general | solution.py:303
  20.1 3.4 %ends.1 = (bf16[1024,256]{1,0:T(8,128)(2,1)}, f32[16,136,128]{2,1,0:T(8,128)}, f32[16,256]{1,0:T(8,128)}) custom-call(bf16[1024,256]{1,0:T(8,128)(2,1)} %fusion.ut_ref, bf16[256,1024]{1,0:T(8,128)(2,1)} %bitcast.31, bf16[256,128]{1,0:T(8,128)(2,1)} %bitcast.32, bf16[256,128]{1,0:T(8,128)(2,1)} %bitcast.27, f32[16,256]{1,0:T(8,128)} %bitcast.35, ...), custom_call_target="tpu_custom_call" | custom-call | flops 134217728 | bytes 4194304 | tf_op jit(solution)/shard_map/ends/pallas_call | solution.py:25
  23.6 2.6 %collective-permute-done.d1 = f32[256,512]{1,0:T(8,128)} collective-permute-done((f32[256,512]{1,0:T(8,128)}, f32[256,512]{1,0:T(8,128)}, u32[]{:S(2)}, u32[]{:S(2)}) %collective-permute-start) | collective-permute-done | bytes 524320 | tf_op jit(solution)/shard_map/ppermute | solution.py:277
  26.3 3.7 %all-to-all-start = ((f32[16,136,128]{2,1,0:T(8,128)}), f32[16,136,128]{2,1,0:T(8,128)S(1)}, u32[]{:S(2)}, u32[]{:S(2)}) async-start(f32[16,136,128]{2,1,0:T(8,128)} %get-tuple-element.66), calls=%async_computation | async-start | bytes 2228224 | tf_op jit(solution)/shard_map/all_to_all | solution.py:289
  30.0 3.3 %far.1 = (f32[256,512]{1,0:T(8,128)}, f32[256,512]{1,0:T(8,128)}, bf16[2,256,512]{2,1,0:T(8,128)(2,1)}, bf16[2,256,512]{2,1,0:T(8,128)(2,1)}) custom-call(s32[4]{0:T(128)} %pad_add_fusion.pos, bf16[256,4096]{1,0:T(8,128)(2,1)} %bitcast.25), custom_call_target="tpu_custom_call" | custom-call | bytes 5242880 | tf_op jit(solution)/shard_map/far/pallas_call | solution.py:25
  33.3 3.3 %collective-permute-start.4 = (f32[256,512]{1,0:T(8,128)}, f32[256,512]{1,0:T(8,128)}, u32[]{:S(2)}, u32[]{:S(2)}) collective-permute-start(f32[256,512]{1,0:T(8,128)} %get-tuple-element.71), channel_id=1, source_target_pairs={{0,8},{4,12},{8,0},{12,4},{16,24},{20,28},{24,16},{28,20},{32,40},... | collective-permute-start | bytes 1572872 | tf_op jit(solution)/shard_map/ppermute | solution.py:277
  36.6 3.0 %collective-permute-start.5 = (f32[256,512]{1,0:T(8,128)}, f32[256,512]{1,0:T(8,128)S(1)}, u32[]{:S(2)}, u32[]{:S(2)}) collective-permute-start(f32[256,512]{1,0:T(8,128)} %get-tuple-element.72), channel_id=1, source_target_pairs={{0,32},{4,36},{8,40},{12,44},{16,48},{20,52},{24,56},{28,60},{32,0... | collective-permute-start | bytes 1572872 | tf_op jit(solution)/shard_map/ppermute | solution.py:277
  39.6 9.1 %all-to-all-done.e_ref = f32[16,136,128]{2,1,0:T(8,128)S(1)} async-done(((f32[16,136,128]{2,1,0:T(8,128)}), f32[16,136,128]{2,1,0:T(8,128)S(1)}, u32[]{:S(2)}, u32[]{:S(2)}) %all-to-all-start) | async-done | bytes 1114144 | tf_op jit(solution)/shard_map/all_to_all | solution.py:289
  48.8 1.0 copy-done.1
  49.8 2.4 %across.1 = f32[16,128,128]{2,1,0:T(8,128)} custom-call(f32[16,136,128]{2,1,0:T(8,128)} %copy-done.1), custom_call_target="tpu_custom_call" | custom-call | bytes 2097152 | tf_op jit(solution)/shard_map/across/pallas_call | solution.py:25
  52.1 4.3 %all-to-all-start.1 = ((f32[16,128,128]{2,1,0:T(8,128)}), f32[16,128,128]{2,1,0:T(8,128)S(1)}, u32[]{:S(2)}, u32[]{:S(2)}) async-start(f32[16,128,128]{2,1,0:T(8,128)} %across.1), calls=%async_computation.1 | async-start | bytes 2097152 | tf_op jit(solution)/shard_map/all_to_all | solution.py:289
  56.4 4.7 %inside.1.in_ref = f32[1024,256]{1,0:T(8,128)} custom-call(f32[16]{0:T(128)} %g_ref.3, bf16[1024,256]{1,0:T(8,128)(2,1)} %get-tuple-element.60.vt_ref, bf16[256,128]{1,0:T(8,128)(2,1)} %bitcast.33, bf16[256,128]{1,0:T(8,128)(2,1)} %bitcast.28, f32[16,256]{1,0:T(8,128)} %bitcast.36, f32[16,256]{1,0:T(8,128)} %get-tuple-element.67.run_ref), custom_call_target="tpu_custom_call" | custom-call | flops 268435456 | bytes 4194304 | tf_op jit(solution)/shard_map/inside/pallas_call | solution.py:25
  61.1 0.1 collective-permute-start.6
  61.2 0.5 collective-permute-start.7
  61.7 0.1 collective-permute-start.8
  61.8 0.4 collective-permute-start.9
  62.3 0.1 collective-permute-start.10
  62.4 7.2 %all-to-all-done.1.st_ref = f32[16,128,128]{2,1,0:T(8,128)S(1)} async-done(((f32[16,128,128]{2,1,0:T(8,128)}), f32[16,128,128]{2,1,0:T(8,128)S(1)}, u32[]{:S(2)}, u32[]{:S(2)}) %all-to-all-start.1) | async-done | bytes 1048608 | tf_op jit(solution)/shard_map/all_to_all | solution.py:289
  69.6 1.0 copy-done.2
  70.6 2.9 %mix.1 = (f32[512,256]{1,0:T(8,128)}, f32[512,256]{1,0:T(8,128)}) custom-call(f32[1024,256]{1,0:T(8,128)} %inside.1.in_ref, bf16[256,128]{1,0:T(8,128)(2,1)} %bitcast.29, f32[16,256]{1,0:T(8,128)} %get-tuple-element.67.run_ref, f32[16,128,128]{2,1,0:T(8,128)} %copy-done.2), custom_call_target="tpu_custom_call" | custom-call | flops 134217728 | bytes 4194304 | tf_op jit(solution)/shard_map/mix/pallas_call | solution.py:25
  73.6 1.5 collective-permute-start.12
  75.0 0.6 collective-permute-start.11
  75.7 0.9 collective-permute-start.15
  76.5 1.7 %collective-permute-start.14 = (f32[512,256]{1,0:T(8,128)}, f32[512,256]{1,0:T(8,128)}, u32[]{:S(2)}, u32[]{:S(2)}) collective-permute-start(f32[512,256]{1,0:T(8,128)} %get-tuple-element.84.ma_ref.m0), channel_id=1, source_target_pairs={{0,8},{4,12},{8,0},{12,4},{16,24},{20,28},{24,16},{28,20},{32,40},... | collective-permute-start | bytes 1572872 | tf_op jit(solution)/shard_map/ppermute | solution.py:277
  78.3 0.4 collective-permute-start.13
  78.7 10.4 %back.1 = (bf16[256,1024]{1,0:T(8,128)(2,1)}, f32[2,256,128]{2,1,0:T(8,128)}, f32[16,256]{1,0:T(8,128)}, f32[1,128]{1,0:T(1,128)}) custom-call(f32[16]{0:T(128)} %g_ref.3, bf16[1024,256]{1,0:T(8,128)(2,1)} %fusion.ut_ref, bf16[1024,256]{1,0:T(8,128)(2,1)} %get-tuple-element.60.vt_ref, bf16[256,128]{1,0:T(8,128)(2,1)} %bitcast.34, bf16[256,128]{1,0:T(8,128)(2,1)} %bitcast.30, ...), custom_call_target="tpu_custom_call" | custom-call | flops 1073741824 | bytes 6291456 | tf_op jit(solution)/shard_map/back/pallas_call | solution.py:25
  89.1 1.3 broadcast_in_dim.21
  90.4 6.6 %all-to-all-start.2 = ((f32[16,1,128]{2,1,0:T(1,128)}), f32[16,1,128]{2,1,0:T(1,128)S(1)}, u32[]{:S(2)}, u32[]{:S(2)}) async-start(f32[16,1,128]{2,1,0:T(1,128)} %broadcast_in_dim.21), calls=%async_computation.2 | async-start | bytes 16384 | tf_op jit(solution)/shard_map/all_to_all | solution.py:289
  97.0 3.5 %collective-permute-start.23 = (f32[512,256]{1,0:T(8,128)S(1)}, f32[512,256]{1,0:T(8,128)S(1)}, u32[]{:S(2)}, u32[]{:S(2)}) collective-permute-start(f32[512,256]{1,0:T(8,128)S(1)} %copy-done.6), channel_id=1, source_target_pairs={{0,32},{4,36},{8,40},{12,44},{16,48},{20,52},{24,56},{28,60},{32,0... | collective-permute-start | bytes 1572872 | tf_op jit(solution)/shard_map/ppermute | solution.py:277
  100.5 4.1 %all-to-all-done.2 = f32[16,1,128]{2,1,0:T(1,128)S(1)} async-done(((f32[16,1,128]{2,1,0:T(1,128)}), f32[16,1,128]{2,1,0:T(1,128)S(1)}, u32[]{:S(2)}, u32[]{:S(2)}) %all-to-all-start.2) | async-done | bytes 8224 | tf_op jit(solution)/shard_map/all_to_all | solution.py:289
  104.6 0.1 collective-permute-start.24
  104.7 0.8 copy-done.10
  105.5 5.3 %grad_w_a.1 = (f32[2,512,128]{2,1,0:T(8,128)}, f32[2,512,128]{2,1,0:T(8,128)}, f32[2,512,128]{2,1,0:T(8,128)}, f32[2,512,128]{2,1,0:T(8,128)}) custom-call(s32[1]{0:T(128)} %bitcast.4.core, f32[512,256]{1,0:T(8,128)} %get-tuple-element.84.ma_ref.m0, f32[512,256]{1,0:T(8,128)} %collective-permute-done.13.m1, f32[512,256]{1,0:T(8,128)} %collective-permute-done.14.m2, ...), custom_call_target="tpu_custom_call" | custom-call | flops 1073741824 | bytes 8388608 | tf_op jit(solution)/shard_map/grad_w_a/pallas_call | solution.py:25
  110.9 0.6 collective-permute-start.19
  111.5 0.2 collective-permute-start.16
  111.7 2.1 %collective-permute-start.20 = (f32[2,512,128]{2,1,0:T(8,128)}, f32[2,512,128]{2,1,0:T(8,128)S(1)}, u32[]{:S(2)}, u32[]{:S(2)}) collective-permute-start(f32[2,512,128]{2,1,0:T(8,128)} %get-tuple-element.93), channel_id=1, source_target_pairs={{0,32},{4,36},{8,40},{12,44},{16,48},{20,52},{24,56},{28,60},{32,0... | collective-permute-start | bytes 1572872 | tf_op jit(solution)/shard_map/ppermute | solution.py:277
  113.8 3.2 %collective-permute-start.18 = (f32[1,128]{1,0:T(1,128)S(1)}, f32[1,128]{1,0:T(1,128)S(1)}, u32[]{:S(2)}, u32[]{:S(2)}) collective-permute-start(f32[1,128]{1,0:T(1,128)S(1)} %bitcast.40), channel_id=1, source_target_pairs={{0,64},{64,0},{1,65},{65,1},{2,66},{66,2},{3,67},{67,3},{4,68},{68... | collective-permute-start | bytes 1544 | tf_op jit(solution)/shard_map/ppermute | solution.py:286
  117.0 1.2 collective-permute-start.21
  118.1 5.2 %grad_w_b.1 = (f32[2,512,128]{2,1,0:T(8,128)}, f32[2,512,128]{2,1,0:T(8,128)}, f32[2,512,128]{2,1,0:T(8,128)}, f32[2,512,128]{2,1,0:T(8,128)}) custom-call(s32[1]{0:T(128)} %bitcast.4.core, f32[512,256]{1,0:T(8,128)} %get-tuple-element.98.mb_ref.m0, f32[512,256]{1,0:T(8,128)} %copy-done.8, f32[512,256]{1,0:T(8,128)} %copy-done.9, f32[512,256]{1,0:T(8,128)} %copy-done.7, ...), custom_call_target="tpu_custom_call" | custom-call | flops 1073741824 | bytes 8388608 | tf_op jit(solution)/shard_map/grad_w_b/pallas_call | solution.py:25
  123.4 0.6 collective-permute-start.25
  123.9 2.1 %collective-permute-start.26 = (f32[2,512,128]{2,1,0:T(8,128)}, f32[2,512,128]{2,1,0:T(8,128)S(1)}, u32[]{:S(2)}, u32[]{:S(2)}) collective-permute-start(f32[2,512,128]{2,1,0:T(8,128)} %get-tuple-element.105), channel_id=1, source_target_pairs={{0,8},{4,12},{8,0},{12,4},{16,24},{20,28},{24,16},{28,20},{32,40},... | collective-permute-start | bytes 1572872 | tf_op jit(solution)/shard_map/ppermute | solution.py:277
  126.0 11.9 %collective-permute-done.19.a1 = f32[2,512,128]{2,1,0:T(8,128)S(1)} collective-permute-done((f32[2,512,128]{2,1,0:T(8,128)}, f32[2,512,128]{2,1,0:T(8,128)S(1)}, u32[]{:S(2)}, u32[]{:S(2)}) %collective-permute-start.19) | collective-permute-done | bytes 524320 | tf_op jit(solution)/shard_map/ppermute | solution.py:277
  137.9 1.2 collective-permute-start.27
  139.1 1.7 collective-permute-start.17
  140.8 0.8 copy-done.14
  141.6 2.4 %gather_sum_a.1 = (f32[512,128]{1,0:T(8,128)}, f32[512,128]{1,0:T(8,128)}) custom-call(f32[2,512,128]{2,1,0:T(8,128)} %get-tuple-element.89.a0, f32[2,512,128]{2,1,0:T(8,128)} %copy-done.12, f32[2,512,128]{2,1,0:T(8,128)} %copy-done.13, f32[2,512,128]{2,1,0:T(8,128)} %copy-done.14), custom_call_target="tpu_custom_call" | custom-call | bytes 3145728 | tf_op jit(solution)/shard_map/gather_sum_a/pallas_call | solution.py:25
  144.0 2.9 %collective-permute-start.22 = (f32[512,128]{1,0:T(8,128)}, f32[512,128]{1,0:T(8,128)S(1)}, u32[]{:S(2)}, u32[]{:S(2)}) collective-permute-start(f32[512,128]{1,0:T(8,128)} %get-tuple-element.96), channel_id=1, source_target_pairs={{0,64},{64,0},{1,65},{65,1},{2,66},{66,2},{3,67},{67,3},{4,68},{68... | collective-permute-start | bytes 786440 | tf_op jit(solution)/shard_map/ppermute | solution.py:286
  146.9 2.4 %collective-permute-done.25.a1 = f32[2,512,128]{2,1,0:T(8,128)S(1)} collective-permute-done((f32[2,512,128]{2,1,0:T(8,128)}, f32[2,512,128]{2,1,0:T(8,128)S(1)}, u32[]{:S(2)}, u32[]{:S(2)}) %collective-permute-start.25) | collective-permute-done | bytes 524320 | tf_op jit(solution)/shard_map/ppermute | solution.py:277
  149.3 2.3 %collective-permute-done.27.a3 = f32[2,512,128]{2,1,0:T(8,128)S(1)} collective-permute-done((f32[2,512,128]{2,1,0:T(8,128)}, f32[2,512,128]{2,1,0:T(8,128)S(1)}, u32[]{:S(2)}, u32[]{:S(2)}) %collective-permute-start.27) | collective-permute-done | bytes 524320 | tf_op jit(solution)/shard_map/ppermute | solution.py:277
  151.7 0.8 copy-done.17
  152.4 2.4 %gather_sum_b.1 = (f32[512,128]{1,0:T(8,128)}, f32[512,128]{1,0:T(8,128)}) custom-call(f32[2,512,128]{2,1,0:T(8,128)} %get-tuple-element.103.a0, f32[2,512,128]{2,1,0:T(8,128)} %copy-done.15, f32[2,512,128]{2,1,0:T(8,128)} %copy-done.16, f32[2,512,128]{2,1,0:T(8,128)} %copy-done.17), custom_call_target="tpu_custom_call" | custom-call | bytes 3145728 | tf_op jit(solution)/shard_map/gather_sum_b/pallas_call | solution.py:25
  154.8 3.2 %collective-permute-start.28 = (f32[512,128]{1,0:T(8,128)}, f32[512,128]{1,0:T(8,128)S(1)}, u32[]{:S(2)}, u32[]{:S(2)}) collective-permute-start(f32[512,128]{1,0:T(8,128)} %get-tuple-element.108), channel_id=1, source_target_pairs={{0,64},{64,0},{1,65},{65,1},{2,66},{66,2},{3,67},{67,3},{4,68},{68... | collective-permute-start | bytes 786440 | tf_op jit(solution)/shard_map/ppermute | solution.py:286
  158.0 0.6 slice_bitcast_fusion
  158.6 0.7 fusion.1
  159.3 4.2 %collective-permute-done.28.b1 = f32[512,128]{1,0:T(8,128)S(1)} collective-permute-done((f32[512,128]{1,0:T(8,128)}, f32[512,128]{1,0:T(8,128)S(1)}, u32[]{:S(2)}, u32[]{:S(2)}) %collective-permute-start.28) | collective-permute-done | bytes 262176 | tf_op jit(solution)/shard_map/ppermute | solution.py:286
  163.6 0.7 copy-done.20
  164.3 2.2 %finish.1 = f32[128,1024]{1,0:T(8,128)} custom-call(f32[512,128]{1,0:T(8,128)} %get-tuple-element.95.a0, f32[512,128]{1,0:T(8,128)} %copy-done.19, f32[512,128]{1,0:T(8,128)} %get-tuple-element.107.b0, f32[512,128]{1,0:T(8,128)} %copy-done.20), custom_call_target="tpu_custom_call" | custom-call | bytes 2097152 | tf_op jit(solution)/shard_map/finish/pallas_call | solution.py:25
  (66 shorter events, 0.2 us)
Async XLA Ops:
  0.6 12.0 %copy-start = (bf16[1,256,4096]{2,1,0:T(8,128)(2,1)S(1)}, bf16[1,256,4096]{2,1,0:T(8,128)(2,1)}, u32[]{:S(2)}) copy-start(bf16[1,256,4096]{2,1,0:T(8,128)(2,1)} %param.15) | copy-start | bytes 6291460
  0.6 11.3 %copy-start.21 = (f32[16]{0:T(128)S(1)}, f32[16]{0:T(128)}, u32[]{:S(2)}) copy-start(f32[16]{0:T(128)} %param.12) | copy-start | bytes 196
  4.5 19.0 %collective-permute-start.1 = (f32[256,512]{1,0:T(8,128)}, f32[256,512]{1,0:T(8,128)}, u32[]{:S(2)}, u32[]{:S(2)}) collective-permute-start(f32[256,512]{1,0:T(8,128)} %get-tuple-element.63), channel_id=1, source_target_pairs={{0,12},{4,0},{8,4},{12,8},{16,28},{20,16},{24,20},{28,24},{32,44},... | collective-permute-start | bytes 1572872 | tf_op jit(solution)/shard_map/ppermute | solution.py:277
  8.7 14.9 %collective-permute-start.2 = (f32[256,512]{1,0:T(8,128)}, f32[256,512]{1,0:T(8,128)S(1)}, u32[]{:S(2)}, u32[]{:S(2)}) collective-permute-start(f32[256,512]{1,0:T(8,128)} %get-tuple-element.64), channel_id=1, source_target_pairs={{0,16},{4,20},{8,24},{12,28},{16,32},{20,36},{24,40},{28,44},{32,4... | collective-permute-start | bytes 1572872 | tf_op jit(solution)/shard_map/ppermute | solution.py:277
  10.1 13.5 %collective-permute-start.3 = (f32[256,512]{1,0:T(8,128)}, f32[256,512]{1,0:T(8,128)S(1)}, u32[]{:S(2)}, u32[]{:S(2)}) collective-permute-start(f32[256,512]{1,0:T(8,128)} %get-tuple-element.65), channel_id=1, source_target_pairs={{0,48},{4,52},{8,56},{12,60},{16,0},{20,4},{24,8},{28,12},{32,16},... | collective-permute-start | bytes 1572872 | tf_op jit(solution)/shard_map/ppermute | solution.py:277
  11.9 14.3 %collective-permute-start = (f32[256,512]{1,0:T(8,128)}, f32[256,512]{1,0:T(8,128)}, u32[]{:S(2)}, u32[]{:S(2)}) collective-permute-start(f32[256,512]{1,0:T(8,128)} %get-tuple-element.58), channel_id=1, source_target_pairs={{0,4},{4,8},{8,12},{12,0},{16,20},{20,24},{24,28},{28,16},{32,36},... | collective-permute-start | bytes 1572872 | tf_op jit(solution)/shard_map/ppermute | solution.py:277
  23.6 38.3 %copy-start.3 = (f32[256,512]{1,0:T(8,128)}, f32[256,512]{1,0:T(8,128)S(1)}, u32[]{:S(2)}) copy-start(f32[256,512]{1,0:T(8,128)S(1)} %collective-permute-done.2.d1) | copy-start | bytes 1572868
  23.6 38.7 %copy-start.4 = (f32[256,512]{1,0:T(8,128)}, f32[256,512]{1,0:T(8,128)S(1)}, u32[]{:S(2)}) copy-start(f32[256,512]{1,0:T(8,128)S(1)} %collective-permute-done.3.d3) | copy-start | bytes 1572868
  26.3 22.5 %all-to-all-start = ((f32[16,136,128]{2,1,0:T(8,128)}), f32[16,136,128]{2,1,0:T(8,128)S(1)}, u32[]{:S(2)}, u32[]{:S(2)}) async-start(f32[16,136,128]{2,1,0:T(8,128)} %get-tuple-element.66), calls=%async_computation | async-start | bytes 2228224 | tf_op jit(solution)/shard_map/all_to_all | solution.py:289
  33.3 27.8 %collective-permute-start.4 = (f32[256,512]{1,0:T(8,128)}, f32[256,512]{1,0:T(8,128)}, u32[]{:S(2)}, u32[]{:S(2)}) collective-permute-start(f32[256,512]{1,0:T(8,128)} %get-tuple-element.71), channel_id=1, source_target_pairs={{0,8},{4,12},{8,0},{12,4},{16,24},{20,28},{24,16},{28,20},{32,40},... | collective-permute-start | bytes 1572872 | tf_op jit(solution)/shard_map/ppermute | solution.py:277
  36.6 24.5 %collective-permute-start.5 = (f32[256,512]{1,0:T(8,128)}, f32[256,512]{1,0:T(8,128)S(1)}, u32[]{:S(2)}, u32[]{:S(2)}) collective-permute-start(f32[256,512]{1,0:T(8,128)} %get-tuple-element.72), channel_id=1, source_target_pairs={{0,32},{4,36},{8,40},{12,44},{16,48},{20,52},{24,56},{28,60},{32,0... | collective-permute-start | bytes 1572872 | tf_op jit(solution)/shard_map/ppermute | solution.py:277
  48.8 1.0 copy-start.1
  52.1 17.4 %all-to-all-start.1 = ((f32[16,128,128]{2,1,0:T(8,128)}), f32[16,128,128]{2,1,0:T(8,128)S(1)}, u32[]{:S(2)}, u32[]{:S(2)}) async-start(f32[16,128,128]{2,1,0:T(8,128)} %across.1), calls=%async_computation.1 | async-start | bytes 2097152 | tf_op jit(solution)/shard_map/all_to_all | solution.py:289
  61.1 57.0 %copy-start.5 = (f32[256,512]{1,0:T(8,128)}, f32[256,512]{1,0:T(8,128)S(1)}, u32[]{:S(2)}) copy-start(f32[256,512]{1,0:T(8,128)S(1)} %collective-permute-done.5.d2) | copy-start | bytes 1572868
  61.1 12.4 %collective-permute-start.6 = (f32[256,512]{1,0:T(8,128)}, f32[256,512]{1,0:T(8,128)}, u32[]{:S(2)}, u32[]{:S(2)}) collective-permute-start(f32[256,512]{1,0:T(8,128)} %collective-permute-done.d1), channel_id=1, source_target_pairs={{0,1},{1,0},{2,3},{3,2},{4,5},{5,4},{6,7},{7,6},{8,9},{9,8},{10,11... | collective-permute-start | bytes 1572872 | tf_op jit(solution)/shard_map/ppermute | solution.py:280
  61.2 12.3 %collective-permute-start.7 = (f32[256,512]{1,0:T(8,128)}, f32[256,512]{1,0:T(8,128)}, u32[]{:S(2)}, u32[]{:S(2)}) collective-permute-start(f32[256,512]{1,0:T(8,128)} %collective-permute-done.4.d2), channel_id=1, source_target_pairs={{0,1},{1,0},{2,3},{3,2},{4,5},{5,4},{6,7},{7,6},{8,9},{9,8},{10,11... | collective-permute-start | bytes 1572872 | tf_op jit(solution)/shard_map/ppermute | solution.py:280
  61.7 11.8 %collective-permute-start.8 = (f32[256,512]{1,0:T(8,128)}, f32[256,512]{1,0:T(8,128)}, u32[]{:S(2)}, u32[]{:S(2)}) collective-permute-start(f32[256,512]{1,0:T(8,128)} %collective-permute-done.1.d3), channel_id=1, source_target_pairs={{0,1},{1,0},{2,3},{3,2},{4,5},{5,4},{6,7},{7,6},{8,9},{9,8},{10,11... | collective-permute-start | bytes 1572872 | tf_op jit(solution)/shard_map/ppermute | solution.py:280
  61.8 11.7 %collective-permute-start.9 = (f32[256,512]{1,0:T(8,128)S(1)}, f32[256,512]{1,0:T(8,128)}, u32[]{:S(2)}, u32[]{:S(2)}) collective-permute-start(f32[256,512]{1,0:T(8,128)S(1)} %collective-permute-done.2.d1), channel_id=1, source_target_pairs={{0,1},{1,0},{2,3},{3,2},{4,5},{5,4},{6,7},{7,6},{8,9},{9,8},{10,11... | collective-permute-start | bytes 1572872 | tf_op jit(solution)/shard_map/ppermute | solution.py:280
  62.3 11.3 %collective-permute-start.10 = (f32[256,512]{1,0:T(8,128)S(1)}, f32[256,512]{1,0:T(8,128)}, u32[]{:S(2)}, u32[]{:S(2)}) collective-permute-start(f32[256,512]{1,0:T(8,128)S(1)} %collective-permute-done.3.d3), channel_id=1, source_target_pairs={{0,1},{1,0},{2,3},{3,2},{4,5},{5,4},{6,7},{7,6},{8,9},{9,8},{10,11... | collective-permute-start | bytes 1572872 | tf_op jit(solution)/shard_map/ppermute | solution.py:280
  69.6 1.0 copy-start.2
  73.5 23.5 %copy-start.6 = (f32[512,256]{1,0:T(8,128)S(1)}, f32[512,256]{1,0:T(8,128)}, u32[]{:S(2)}) copy-start(f32[512,256]{1,0:T(8,128)} %get-tuple-element.98.mb_ref.m0) | copy-start | bytes 1572868
  73.6 15.5 %collective-permute-start.12 = (f32[512,256]{1,0:T(8,128)}, f32[512,256]{1,0:T(8,128)S(1)}, u32[]{:S(2)}, u32[]{:S(2)}) collective-permute-start(f32[512,256]{1,0:T(8,128)} %get-tuple-element.98.mb_ref.m0), channel_id=1, source_target_pairs={{0,48},{4,52},{8,56},{12,60},{16,0},{20,4},{24,8},{28,12},{32,16},... | collective-permute-start | bytes 1572872 | tf_op jit(solution)/shard_map/ppermute | solution.py:277
  75.0 14.1 %collective-permute-start.11 = (f32[512,256]{1,0:T(8,128)}, f32[512,256]{1,0:T(8,128)S(1)}, u32[]{:S(2)}, u32[]{:S(2)}) collective-permute-start(f32[512,256]{1,0:T(8,128)} %get-tuple-element.98.mb_ref.m0), channel_id=1, source_target_pairs={{0,16},{4,20},{8,24},{12,28},{16,32},{20,36},{24,40},{28,44},{32,4... | collective-permute-start | bytes 1572872 | tf_op jit(solution)/shard_map/ppermute | solution.py:277
  75.7 29.0 %collective-permute-start.15 = (f32[512,256]{1,0:T(8,128)}, f32[512,256]{1,0:T(8,128)S(1)}, u32[]{:S(2)}, u32[]{:S(2)}) collective-permute-start(f32[512,256]{1,0:T(8,128)} %get-tuple-element.84.ma_ref.m0), channel_id=1, source_target_pairs={{0,12},{4,0},{8,4},{12,8},{16,28},{20,16},{24,20},{28,24},{32,44},... | collective-permute-start | bytes 1572872 | tf_op jit(solution)/shard_map/ppermute | solution.py:277
  76.5 28.2 %collective-permute-start.14 = (f32[512,256]{1,0:T(8,128)}, f32[512,256]{1,0:T(8,128)}, u32[]{:S(2)}, u32[]{:S(2)}) collective-permute-start(f32[512,256]{1,0:T(8,128)} %get-tuple-element.84.ma_ref.m0), channel_id=1, source_target_pairs={{0,8},{4,12},{8,0},{12,4},{16,24},{20,28},{24,16},{28,20},{32,40},... | collective-permute-start | bytes 1572872 | tf_op jit(solution)/shard_map/ppermute | solution.py:277
  78.3 26.4 %collective-permute-start.13 = (f32[512,256]{1,0:T(8,128)}, f32[512,256]{1,0:T(8,128)}, u32[]{:S(2)}, u32[]{:S(2)}) collective-permute-start(f32[512,256]{1,0:T(8,128)} %get-tuple-element.84.ma_ref.m0), channel_id=1, source_target_pairs={{0,4},{4,8},{8,12},{12,0},{16,20},{20,24},{24,28},{28,16},{32,36},... | collective-permute-start | bytes 1572872 | tf_op jit(solution)/shard_map/ppermute | solution.py:277
  89.1 21.8 %copy-start.7 = (f32[512,256]{1,0:T(8,128)}, f32[512,256]{1,0:T(8,128)S(1)}, u32[]{:S(2)}) copy-start(f32[512,256]{1,0:T(8,128)S(1)} %collective-permute-done.12.m3) | copy-start | bytes 1572868
  89.1 21.7 %copy-start.8 = (f32[512,256]{1,0:T(8,128)}, f32[512,256]{1,0:T(8,128)S(1)}, u32[]{:S(2)}) copy-start(f32[512,256]{1,0:T(8,128)S(1)} %collective-permute-done.11.m1) | copy-start | bytes 1572868
  90.4 14.2 %all-to-all-start.2 = ((f32[16,1,128]{2,1,0:T(1,128)}), f32[16,1,128]{2,1,0:T(1,128)S(1)}, u32[]{:S(2)}, u32[]{:S(2)}) async-start(f32[16,1,128]{2,1,0:T(1,128)} %broadcast_in_dim.21), calls=%async_computation.2 | async-start | bytes 16384 | tf_op jit(solution)/shard_map/all_to_all | solution.py:289
  97.0 16.7 %collective-permute-start.23 = (f32[512,256]{1,0:T(8,128)S(1)}, f32[512,256]{1,0:T(8,128)S(1)}, u32[]{:S(2)}, u32[]{:S(2)}) collective-permute-start(f32[512,256]{1,0:T(8,128)S(1)} %copy-done.6), channel_id=1, source_target_pairs={{0,32},{4,36},{8,40},{12,44},{16,48},{20,52},{24,56},{28,60},{32,0... | collective-permute-start | bytes 1572872 | tf_op jit(solution)/shard_map/ppermute | solution.py:277
  104.6 12.4 %collective-permute-start.24 = (f32[256,512]{1,0:T(8,128)S(1)}, f32[256,512]{1,0:T(8,128)S(1)}, u32[]{:S(2)}, u32[]{:S(2)}) collective-permute-start(f32[256,512]{1,0:T(8,128)S(1)} %collective-permute-done.5.d2), channel_id=1, source_target_pairs={{0,1},{1,0},{2,3},{3,2},{4,5},{5,4},{6,7},{7,6},{8,9},{9,8},{10,11... | collective-permute-start | bytes 1572872 | tf_op jit(solution)/shard_map/ppermute | solution.py:280
  104.7 0.8 copy-start.10
  105.5 6.0 %copy-start.18 = (f32[2,256,128]{2,1,0:T(8,128)S(1)}, f32[2,256,128]{2,1,0:T(8,128)}, u32[]{:S(2)}) copy-start(f32[2,256,128]{2,1,0:T(8,128)} %get-tuple-element.90) | copy-start | bytes 786436
  110.9 27.0 %collective-permute-start.19 = (f32[2,512,128]{2,1,0:T(8,128)}, f32[2,512,128]{2,1,0:T(8,128)S(1)}, u32[]{:S(2)}, u32[]{:S(2)}) collective-permute-start(f32[2,512,128]{2,1,0:T(8,128)} %get-tuple-element.92), channel_id=1, source_target_pairs={{0,16},{4,20},{8,24},{12,28},{16,32},{20,36},{24,40},{28,44},{32,4... | collective-permute-start | bytes 1572872 | tf_op jit(solution)/shard_map/ppermute | solution.py:277
  111.5 12.5 %collective-permute-start.16 = (f32[2,256,128]{2,1,0:T(8,128)S(1)}, f32[2,256,128]{2,1,0:T(8,128)S(1)}, u32[]{:S(2)}, u32[]{:S(2)}) collective-permute-start(f32[2,256,128]{2,1,0:T(8,128)S(1)} %copy-done.18), channel_id=1, source_target_pairs={{0,1},{1,0},{2,3},{3,2},{4,5},{5,4},{6,7},{7,6},{8,9},{9,8},{10,11... | collective-permute-start | bytes 786440 | tf_op jit(solution)/shard_map/ppermute | solution.py:280
  111.7 27.4 %collective-permute-start.20 = (f32[2,512,128]{2,1,0:T(8,128)}, f32[2,512,128]{2,1,0:T(8,128)S(1)}, u32[]{:S(2)}, u32[]{:S(2)}) collective-permute-start(f32[2,512,128]{2,1,0:T(8,128)} %get-tuple-element.93), channel_id=1, source_target_pairs={{0,32},{4,36},{8,40},{12,44},{16,48},{20,52},{24,56},{28,60},{32,0... | collective-permute-start | bytes 1572872 | tf_op jit(solution)/shard_map/ppermute | solution.py:277
  113.8 4.4 %copy-start.9 = (f32[512,256]{1,0:T(8,128)}, f32[512,256]{1,0:T(8,128)S(1)}, u32[]{:S(2)}) copy-start(f32[512,256]{1,0:T(8,128)S(1)} %collective-permute-done.23.m2) | copy-start | bytes 1572868
  113.8 9.6 %collective-permute-start.18 = (f32[1,128]{1,0:T(1,128)S(1)}, f32[1,128]{1,0:T(1,128)S(1)}, u32[]{:S(2)}, u32[]{:S(2)}) collective-permute-start(f32[1,128]{1,0:T(1,128)S(1)} %bitcast.40), channel_id=1, source_target_pairs={{0,64},{64,0},{1,65},{65,1},{2,66},{66,2},{3,67},{67,3},{4,68},{68... | collective-permute-start | bytes 1544 | tf_op jit(solution)/shard_map/ppermute | solution.py:286
  117.0 1.2 copy-start.11
  117.0 23.8 %collective-permute-start.21 = (f32[2,512,128]{2,1,0:T(8,128)}, f32[2,512,128]{2,1,0:T(8,128)S(1)}, u32[]{:S(2)}, u32[]{:S(2)}) collective-permute-start(f32[2,512,128]{2,1,0:T(8,128)} %get-tuple-element.94), channel_id=1, source_target_pairs={{0,48},{4,52},{8,56},{12,60},{16,0},{20,4},{24,8},{28,12},{32,16},... | collective-permute-start | bytes 1572872 | tf_op jit(solution)/shard_map/ppermute | solution.py:277
  123.4 26.0 %collective-permute-start.25 = (f32[2,512,128]{2,1,0:T(8,128)}, f32[2,512,128]{2,1,0:T(8,128)S(1)}, u32[]{:S(2)}, u32[]{:S(2)}) collective-permute-start(f32[2,512,128]{2,1,0:T(8,128)} %get-tuple-element.104), channel_id=1, source_target_pairs={{0,4},{4,8},{8,12},{12,0},{16,20},{20,24},{24,28},{28,16},{32,36},... | collective-permute-start | bytes 1572872 | tf_op jit(solution)/shard_map/ppermute | solution.py:277
  123.9 25.4 %collective-permute-start.26 = (f32[2,512,128]{2,1,0:T(8,128)}, f32[2,512,128]{2,1,0:T(8,128)S(1)}, u32[]{:S(2)}, u32[]{:S(2)}) collective-permute-start(f32[2,512,128]{2,1,0:T(8,128)} %get-tuple-element.105), channel_id=1, source_target_pairs={{0,8},{4,12},{8,0},{12,4},{16,24},{20,28},{24,16},{28,20},{32,40},... | collective-permute-start | bytes 1572872 | tf_op jit(solution)/shard_map/ppermute | solution.py:277
  137.9 2.9 %copy-start.12 = (f32[2,512,128]{2,1,0:T(8,128)}, f32[2,512,128]{2,1,0:T(8,128)S(1)}, u32[]{:S(2)}) copy-start(f32[2,512,128]{2,1,0:T(8,128)S(1)} %collective-permute-done.19.a1) | copy-start | bytes 1572868
  137.9 13.7 %collective-permute-start.27 = (f32[2,512,128]{2,1,0:T(8,128)}, f32[2,512,128]{2,1,0:T(8,128)S(1)}, u32[]{:S(2)}, u32[]{:S(2)}) collective-permute-start(f32[2,512,128]{2,1,0:T(8,128)} %get-tuple-element.106), channel_id=1, source_target_pairs={{0,12},{4,0},{8,4},{12,8},{16,28},{20,16},{24,20},{28,24},{32,44},... | collective-permute-start | bytes 1572872 | tf_op jit(solution)/shard_map/ppermute | solution.py:277
  139.1 1.7 %copy-start.13 = (f32[2,512,128]{2,1,0:T(8,128)}, f32[2,512,128]{2,1,0:T(8,128)S(1)}, u32[]{:S(2)}) copy-start(f32[2,512,128]{2,1,0:T(8,128)S(1)} %collective-permute-done.20.a2) | copy-start | bytes 1572868
  139.1 19.4 %collective-permute-start.17 = (f32[2,256,128]{2,1,0:T(8,128)S(1)}, f32[2,256,128]{2,1,0:T(8,128)S(1)}, u32[]{:S(2)}, u32[]{:S(2)}) collective-permute-start(f32[2,256,128]{2,1,0:T(8,128)S(1)} %add.10), channel_id=1, source_target_pairs={{0,2},{2,0},{1,3},{3,1},{4,6},{6,4},{5,7},{7,5},{8,10},{10,8},{9,1... | collective-permute-start | bytes 786440 | tf_op jit(solution)/shard_map/ppermute | solution.py:283
  140.8 0.8 copy-start.14
  144.0 15.4 %collective-permute-start.22 = (f32[512,128]{1,0:T(8,128)}, f32[512,128]{1,0:T(8,128)S(1)}, u32[]{:S(2)}, u32[]{:S(2)}) collective-permute-start(f32[512,128]{1,0:T(8,128)} %get-tuple-element.96), channel_id=1, source_target_pairs={{0,64},{64,0},{1,65},{65,1},{2,66},{66,2},{3,67},{67,3},{4,68},{68... | collective-permute-start | bytes 786440 | tf_op jit(solution)/shard_map/ppermute | solution.py:286
  149.3 2.3 %copy-start.15 = (f32[2,512,128]{2,1,0:T(8,128)}, f32[2,512,128]{2,1,0:T(8,128)S(1)}, u32[]{:S(2)}) copy-start(f32[2,512,128]{2,1,0:T(8,128)S(1)} %collective-permute-done.25.a1) | copy-start | bytes 1572868
  149.3 2.3 %copy-start.16 = (f32[2,512,128]{2,1,0:T(8,128)}, f32[2,512,128]{2,1,0:T(8,128)S(1)}, u32[]{:S(2)}) copy-start(f32[2,512,128]{2,1,0:T(8,128)S(1)} %collective-permute-done.26.a2) | copy-start | bytes 1572868
  151.6 0.8 copy-start.17
  154.8 8.7 %collective-permute-start.28 = (f32[512,128]{1,0:T(8,128)}, f32[512,128]{1,0:T(8,128)S(1)}, u32[]{:S(2)}, u32[]{:S(2)}) collective-permute-start(f32[512,128]{1,0:T(8,128)} %get-tuple-element.108), channel_id=1, source_target_pairs={{0,64},{64,0},{1,65},{65,1},{2,66},{66,2},{3,67},{67,3},{4,68},{68... | collective-permute-start | bytes 786440 | tf_op jit(solution)/shard_map/ppermute | solution.py:286
  159.3 4.2 %copy-start.19 = (f32[512,128]{1,0:T(8,128)}, f32[512,128]{1,0:T(8,128)S(1)}, u32[]{:S(2)}) copy-start(f32[512,128]{1,0:T(8,128)S(1)} %collective-permute-done.22.a1) | copy-start | bytes 786436
  163.5 0.7 copy-start.20
